TPU v7x, 512 devices: a whole 4x4x16 slice. The times are simulated.
512 devices in a mesh: lon: 128 (over y, z, x_hi), lat: 4 (over x_lo, core).
Axes of the slice: x: 4 (x_hi: 2, x_lo: 2; x = x_hi * 2 + x_lo), y: 4, z: 16, core: 2. Of those that a mesh axis runs over, the one named last changes fastest.
Arguments:
- features: bfloat16 [128, 4, 16, 16, 128], P('lon', 'lat'), may hold values from -12 to 12
- conv_first: bfloat16 [3, 3, 128, 256], replicated, may hold values from -0.1875 to 0.1875
- conv_second: bfloat16 [3, 3, 256, 256], replicated, may hold values from -0.125 to 0.125
- cotangent: bfloat16 [128, 4, 8, 8, 256], P('lon', 'lat'), may hold values from -60 to 60
- edge_pick: int32 [128, 4, 2], P('lon', 'lat'), may hold values from 0 to 3
- edge_flip: int32 [128, 4, 2], P('lon', 'lat'), may hold values from 0 to 1
- corner_rule: int32 [128, 4, 4], P('lon', 'lat'), may hold values from 0 to 1
Outputs:
- pooled: bfloat16 [128, 4, 8, 8, 256], P('lon', 'lat')
- input_grad: bfloat16 [128, 4, 16, 16, 128], P('lon', 'lat')
- scaled_first: bfloat16 [3, 3, 128, 256], replicated
- scaled_second: bfloat16 [3, 3, 256, 256], replicated
All inputs are finite; a program needn't handle non-finite values.
Results may differ from a plain program's by a relative error of at most 0.015.
Values may be sent and summed in bfloat16 or wider, within the bound.
A program may use at most 64 MiB of HBM per device.

v0:
```python
import math

import jax
import jax.numpy as jnp
from jax import lax
from jax.sharding import PartitionSpec as P


def passed_along(value, axis, steps):
    count = lax.axis_size(axis)
    leading, last = (max(0, -steps), min(count, count - steps))
    return lax.ppermute(value, axis, [(source, source + steps) for source in range(leading, last)])


def shifted(value, axis, steps):
    count = lax.axis_size(axis)
    pairs = [(source, (source + steps) % count) for source in range(count)]
    return lax.ppermute(value, axis, pairs)


def normal_cdf(values):
    return 0.5 * (1.0 + lax.erf(values * (1.0 / math.sqrt(2.0))))


def gelu_value(values):
    return values * normal_cdf(values)


def gelu_slope(values):
    return normal_cdf(values) + values * jnp.exp(-0.5 * values * values) * (
        1.0 / math.sqrt(2.0 * math.pi)
    )


def edge_pack(square):
    return jnp.stack([square[0], square[-1], square[:, 0], square[:, -1]])


def pick_row(bundle, choose_edge, reverse_flag):
    chosen = jnp.zeros_like(bundle[0])
    for edge_id in range(4):
        chosen = jnp.where(choose_edge == edge_id, bundle[edge_id], chosen)
    return jnp.where(reverse_flag == 1, chosen[::-1], chosen)


def extend_rows(square, from_north, from_south, edge_picks, edge_flips):
    south_row = pick_row(from_south, edge_picks[0], edge_flips[0])
    north_row = pick_row(from_north, edge_picks[1], edge_flips[1])
    return jnp.concatenate([south_row[None], square, north_row[None]], axis=0)


def extend_cols(extended, west_column, east_column, corner_rules):
    padded = jnp.concatenate([west_column[:, None], extended, east_column[:, None]], axis=1)
    far_edge = padded.shape[0] - 1
    corner_spots = (
        (0, 0, 0, 1, 1, 0),
        (0, far_edge, 0, far_edge - 1, 1, far_edge),
        (far_edge, 0, far_edge, 1, far_edge - 1, 0),
        (far_edge, far_edge, far_edge, far_edge - 1, far_edge - 1, far_edge),
    )
    for corner_id, corner_spot in enumerate(corner_spots):
        row_at, col_at, first_row, first_col, second_row, second_col = corner_spot
        blended = 0.5 * (padded[first_row, first_col] + padded[second_row, second_col])
        padded = padded.at[row_at, col_at].set(
            jnp.where(corner_rules[corner_id] == 1, blended, padded[row_at, col_at])
        )
    return padded


def halo_local(square, edge_picks, edge_flips, corner_rules):
    band_at = lax.axis_index("lat")
    band_count = lax.axis_size("lat")
    at_bottom = band_at == 0
    at_top = band_at == band_count - 1
    bundle = edge_pack(square)
    north_band = passed_along(bundle, "lat", -1)
    south_band = passed_along(bundle, "lat", 1)
    across_pole = shifted(bundle, "lon", lax.axis_size("lon") // 2)
    from_north = jnp.where(at_top, across_pole, north_band)
    from_south = jnp.where(at_bottom, across_pole, south_band)
    extended = extend_rows(square, from_north, from_south, edge_picks, edge_flips)
    west_column = shifted(extended[:, -1], "lon", 1)
    east_column = shifted(extended[:, 0], "lon", -1)
    return extend_cols(extended, west_column, east_column, corner_rules)


def halo_back(grad_pad, edge_picks, edge_flips, corner_rules):
    side_cells, channels = (grad_pad.shape[0] - 2, grad_pad.shape[2])
    blank_ext = jnp.zeros((side_cells + 2, side_cells, channels), jnp.float32)
    blank_column = jnp.zeros((side_cells + 2, channels), jnp.float32)
    _, cols_back = jax.vjp(
        lambda ext_in, west_in, east_in: extend_cols(ext_in, west_in, east_in, corner_rules),
        blank_ext,
        blank_column,
        blank_column,
    )
    ext_grad, west_grad, east_grad = cols_back(grad_pad)
    from_east = shifted(west_grad, "lon", -1)
    from_west = shifted(east_grad, "lon", 1)
    ext_grad = ext_grad.at[:, -1].add(from_east).at[:, 0].add(from_west)
    band_at = lax.axis_index("lat")
    band_count = lax.axis_size("lat")
    at_top = band_at == band_count - 1
    at_bottom = band_at == 0
    blank_square = jnp.zeros((side_cells, side_cells, channels), jnp.float32)
    blank_bundle = jnp.zeros((4, side_cells, channels), jnp.float32)
    _, rows_back = jax.vjp(
        lambda square_in, north_in, south_in: extend_rows(
            square_in, north_in, south_in, edge_picks, edge_flips
        ),
        blank_square,
        blank_bundle,
        blank_bundle,
    )
    square_grad, north_grad, south_grad = rows_back(ext_grad)
    nothing = jnp.zeros_like(north_grad)
    to_north = passed_along(
        jnp.where(at_top, nothing, north_grad).astype(jnp.bfloat16), "lat", 1
    ).astype(jnp.float32)
    to_south = passed_along(
        jnp.where(at_bottom, nothing, south_grad).astype(jnp.bfloat16), "lat", -1
    ).astype(jnp.float32)
    polar_grad = jnp.where(at_top, north_grad, nothing) + jnp.where(at_bottom, south_grad, nothing)
    to_pole = shifted(polar_grad.astype(jnp.bfloat16), "lon", lax.axis_size("lon") // 2).astype(
        polar_grad.dtype
    )
    bundle_grad = to_north + to_south + to_pole
    square_grad = square_grad.at[0].add(bundle_grad[0]).at[-1].add(bundle_grad[1])
    square_grad = square_grad.at[:, 0].add(bundle_grad[2]).at[:, -1].add(bundle_grad[3])
    return square_grad


def convolve(padded, weight):
    tile_count, tile_width = (padded.shape[0], padded.shape[1] - 2)
    summed = jnp.zeros((tile_count * tile_width * tile_width, weight.shape[3]), jnp.float32)
    for shift_row in range(3):
        for shift_col in range(3):
            window = padded[
                :, shift_row : shift_row + tile_width, shift_col : shift_col + tile_width
            ].reshape(tile_count * tile_width * tile_width, -1)
            summed = summed + jnp.dot(
                window, weight[shift_row, shift_col], preferred_element_type=jnp.float32
            )
    return summed.reshape(tile_count, tile_width, tile_width, -1)


def weight_grad(padded, gradient):
    tile_count, tile_width = (gradient.shape[0], gradient.shape[1])
    flat_grad = gradient.reshape(tile_count * tile_width * tile_width, -1)
    blocks = []
    for shift_row in range(3):
        for shift_col in range(3):
            window = padded[
                :, shift_row : shift_row + tile_width, shift_col : shift_col + tile_width
            ].reshape(tile_count * tile_width * tile_width, -1)
            blocks.append(
                lax.dot_general(
                    window, flat_grad, (((0,), (0,)), ((), ())), preferred_element_type=jnp.float32
                )
            )
    return jnp.stack(blocks).reshape(3, 3, padded.shape[3], gradient.shape[3])


def input_side_grad(gradient, weight):
    tile_count, tile_width = (gradient.shape[0], gradient.shape[1])
    flat_grad = gradient.reshape(tile_count * tile_width * tile_width, -1)
    summed = jnp.zeros((tile_count, tile_width + 2, tile_width + 2, weight.shape[2]), jnp.float32)
    for shift_row in range(3):
        for shift_col in range(3):
            product = lax.dot_general(
                flat_grad,
                weight[shift_row, shift_col],
                (((1,), (1,)), ((), ())),
                preferred_element_type=jnp.float32,
            )
            product = product.reshape(tile_count, tile_width, tile_width, -1)
            summed = summed + jnp.pad(
                product, ((0, 0), (shift_row, 2 - shift_row), (shift_col, 2 - shift_col), (0, 0))
            )
    return summed


def pool_cells(values):
    tile_count, tile_width, channels = (values.shape[0], values.shape[1], values.shape[3])
    grouped = values.reshape(tile_count, tile_width // 2, 2, tile_width // 2, 2, channels)
    return jnp.sum(grouped, axis=(2, 4)) * 0.25


def expand_grad(values):
    tile_count, half_width, channels = (values.shape[0], values.shape[1], values.shape[3])
    spread = jnp.broadcast_to(
        values[:, :, None, :, None, :], (tile_count, half_width, 2, half_width, 2, channels)
    )
    return spread.reshape(tile_count, 2 * half_width, 2 * half_width, channels) * 0.25


def on_device(features, conv_first, conv_second, cotangent, edge_pick, edge_flip, corner_rule):
    edge_picks = edge_pick[0, 0]
    edge_flips = edge_flip[0, 0]
    corner_rules = corner_rule[0, 0]
    features_pad = halo_local(features[0, 0], edge_picks, edge_flips, corner_rules)[None]
    first_pre = convolve(features_pad, conv_first)
    first_act = gelu_value(first_pre).astype(jnp.bfloat16)
    first_pad = halo_local(first_act[0], edge_picks, edge_flips, corner_rules)[None]
    second_pre = convolve(first_pad, conv_second)
    pooled = pool_cells(gelu_value(second_pre)).astype(jnp.bfloat16)
    second_grad = (expand_grad(cotangent[0].astype(jnp.float32)) * gelu_slope(second_pre)).astype(
        jnp.bfloat16
    )
    grad_second = weight_grad(first_pad, second_grad)
    first_pad_grad = input_side_grad(second_grad, conv_second).astype(jnp.bfloat16)
    first_grad = halo_back(
        first_pad_grad[0].astype(jnp.float32), edge_picks, edge_flips, corner_rules
    )[None]
    pre_grad = (first_grad * gelu_slope(first_pre)).astype(jnp.bfloat16)
    grad_first = weight_grad(features_pad, pre_grad)
    features_pad_grad = input_side_grad(pre_grad, conv_first).astype(jnp.bfloat16)
    input_grad = halo_back(
        features_pad_grad[0].astype(jnp.float32), edge_picks, edge_flips, corner_rules
    )
    input_grad = input_grad.astype(jnp.bfloat16)[None, None]
    norm_target = math.sqrt(9.0 * (conv_first.shape[2] + conv_first.shape[3]) * conv_first.shape[3])
    first_total, second_total = lax.psum((grad_first, grad_second), ("lon", "lat"))
    squared = jnp.sum(first_total * first_total) + jnp.sum(second_total * second_total)
    norm_scale = norm_target / jnp.sqrt(squared + 1e-06)
    scaled_first = (first_total * norm_scale).astype(jnp.bfloat16)
    scaled_second = (second_total * norm_scale).astype(jnp.bfloat16)
    return (pooled[None], input_grad, scaled_first, scaled_second)


def solution(mesh):
    return jax.shard_map(
        on_device,
        mesh=mesh,
        in_specs=(
            P("lon", "lat", None, None, None),
            P(),
            P(),
            P("lon", "lat", None, None, None),
            P("lon", "lat", None),
            P("lon", "lat", None),
            P("lon", "lat", None),
        ),
        out_specs=(P("lon", "lat", None, None, None), P("lon", "lat", None, None, None), P(), P()),
        check_vma=False,
    )
```

profile of v0, /device:TPU:1, one launch (start us, length us, event | category | flops | bytes accessed | tf_op | source)
XLA Modules:
  0.0 638.8 jit_solution(80591587733191602)
XLA Ops:
  8.8 8.8 %collective-permute-start.2 = (bf16[4,16,128]{2,1,0:T(8,128)(2,1)S(1)}, bf16[4,16,128]{2,1,0:T(8,128)(2,1)S(1)}, u32[]{:S(2)}, u32[]{:S(2)}) collective-permute-start(bf16[4,16,128]{2,1,0:T(8,128)(2,1)S(1)} %pad_maximum_fusion.6), channel_id=1, source_target_pairs={{1,0},{2,1},{3,2},{5,4},{6,5},{7,6},{9,8},{10,9},{11,10},{13,12},{... | collective-permute-start | bytes 49160 | tf_op jit(solution)/shard_map/ppermute | solution.py:12
  17.6 1.9 collective-permute-start.1
  19.5 1.9 collective-permute-start
  34.3 12.7 %collective-permute-start.4 = (bf16[18,128]{1,0:T(8,128)(2,1)S(1)}, bf16[18,128]{1,0:T(8,128)(2,1)S(1)}, u32[]{:S(2)}, u32[]{:S(2)}) collective-permute-start(bf16[18,128]{1,0:T(8,128)(2,1)S(1)} %bitcast.652), channel_id=1, source_target_pairs={{0,508},{4,0},{8,4},{12,8},{16,12},{20,16},{24,20},{28,24},{32,28}... | collective-permute-start | bytes 13832 | tf_op jit(solution)/shard_map/ppermute | solution.py:18
  52.0 5.1 collective-permute-done.3
  63.3 3.1 collective-permute-start.7
  66.3 2.5 collective-permute-start.6
  68.9 2.1 collective-permute-start.5
  71.0 4.0 collective-permute-done.5
  75.3 4.0 collective-permute-start.9
  79.4 2.8 collective-permute-start.8
  82.5 7.0 %collective-permute-done.8 = bf16[18,256]{1,0:T(8,128)(2,1)S(1)} collective-permute-done((bf16[18,256]{1,0:T(8,128)(2,1)S(1)}, bf16[18,256]{1,0:T(8,128)(2,1)S(1)}, u32[]{:S(2)}, u32[]{:S(2)}) %collective-permute-start.8) | collective-permute-done | bytes 9248 | tf_op jit(solution)/shard_map/ppermute | solution.py:18
  108.0 4.9 collective-permute-start.11
  113.1 5.2 collective-permute-done.11
  118.6 5.0 collective-permute-start.12
  136.8 2.0 collective-permute-start.15
  138.8 4.8 collective-permute-start.16
  146.3 2.6 collective-permute-done.16
  149.1 3.2 collective-permute-start.17
  152.3 3.5 collective-permute-start.19
  158.4 2.9 collective-permute-done.18
  162.1 460.7 %all-reduce.61.cloned.1.call-done = (f32[3,3,128,256]{3,2,1,0:T(8,128)}, f32[3,3,256,256]{3,2,1,0:T(8,128)}) async-done(((f32[3,3,128,256]{3,2,1,0:T(8,128)}, f32[3,3,256,256]{3,2,1,0:T(8,128)}), (f32[3,3,128,256]{3,2,1,0:T(8,128)}, f32[3,3,256,256]{3,2,1,0:T(8,128)})) %all-reduce.61.cloned.1.call-update) | async-done | bytes 3538960 | tf_op jit(solution)/shard_map/psum | solution.py:223
  622.9 3.0 multiply_reduce_fusion
  625.9 2.2 multiply_reduce_fusion.1
  (248 shorter events, 57.1 us)
Async XLA Ops:
  7.2 54.1 %copy-start.3 = (bf16[3,3,128,256]{3,2,1,0:T(8,128)(2,1)S(1)}, bf16[3,3,128,256]{3,2,1,0:T(8,128)(2,1)}, u32[]{:S(2)}) copy-start(bf16[3,3,128,256]{3,2,1,0:T(8,128)(2,1)} %param.64) | copy-start | bytes 1769476
  7.2 615.7 %all-reduce.61.cloned.1.call-start = ((), (), s32[]{:S(2)}) async-start(), calls=%async_computation | async-start | bytes 7077888 | tf_op jit(solution)/shard_map/psum | solution.py:223
  8.8 24.6 %collective-permute-start.2 = (bf16[4,16,128]{2,1,0:T(8,128)(2,1)S(1)}, bf16[4,16,128]{2,1,0:T(8,128)(2,1)S(1)}, u32[]{:S(2)}, u32[]{:S(2)}) collective-permute-start(bf16[4,16,128]{2,1,0:T(8,128)(2,1)S(1)} %pad_maximum_fusion.6), channel_id=1, source_target_pairs={{1,0},{2,1},{3,2},{5,4},{6,5},{7,6},{9,8},{10,9},{11,10},{13,12},{... | collective-permute-start | bytes 49160 | tf_op jit(solution)/shard_map/ppermute | solution.py:12
  17.6 15.8 %collective-permute-start.1 = (bf16[4,16,128]{2,1,0:T(8,128)(2,1)S(1)}, bf16[4,16,128]{2,1,0:T(8,128)(2,1)S(1)}, u32[]{:S(2)}, u32[]{:S(2)}) collective-permute-start(bf16[4,16,128]{2,1,0:T(8,128)(2,1)S(1)} %pad_maximum_fusion.6), channel_id=1, source_target_pairs={{0,1},{1,2},{2,3},{4,5},{5,6},{6,7},{8,9},{9,10},{10,11},{12,13},{... | collective-permute-start | bytes 49160 | tf_op jit(solution)/shard_map/ppermute | solution.py:12
  19.5 13.9 %collective-permute-start = (bf16[4,16,128]{2,1,0:T(8,128)(2,1)S(1)}, bf16[4,16,128]{2,1,0:T(8,128)(2,1)S(1)}, u32[]{:S(2)}, u32[]{:S(2)}) collective-permute-start(bf16[4,16,128]{2,1,0:T(8,128)(2,1)S(1)} %pad_maximum_fusion.6), channel_id=1, source_target_pairs={{0,256},{4,260},{8,264},{12,268},{16,272},{20,276},{24,280},{28,28... | collective-permute-start | bytes 49160 | tf_op jit(solution)/shard_map/ppermute | solution.py:18
  34.3 17.7 %collective-permute-start.4 = (bf16[18,128]{1,0:T(8,128)(2,1)S(1)}, bf16[18,128]{1,0:T(8,128)(2,1)S(1)}, u32[]{:S(2)}, u32[]{:S(2)}) collective-permute-start(bf16[18,128]{1,0:T(8,128)(2,1)S(1)} %bitcast.652), channel_id=1, source_target_pairs={{0,508},{4,0},{8,4},{12,8},{16,12},{20,16},{24,20},{28,24},{32,28}... | collective-permute-start | bytes 13832 | tf_op jit(solution)/shard_map/ppermute | solution.py:18
  47.0 10.1 %collective-permute-start.3 = (bf16[18,128]{1,0:T(8,128)(2,1)S(1)}, bf16[18,128]{1,0:T(8,128)(2,1)S(1)}, u32[]{:S(2)}, u32[]{:S(2)}) collective-permute-start(bf16[18,128]{1,0:T(8,128)(2,1)S(1)} %bitcast.651), channel_id=1, source_target_pairs={{0,4},{4,8},{8,12},{12,16},{16,20},{20,24},{24,28},{28,32},{32,36}... | collective-permute-start | bytes 13832 | tf_op jit(solution)/shard_map/ppermute | solution.py:18
  62.7 19.4 %copy-start.6 = (bf16[1,1,8,8,256]{4,3,2,1,0:T(8,128)(2,1)S(1)}, bf16[1,1,8,8,256]{4,3,2,1,0:T(8,128)(2,1)}, u32[]{:S(2)}) copy-start(bf16[1,1,8,8,256]{4,3,2,1,0:T(8,128)(2,1)} %param.66) | copy-start | bytes 98308
  63.3 7.7 %collective-permute-start.7 = (bf16[4,16,256]{2,1,0:T(8,128)(2,1)S(1)}, bf16[4,16,256]{2,1,0:T(8,128)(2,1)S(1)}, u32[]{:S(2)}, u32[]{:S(2)}) collective-permute-start(bf16[4,16,256]{2,1,0:T(8,128)(2,1)S(1)} %pad_maximum_fusion.2), channel_id=1, source_target_pairs={{1,0},{2,1},{3,2},{5,4},{6,5},{7,6},{9,8},{10,9},{11,10},{13,12},{... | collective-permute-start | bytes 98312 | tf_op jit(solution)/shard_map/ppermute | solution.py:12
  66.3 4.7 collective-permute-start.6
  68.9 6.2 collective-permute-start.5
  75.3 7.1 %collective-permute-start.9 = (bf16[18,256]{1,0:T(8,128)(2,1)S(1)}, bf16[18,256]{1,0:T(8,128)(2,1)S(1)}, u32[]{:S(2)}, u32[]{:S(2)}) collective-permute-start(bf16[18,256]{1,0:T(8,128)(2,1)S(1)} %bitcast.648), channel_id=1, source_target_pairs={{0,508},{4,0},{8,4},{12,8},{16,12},{20,16},{24,20},{28,24},{32,28}... | collective-permute-start | bytes 27656 | tf_op jit(solution)/shard_map/ppermute | solution.py:18
  79.4 10.2 %collective-permute-start.8 = (bf16[18,256]{1,0:T(8,128)(2,1)S(1)}, bf16[18,256]{1,0:T(8,128)(2,1)S(1)}, u32[]{:S(2)}, u32[]{:S(2)}) collective-permute-start(bf16[18,256]{1,0:T(8,128)(2,1)S(1)} %bitcast.647), channel_id=1, source_target_pairs={{0,4},{4,8},{8,12},{12,16},{16,20},{20,24},{24,28},{28,32},{32,36}... | collective-permute-start | bytes 27656 | tf_op jit(solution)/shard_map/ppermute | solution.py:18
  101.9 11.2 %collective-permute-start.10 = (f32[18,256]{1,0:T(8,128)S(1)}, f32[18,256]{1,0:T(8,128)S(1)}, u32[]{:S(2)}, u32[]{:S(2)}) collective-permute-start(f32[18,256]{1,0:T(8,128)S(1)} %bitcast.642), channel_id=1, source_target_pairs={{0,508},{4,0},{8,4},{12,8},{16,12},{20,16},{24,20},{28,24},{32,28}... | collective-permute-start | bytes 55304 | tf_op jit(solution)/shard_map/ppermute | solution.py:18
  108.0 10.3 %collective-permute-start.11 = (f32[18,256]{1,0:T(8,128)S(1)}, f32[18,256]{1,0:T(8,128)S(1)}, u32[]{:S(2)}, u32[]{:S(2)}) collective-permute-start(f32[18,256]{1,0:T(8,128)S(1)} %bitcast.643), channel_id=1, source_target_pairs={{0,4},{4,8},{8,12},{12,16},{16,20},{20,24},{24,28},{28,32},{32,36}... | collective-permute-start | bytes 55304 | tf_op jit(solution)/shard_map/ppermute | solution.py:18
  118.6 9.3 %collective-permute-start.12 = (bf16[4,16,256]{2,1,0:T(8,128)(2,1)S(1)}, bf16[4,16,256]{2,1,0:T(8,128)(2,1)S(1)}, u32[]{:S(2)}, u32[]{:S(2)}) collective-permute-start(bf16[4,16,256]{2,1,0:T(8,128)(2,1)S(1)} %get-tuple-element.432), channel_id=1, source_target_pairs={{0,1},{1,2},{2,3},{4,5},{5,6},{6,7},{8,9},{9,10},{10,11},{12,13},{... | collective-permute-start | bytes 98312 | tf_op jit(solution)/shard_map/ppermute | solution.py:12
  123.7 6.2 collective-permute-start.14
  125.6 5.2 collective-permute-start.13
  136.8 9.5 %collective-permute-start.15 = (f32[18,128]{1,0:T(8,128)S(1)}, f32[18,128]{1,0:T(8,128)S(1)}, u32[]{:S(2)}, u32[]{:S(2)}) collective-permute-start(f32[18,128]{1,0:T(8,128)S(1)} %bitcast.646), channel_id=1, source_target_pairs={{0,508},{4,0},{8,4},{12,8},{16,12},{20,16},{24,20},{28,24},{32,28}... | collective-permute-start | bytes 27656 | tf_op jit(solution)/shard_map/ppermute | solution.py:18
  138.8 10.2 %collective-permute-start.16 = (f32[18,128]{1,0:T(8,128)S(1)}, f32[18,128]{1,0:T(8,128)S(1)}, u32[]{:S(2)}, u32[]{:S(2)}) collective-permute-start(f32[18,128]{1,0:T(8,128)S(1)} %bitcast.645), channel_id=1, source_target_pairs={{0,4},{4,8},{8,12},{12,16},{16,20},{20,24},{24,28},{28,32},{32,36}... | collective-permute-start | bytes 27656 | tf_op jit(solution)/shard_map/ppermute | solution.py:18
  149.1 9.3 %collective-permute-start.17 = (bf16[4,16,128]{2,1,0:T(8,128)(2,1)S(1)}, bf16[4,16,128]{2,1,0:T(8,128)(2,1)S(1)}, u32[]{:S(2)}, u32[]{:S(2)}) collective-permute-start(bf16[4,16,128]{2,1,0:T(8,128)(2,1)S(1)} %get-tuple-element.441), channel_id=1, source_target_pairs={{0,1},{1,2},{2,3},{4,5},{5,6},{6,7},{8,9},{9,10},{10,11},{12,13},{... | collective-permute-start | bytes 49160 | tf_op jit(solution)/shard_map/ppermute | solution.py:12
  152.3 6.1 collective-permute-start.19
  155.8 5.5 collective-permute-start.18
  622.9 6.5 %copy-start = (f32[3,3,256,256]{3,2,1,0:T(8,128)S(1)}, f32[3,3,256,256]{3,2,1,0:T(8,128)}, u32[]{:S(2)}) copy-start(f32[3,3,256,256]{3,2,1,0:T(8,128)} %get-tuple-element.365) | copy-start | bytes 7077892
  (4 other events, 5.3 us)
Sparse Core Ops, SparseCore 0:
  146.4 476.4 all-reduce.60
where the time goes:
time: 641 us; the launch traced here: 639 us
  waiting for transfers between devices  490 us (76%)
  starting transfers between devices  72.8 us (11%)
  between operations  25.8 us (4%)
  other arithmetic  20.8 us (3%)
  local copies, waits for them, and re-layouts  18.2 us (3%)
  matrix products  10.8 us (2%)
    psum x1, waiting for transfers between devices, on_device(): lax.psum((grad_first, grad_second), ('lon', 'lat'))  461 us
    ppermute x12, starting transfers between devices, shifted(): return lax.ppermute(value, axis, pairs)  44.4 us
    ppermute x8, starting transfers between devices, passed_along(): lax.ppermute(value, axis, [(source, source + steps) for source in range(l...  28.3 us
    ppermute x12, waiting for transfers between devices, shifted(): return lax.ppermute(value, axis, pairs)  25.9 us
  transfers between devices with their start and end apart: 21, of which 9 were waited for; matrix products, arithmetic and copies ran while one was open for 2% of the time, Pallas kernels for 0%

commit v1 on v0

v1 whole, which is shorter than its diff:
```python
import math

import jax
import jax.numpy as jnp
from jax import lax
from jax.experimental import pallas as pl
from jax.experimental.pallas import tpu as pltpu
from jax.sharding import PartitionSpec as P

MESH = pl.DeviceIdType.MESH
BF = jnp.bfloat16
F32 = jnp.float32
NX, NY, NZ = 4, 4, 16
LON, LAT = 2 * NY * NZ, 4
C1, C2 = 128, 256


def normal_cdf(values):
    return 0.5 * (1.0 + lax.erf(values * (1.0 / math.sqrt(2.0))))


def gelu_slope(values, cdf):
    return cdf + values * jnp.exp(-0.5 * values * values) * (1.0 / math.sqrt(2.0 * math.pi))


def iota(shape, dim):
    return lax.broadcasted_iota(jnp.int32, shape, dim)


def hot(cond, value=1.0):
    return jnp.where(cond, jnp.float32(value), jnp.float32(0.0))


def mm(a, b):
    return jnp.dot(a, b, preferred_element_type=F32)


def mm_nt(a, b):
    return lax.dot_general(a, b, (((1,), (1,)), ((), ())), preferred_element_type=F32)


def mm_tn(a, b):
    return lax.dot_general(a, b, (((0,), (0,)), ((), ())), preferred_element_type=F32)


def remote(src, dst, send_sem, recv_sem, device):
    return pltpu.make_async_remote_copy(
        src_ref=src, dst_ref=dst, send_sem=send_sem, recv_sem=recv_sem,
        device_id=device, device_id_type=MESH,
    )


def corner_slot(edge, at_end):
    return jnp.where(
        edge == 0, at_end, jnp.where(edge == 1, 2 + at_end, jnp.where(edge == 2, 2 * at_end, 1 + 2 * at_end))
    )


class Reduce:
    def __init__(self, m, z_base, refs, place):
        self.m = m
        self.z_base = z_base
        self.total = m[0] + m[1]
        self.start = (0, 16 * m[0])
        (self.halves, self.r0, self.a1, self.r1a, self.r1b, self.a2a, self.a2b, self.r2a, self.r2b,
         self.a3, self.r3, self.out, self.s_send, self.s_recv, self.z_recv, self.g_send, self.g_recv,
         self.gz_send) = refs
        self.place = place
        self.x, self.y, self.z, self.core, self.device = place
        self.pending = []

    def peer(self, axis, d):
        x, y = self.x, self.y
        if axis == "x":
            x = lax.rem(x + d, NX)
        else:
            y = lax.rem(y + d, NY)
        return x, y

    def axes(self, part):
        return ("x", "y") if part == 0 else ("y", "x")

    def coords(self, part):
        return (self.x, self.y) if part == 0 else (self.y, self.x)

    def send(self, copy):
        copy.start()
        self.pending.append(copy)

    def finish(self):
        for copy in self.pending:
            copy.wait_send()
        self.pending = []

    def core_send(self):
        self.send(remote(self.halves.at[1 - self.core], self.r0, self.s_send.at[0], self.s_recv.at[0],
                         self.device(self.x, self.y, self.z, 1 - self.core)))

    def core_add(self):
        remote(self.halves.at[0], self.r0, self.s_send.at[0], self.s_recv.at[0],
               self.device(self.x, self.y, self.z, 1 - self.core)).wait_recv()
        units = 16 * self.total

        step = 8

        def body(i, carry):
            at = pl.ds(i * step, step)
            self.a1[at] = (self.halves[self.core, at].astype(F32) + self.r0[at].astype(F32)).astype(BF)
            return carry

        lax.fori_loop(0, units // step, body, 0)

    def first_send(self):
        for part in range(2):
            n = 4 * self.m[part]
            r1 = (self.r1a, self.r1b)[part]
            mine = self.coords(part)[0]
            for d in (2, 1, 3):
                x, y = self.peer(self.axes(part)[0], d)
                block = lax.rem(mine + d, 4)
                k = 1 + part * 3 + d - 1
                self.send(remote(self.a1.at[pl.ds(self.start[part] + block * n, n)], r1.at[d - 1],
                                 self.s_send.at[k], self.s_recv.at[k], self.device(x, y, self.z, self.core)))

    def first_add(self):
        for part in range(2):
            n = 4 * self.m[part]
            r1 = (self.r1a, self.r1b)[part]
            a2 = (self.a2a, self.a2b)[part]
            mine = self.coords(part)[0]
            for d in (1, 2, 3):
                k = 1 + part * 3 + d - 1
                remote(r1.at[d - 1], r1.at[d - 1], self.s_send.at[k], self.s_recv.at[k],
                       self.device(self.x, self.y, self.z, 1 - self.core)).wait_recv()
            step = self.m[part]

            def body(i, carry):
                at = pl.ds(i * step, step)
                total = self.a1[pl.ds(self.start[part] + mine * n + i * step, step)].astype(F32)
                for d in range(3):
                    total = total + r1[d, at].astype(F32)
                a2[at] = total.astype(BF)
                return carry

            lax.fori_loop(0, 4, body, 0)

    def second_send(self):
        for part in range(2):
            m = self.m[part]
            a2 = (self.a2a, self.a2b)[part]
            r2 = (self.r2a, self.r2b)[part]
            mine = self.coords(part)[1]
            for d in (2, 1, 3):
                x, y = self.peer(self.axes(part)[1], d)
                block = lax.rem(mine + d, 4)
                k = 7 + part * 3 + d - 1
                self.send(remote(a2.at[pl.ds(block * m, m)], r2.at[d - 1],
                                 self.s_send.at[k], self.s_recv.at[k], self.device(x, y, self.z, self.core)))

    def second_add(self):
        for part in range(2):
            m = self.m[part]
            a2 = (self.a2a, self.a2b)[part]
            r2 = (self.r2a, self.r2b)[part]
            mine = self.coords(part)[1]
            for d in (1, 2, 3):
                k = 7 + part * 3 + d - 1
                remote(r2.at[d - 1], r2.at[d - 1], self.s_send.at[k], self.s_recv.at[k],
                       self.device(self.x, self.y, self.z, 1 - self.core)).wait_recv()
            total = a2[pl.ds(mine * m, m)].astype(F32)
            for d in range(3):
                total = total + r2[d].astype(F32)
            self.a3[pl.ds(part * self.m[0], m)] = total.astype(BF)

    def z_send(self):
        for u in range(self.total):
            owner = self.z_base + u
            away = lax.rem(self.z - owner + NZ, NZ)

            @pl.when(away != 0)
            def _():
                remote(self.a3.at[u], self.r3.at[away - 1], self.s_send.at[13 + u], self.z_recv.at[away - 1],
                       self.device(self.x, self.y, owner, self.core)).start()

    def z_send_done(self):
        for u in range(self.total):
            @pl.when(self.z != self.z_base + u)
            def _():
                remote(self.a3.at[u], self.r3.at[0], self.s_send.at[13 + u], self.z_recv.at[0],
                       self.device(self.x, self.y, self.z_base + u, self.core)).wait_send()

    def unit_at(self, u):
        ma, mb = self.m
        first = (self.x * 4 + self.y) * ma + u
        second = self.start[1] + (self.y * 4 + self.x) * mb + u - ma
        if isinstance(u, int):
            return first if u < ma else second
        return jnp.where(u < ma, first, second)

    def owner(self):
        return jnp.logical_and(self.z >= self.z_base, self.z < self.z_base + self.total)

    def z_add_and_gather(self):
        mine = self.z - self.z_base

        @pl.when(self.owner())
        def _():
            for d in range(1, NZ):
                remote(self.r3.at[d - 1], self.r3.at[d - 1], self.s_send.at[13], self.z_recv.at[d - 1],
                       self.device(self.x, self.y, self.z, 1 - self.core)).wait_recv()
            total = self.a3[mine].astype(F32)
            for d in range(NZ - 1):
                total = total + self.r3[d].astype(F32)
            at = self.unit_at(mine)
            self.out[self.core, at] = total.astype(BF)
            for d in (8, 7, 9, 6, 10, 5, 11, 4, 12, 3, 13, 2, 14, 1, 15):
                remote(self.out.at[self.core, at], self.out.at[self.core, at], self.gz_send.at[d - 1],
                       self.g_recv.at[mine],
                       self.device(self.x, self.y, lax.rem(self.z + d, NZ), self.core)).start()

    def z_gather_sent(self):
        mine = self.z - self.z_base

        @pl.when(self.owner())
        def _():
            at = self.unit_at(mine)
            for d in range(1, NZ):
                remote(self.out.at[self.core, at], self.out.at[self.core, at], self.gz_send.at[d - 1],
                       self.g_recv.at[mine],
                       self.device(self.x, self.y, lax.rem(self.z + d, NZ), self.core)).wait_send()

    def gather_second(self):
        for u in range(self.total):
            at = self.unit_at(u)

            @pl.when(self.z != self.z_base + u)
            def _():
                remote(self.out.at[self.core, at], self.out.at[self.core, at], self.gz_send.at[0],
                       self.g_recv.at[u], self.device(self.x, self.y, self.z, 1 - self.core)).wait_recv()
        for part in range(2):
            m = self.m[part]
            ca, cb = self.coords(part)
            at = pl.ds(self.start[part] + (ca * 4 + cb) * m, m)
            for d in (2, 1, 3):
                x, y = self.peer(self.axes(part)[1], d)
                k = part * 3 + d - 1
                self.send(remote(self.out.at[self.core, at], self.out.at[self.core, at], self.g_send.at[k],
                                 self.g_recv.at[9 + k], self.device(x, y, self.z, self.core)))

    def gather_first(self):
        for part in range(2):
            m = self.m[part]
            ca, cb = self.coords(part)
            for d in (1, 3, 2):
                k = part * 3 + d - 1
                there = lax.rem(cb + 4 - d, 4)
                at = pl.ds(self.start[part] + (ca * 4 + there) * m, m)
                remote(self.out.at[self.core, at], self.out.at[self.core, at], self.g_send.at[k],
                       self.g_recv.at[9 + k], self.device(self.x, self.y, self.z, 1 - self.core)).wait_recv()
            at = pl.ds(self.start[part] + ca * 4 * m, 4 * m)
            for d in (2, 1, 3):
                x, y = self.peer(self.axes(part)[0], d)
                k = 6 + part * 3 + d - 1
                self.send(remote(self.out.at[self.core, at], self.out.at[self.core, at], self.g_send.at[k],
                                 self.g_recv.at[9 + k], self.device(x, y, self.z, self.core)))
            self.to_core(part, 0, at)

    def to_core(self, part, d, at):
        k = 12 + part * 4 + d
        self.send(remote(self.out.at[self.core, at], self.out.at[self.core, at], self.g_send.at[k],
                         self.g_recv.at[9 + k], self.device(self.x, self.y, self.z, 1 - self.core)))

    def gather_core(self):
        for d in (1, 3, 2):
            for part in range(2):
                n = 4 * self.m[part]
                ca = self.coords(part)[0]
                k = 6 + part * 3 + d - 1
                at = pl.ds(self.start[part] + lax.rem(ca + 4 - d, 4) * n, n)
                remote(self.out.at[self.core, at], self.out.at[self.core, at], self.g_send.at[k],
                       self.g_recv.at[9 + k], self.device(self.x, self.y, self.z, 1 - self.core)).wait_recv()
                self.to_core(part, d, at)

    def gather_done(self):
        for part in range(2):
            n = 4 * self.m[part]
            ca = self.coords(part)[0]
            for d in range(4):
                k = 12 + part * 4 + d
                at = pl.ds(self.start[part] + lax.rem(ca + 4 - d, 4) * n, n)
                remote(self.out.at[1 - self.core, at], self.out.at[1 - self.core, at], self.g_send.at[k],
                       self.g_recv.at[9 + k], self.device(self.x, self.y, self.z, 1 - self.core)).wait_recv()


def reduce_scratch(ma, mb):
    units = 16 * (ma + mb)
    total = ma + mb
    return [
        pltpu.VMEM((2, units, 16, 128), BF),
        pltpu.VMEM((units, 16, 128), BF),
        pltpu.VMEM((units, 16, 128), BF),
        pltpu.VMEM((3, 4 * ma, 16, 128), BF),
        pltpu.VMEM((3, 4 * mb, 16, 128), BF),
        pltpu.VMEM((4 * ma, 16, 128), BF),
        pltpu.VMEM((4 * mb, 16, 128), BF),
        pltpu.VMEM((3, ma, 16, 128), BF),
        pltpu.VMEM((3, mb, 16, 128), BF),
        pltpu.VMEM((total, 16, 128), BF),
        pltpu.VMEM((NZ - 1, 16, 128), BF),
        pltpu.VMEM((2, units, 16, 128), BF),
        pltpu.SemaphoreType.DMA((13 + total,)),
        pltpu.SemaphoreType.DMA((13,)),
        pltpu.SemaphoreType.DMA((NZ - 1,)),
        pltpu.SemaphoreType.DMA((20,)),
        pltpu.SemaphoreType.DMA((9 + 20,)),
        pltpu.SemaphoreType.DMA((NZ - 1,)),
    ]


N_REDUCE = 18
M2 = (5, 4)
M1 = (3, 2)
FIRST_ROWS = ((0, 0, 40), (48, 40, 32))


def halo_scratch(channels):
    return [
        pltpu.VMEM((80, channels), BF),
        pltpu.VMEM((256, channels), BF),
        pltpu.SemaphoreType.DMA((8,)),
        pltpu.SemaphoreType.DMA((8,)),
        pltpu.VMEM((304, channels), F32),
        pltpu.VMEM((288, 3 * channels), BF),
        pltpu.VMEM((416, C2), BF),
        pltpu.VMEM((304, 3 * channels), F32),
        pltpu.VMEM((384, channels), BF),
        pltpu.VMEM((128, channels), BF),
        pltpu.VMEM((128, channels), BF),
        pltpu.SemaphoreType.DMA((8,)),
        pltpu.SemaphoreType.DMA((8,)),
    ]


N_HALO = 13


def step_kernel(*refs):
    (feat_ref, w1_hbm, w2_hbm, cot_ref, pick_ref, flip_ref, rule_ref,
     pooled_ref, grad_ref, first_ref, second_ref) = refs[:11]
    refs = refs[11:]
    halo1, refs = refs[:N_HALO], refs[N_HALO:]
    halo2, refs = refs[:N_HALO], refs[N_HALO:]
    red2_refs, refs = refs[:N_REDUCE], refs[N_REDUCE:]
    red1_refs, refs = refs[:N_REDUCE], refs[N_REDUCE:]
    (w1, w2, w_sem, rules_out, rules_in, rule_send, rule_recv, q_fwd, q_back, slope1, pre2) = refs

    lon, lat = lax.axis_index("lon"), lax.axis_index("lat")
    y = lax.div(lon, 2 * NZ)
    z = lax.div(lax.rem(lon, 2 * NZ), 2)
    x = lax.rem(lon, 2) * 2 + lax.div(lat, 2)
    core = lax.rem(lat, 2)

    def device(x_at, y_at, z_at, core_at):
        return (y_at * (2 * NZ) + z_at * 2 + lax.div(x_at, 2), lax.rem(x_at, 2) * 2 + core_at)

    across = lax.rem(lon + LON // 2, LON)
    below, above = lat == 0, lat == LAT - 1
    vert = (
        (jnp.where(below, across, lon), jnp.where(below, lat, lat - 1)),
        (jnp.where(above, across, lon), jnp.where(above, lat, lat + 1)),
    )
    seen = (jnp.where(below, 0, 1), jnp.where(above, 1, 0))

    def west_of(at):
        return (lax.rem(at[0] + LON - 1, LON), at[1])

    def east_of(at):
        return (lax.rem(at[0] + 1, LON), at[1])

    here = (lon, lat)
    west, east = west_of(here), east_of(here)
    diagonal = [
        (west_of(vert[0]), 2 * seen[0] + 1),
        (east_of(vert[0]), 2 * seen[0]),
        (west_of(vert[1]), 2 * seen[1] + 1),
        (east_of(vert[1]), 2 * seen[1]),
    ]

    load1 = pltpu.make_async_copy(w1_hbm, w1, w_sem.at[0])
    load2 = pltpu.make_async_copy(w2_hbm, w2, w_sem.at[1])
    load1.start()
    load2.start()

    barrier = pltpu.get_barrier_semaphore()
    partners = [vert[0], vert[1], west, east] + [d[0] for d in diagonal]
    partners.append(device(x, y, z, 1 - core))
    for d in (1, 2, 3):
        partners.append(device(lax.rem(x + d, NX), y, z, core))
        partners.append(device(x, lax.rem(y + d, NY), z, core))
    for d in range(1, NZ):
        partners.append(device(x, y, lax.rem(z + d, NZ), core))
    for partner in partners:
        pl.semaphore_signal(barrier, inc=1, device_id=partner, device_id_type=MESH)

    picks = [pick_ref[0, 0, s] for s in range(2)]
    flips = [flip_ref[0, 0, s] for s in range(2)]
    rules = [rule_ref[0, 0, k] for k in range(4)]

    row8 = iota((8, 256), 0)
    rules_out[...] = jnp.where(
        row8 == 0, picks[0], jnp.where(row8 == 1, flips[0], jnp.where(row8 == 2, picks[1], flips[1]))
    )

    p, cell = iota((80, 256), 0), iota((80, 256), 1)
    k = p & 15
    want = jnp.where(
        p < 16, k, jnp.where(p < 32, 240 + k, jnp.where(p < 48, 16 * k, jnp.where(p < 64, 16 * k + 15, (
            jnp.where(k == 0, 0, jnp.where(k == 1, 15, jnp.where(k == 2, 240, jnp.where(k == 3, 255, -1))))
        ))))
    )
    take_edges = hot(cell == want).astype(BF)

    halo1[0][...] = mm(take_edges, feat_ref[...]).astype(BF)
    halo1[1][224:256, :] = jnp.zeros((32, C1), BF)
    halo2[1][224:256, :] = jnp.zeros((32, C2), BF)

    pl.semaphore_wait(barrier, len(partners))

    def halo_sends(halo):
        out, got, send, recv = halo[:4]
        copies = []
        for side in range(2):
            copies.append(remote(out.at[0:64], got.at[pl.ds(pl.multiple_of(64 * seen[side], 64), 64)],
                                 send.at[side], recv.at[seen[side]], vert[side]))
        copies.append(remote(out.at[32:48], got.at[144:160], send.at[2], recv.at[3], west))
        copies.append(remote(out.at[48:64], got.at[128:144], send.at[3], recv.at[2], east))
        for i, (target, slot) in enumerate(diagonal):
            copies.append(remote(out.at[64:80], got.at[pl.ds(pl.multiple_of(160 + 16 * slot, 16), 16)],
                                 send.at[4 + i], recv.at[4 + slot], target))
        for copy in copies:
            copy.start()
        return copies

    def halo_waits(halo):
        out, got, send, recv = halo[:4]
        spots = [(0, 64), (64, 64), (128, 16), (144, 16), (160, 16), (176, 16), (192, 16), (208, 16)]
        for i, (at, size) in enumerate(spots):
            remote(out.at[0:size], got.at[at:at + size], send.at[i], recv.at[i], west).wait_recv()

    rule_copies = []
    for i, (target, slot) in enumerate(((vert[0], seen[0]), (vert[1], seen[1]), (west, 3), (east, 2))):
        rule_copies.append(remote(rules_out, rules_in.at[slot], rule_send.at[i], rule_recv.at[slot], target))
    for copy in rule_copies:
        copy.start()
    sent = halo_sends(halo1)

    r, c = iota((288, 256), 0), iota((288, 256), 1)
    j, i = r & 15, r >> 4
    want = jnp.where(j == 0, 127 + i, jnp.where(j == 15, 143 + i, -1))
    q_fwd[0:288, :] = hot(c == want).astype(BF)
    r, c = iota((32, 256), 0), iota((32, 256), 1)
    k, north = r & 15, r >= 16
    flip = jnp.where(north, flips[1], flips[0])
    pick = jnp.where(north, picks[1], picks[0])
    want = jnp.where(north, 64, 0) + 16 * pick + jnp.where(flip == 1, 15 - k, k)
    q_fwd[288:320, :] = hot(c == want).astype(BF)

    p, q = iota((128, 384), 0), iota((128, 384), 1)
    block, k = p >> 4, p & 15
    low, high = k == 0, k == 15
    corner_at = (0, 15, 272, 287)
    want = jnp.where(block == 0, 288 + k, jnp.where(block == 1, 304 + k, jnp.where(
        block == 2, 16 * k + 16, jnp.where(block == 3, 16 * k + 31, -1))))
    half = jnp.full_like(want, -1)
    ends = ((0, 1), (2, 3), (0, 2), (1, 3))
    for b in range(4):
        first, second = ends[b]
        half = jnp.where((block == b) & low & (rules[first] == 1), corner_at[first], half)
        half = jnp.where((block == b) & high & (rules[second] == 1), corner_at[second], half)
        want = jnp.where((block == 4 + b) & low & (rules[b] != 1), corner_at[b], want)
    q_back[...] = (hot(q == want) + hot(q == half, 0.5)).astype(BF)

    for halo in (halo1, halo2):
        g_pad = halo[6]
        g_pad[0:32, :] = jnp.zeros((32, C2), BF)
        g_pad[288:416, :] = jnp.zeros((128, C2), BF)
        halo[8][320:384, :] = jnp.zeros((64, halo[8].shape[1]), BF)

    red2 = Reduce(M2, 0, red2_refs, (x, y, z, core, device))
    red1 = Reduce(M1, 9, red1_refs, (x, y, z, core, device))
    red1.halves[:, 40:48] = jnp.zeros((2, 8, 16, 128), BF)

    for slot in range(4):
        remote(rules_out, rules_in.at[slot], rule_send.at[slot], rule_recv.at[slot], west).wait_recv()

    r, c = iota((16, 256), 0), iota((16, 256), 1)
    for side in range(2):
        def source(position):
            return 64 * side + 16 * picks[side] + jnp.where(flips[side] == 1, 15 - position, position)

        rows = 2 * side
        w_pick, w_flip = rules_in[2, rows:rows + 1, :], rules_in[2, rows + 1:rows + 2, :]
        e_pick, e_flip = rules_in[3, rows:rows + 1, :], rules_in[3, rows + 1:rows + 2, :]
        w_at = 160 + 32 * side + corner_slot(w_pick, jnp.where(w_flip == 1, 0, 1))
        e_at = 176 + 32 * side + corner_slot(e_pick, jnp.where(e_flip == 1, 1, 0))
        w_rule, e_rule = rules[2 * side] == 1, rules[2 * side + 1] == 1
        shape = (16, 256)
        w_main = jnp.where(w_rule, jnp.full(shape, -1), jnp.broadcast_to(w_at, shape))
        e_main = jnp.where(e_rule, jnp.full(shape, -1), jnp.broadcast_to(e_at, shape))
        w_a, w_c = jnp.where(w_rule, source(0), -1), jnp.where(w_rule, 128 + 15 * side, -1)
        e_a, e_c = jnp.where(e_rule, source(15), -1), jnp.where(e_rule, 144 + 15 * side, -1)
        w_row = hot(c == w_main) + hot(c == w_a, 0.5) + hot(c == w_c, 0.5)
        e_row = hot(c == e_main) + hot(c == e_a, 0.5) + hot(c == e_c, 0.5)
        values = jnp.where(r == 0, w_row, jnp.where(r == 15, e_row, 0.0))
        q_fwd[272 * side:272 * side + 16, :] = values.astype(BF)

    face = (jnp.where(below, 0, 1), jnp.where(above, 1, 0))
    facing = []
    for side in range(2):
        south = face[side] == 0
        facing.append((
            jnp.where(south, rules_in[side, 0:1, 0:128], rules_in[side, 2:3, 0:128]),
            jnp.where(south, rules_in[side, 1:2, 0:128], rules_in[side, 3:4, 0:128]),
        ))
    p = iota((1, 128), 1)
    block, k = p >> 4, p & 15
    on_north = (block == 1) | (block >= 6)
    pick = jnp.where(on_north, facing[1][0], facing[0][0])
    flip = jnp.where(on_north, facing[1][1], facing[0][1])
    position = jnp.where(block < 2, k, jnp.where((block & 1) == 1, 15, 0))
    position = jnp.where(flip == 1, 15 - position, position)
    target = jnp.where(pick == 0, position, jnp.where(pick == 1, 240 + position, jnp.where(
        pick == 2, 16 * position, 16 * position + 15)))
    target = jnp.where(block == 2, 16 * k + 15, jnp.where(block == 3, 16 * k, target))
    target = jnp.where((block >= 4) & (k != 0), -1, target)
    place_grads = hot(iota((256, 128), 0) == target).astype(BF)

    def pad_tile(halo, tile, channels):
        got, ext, padded = halo[1], halo[4], halo[5]
        cells = mm(q_fwd[...], got[...])
        south, north = cells[288:304], cells[304:320]
        ext[8:24, :] = south
        ext[24:280, :] = tile.astype(F32)
        ext[280:296, :] = north
        j = iota((288, channels), 0) & 15
        padded[:, 0:channels] = jnp.where(j == 0, cells[0:288], ext[7:295, :]).astype(BF)
        padded[:, channels:2 * channels] = ext[8:296, :].astype(BF)
        padded[:, 2 * channels:] = jnp.where(j == 15, cells[0:288], ext[9:297, :]).astype(BF)

    def convolve(halo, weight):
        padded = halo[5]
        total = mm(padded[0:256, :], weight[0])
        for dh in (1, 2):
            total = total + mm(padded[16 * dh:16 * dh + 256, :], weight[dh])
        return total

    def input_side(halo, weight, channels):
        g_pad, by_shift, leaving, out = halo[6], halo[7], halo[8], halo[9]
        total = mm_nt(g_pad[32:320, :], weight[0])
        for dh in (1, 2):
            at = 32 - 16 * dh
            total = total + mm_nt(g_pad[at:at + 288, :], weight[dh])
        by_shift[8:296, :] = total
        j = iota((288, channels), 0) & 15
        centre = by_shift[8:296, channels:2 * channels]
        centre = centre + jnp.where(j == 15, 0.0, by_shift[9:297, 0:channels])
        centre = centre + jnp.where(j == 0, 0.0, by_shift[7:295, 2 * channels:])
        centre = centre.astype(BF)
        sides = jnp.where(j == 0, by_shift[8:296, 0:channels], by_shift[8:296, 2 * channels:])
        sides = jnp.where((j == 0) | (j == 15), sides, 0.0)
        leaving[0:288, :] = sides.astype(BF)
        leaving[288:304, :] = centre[0:16]
        leaving[304:320, :] = centre[272:288]
        out[...] = mm(q_back[...], leaving[...]).astype(BF)
        return centre[16:272]

    def grad_sends(halo):
        out, got, send, recv = halo[9:13]
        copies = []
        for side in range(2):
            copies.append(remote(out.at[16 * side:16 * side + 16],
                                 got.at[pl.ds(pl.multiple_of(16 * seen[side], 16), 16)],
                                 send.at[side], recv.at[seen[side]], vert[side]))
        copies.append(remote(out.at[32:48], got.at[32:48], send.at[2], recv.at[2], west))
        copies.append(remote(out.at[48:64], got.at[48:64], send.at[3], recv.at[3], east))
        for i, (target_at, slot) in enumerate(diagonal):
            copies.append(remote(out.at[64 + 16 * i:80 + 16 * i],
                                 got.at[pl.ds(pl.multiple_of(64 + 16 * slot, 16), 16)],
                                 send.at[4 + i], recv.at[4 + slot], target_at))
        for copy in copies:
            copy.start()
        return copies

    def grad_waits(halo):
        out, got, send, recv = halo[9:13]
        for i in range(8):
            remote(out.at[0:16], got.at[16 * i:16 * i + 16], send.at[i], recv.at[i], west).wait_recv()

    def weight_grads(halo, halves, channels, starts):
        padded, g_pad = halo[5], halo[6]
        units = channels // 16
        gradient = g_pad[32:288, :]
        for dh in range(3):
            for dw in range(3):
                tap = 3 * dh + dw
                block = mm_tn(padded[16 * dh:16 * dh + 256, dw * channels:(dw + 1) * channels], gradient)
                block = block.astype(BF)
                for h in range(2):
                    halves[h, starts[tap]:starts[tap] + units] = (
                        block[:, 128 * h:128 * h + 128].reshape(units, 16, 128)
                    )

    halo_waits(halo1)
    pad_tile(halo1, feat_ref[...], C1)
    load1.wait()
    pre1 = convolve(halo1, w1)
    cdf1 = normal_cdf(pre1)
    act1 = (pre1 * cdf1).astype(BF)
    halo2[0][...] = mm(take_edges, act1).astype(BF)
    sent += halo_sends(halo2)
    slope1[...] = gelu_slope(pre1, cdf1)
    r, c = iota((256, 64), 0), iota((256, 64), 1)
    spread = hot(c == 8 * (r >> 5) + ((r & 15) >> 1), 0.25).astype(BF)
    cot = mm(spread, cot_ref[...])
    load2.wait()

    halo_waits(halo2)
    pad_tile(halo2, act1, C2)
    second_pre = convolve(halo2, w2)
    cdf2 = normal_cdf(second_pre)
    halo2[6][32:288, :] = (cot * gelu_slope(second_pre, cdf2)).astype(BF)
    centre2 = input_side(halo2, w2, C2)
    sent += grad_sends(halo2)
    pre2[...] = second_pre * cdf2
    weight_grads(halo2, red2.halves, C2, [16 * tap for tap in range(9)])
    red2.core_send()

    grad_waits(halo2)
    first_grad = centre2.astype(F32) + mm(place_grads, halo2[10][...])
    halo1[6][32:288, :] = (first_grad * slope1[...]).astype(BF)
    weight_grads(halo1, red1.halves, C1, [8 * tap + (8 if tap >= 5 else 0) for tap in range(9)])
    red1.core_send()
    red2.core_add()
    red2.first_send()
    centre1 = input_side(halo1, w1, C1)
    sent += grad_sends(halo1)
    red1.core_add()
    red1.first_send()
    red2.first_add()
    red2.second_send()
    red1.first_add()
    red1.second_send()
    red2.second_add()
    red2.z_send()
    red1.second_add()
    red1.z_send()

    r, c = iota((64, 256), 0), iota((64, 256), 1)
    gather_cells = hot(r == 8 * (c >> 5) + ((c & 15) >> 1), 0.25).astype(BF)
    act2 = pre2[...]
    high = act2.astype(BF)
    low = (act2 - high.astype(F32)).astype(BF)
    pooled_ref[...] = (mm(gather_cells, high) + mm(gather_cells, low)).astype(BF)

    grad_waits(halo1)
    grad_ref[...] = (centre1.astype(F32) + mm(place_grads, halo1[10][...])).astype(BF)

    red2.z_add_and_gather()
    red1.z_add_and_gather()
    red2.gather_second()
    red1.gather_second()
    red2.gather_first()
    red1.gather_first()
    red2.gather_core()
    red1.gather_core()
    red2.gather_done()
    red1.gather_done()

    def squares(ref, at, count, total):
        def body(i, total):
            values = ref[:, pl.ds(at + i * 8, 8)].astype(F32)
            return total + jnp.sum(values * values, axis=(0, 1))

        return lax.fori_loop(0, count // 8, body, total)

    total = jnp.zeros((16, 128), F32)
    total = squares(red2.out, 0, 144, total)
    for at, _, count in FIRST_ROWS:
        total = squares(red1.out, at, count, total)
    squared = jnp.sum(jnp.sum(total, axis=0, keepdims=True), axis=1, keepdims=True)
    target_norm = math.sqrt(9.0 * (C1 + C2) * C2)
    scale = jnp.broadcast_to(target_norm / jnp.sqrt(squared + 1e-06), (16, 128))

    def write(ref, at, to, count, out):
        def body(i, carry):
            for h in range(2):
                values = ref[h, pl.ds(at + i * 8, 8)].astype(F32) * scale
                rows = pl.ds(pl.multiple_of((to + i * 8) * 16, 128), 128)
                out[rows, 128 * h:128 * h + 128] = values.astype(BF).reshape(128, 128)
            return carry

        lax.fori_loop(0, count // 8, body, 0)

    write(red2.out, 0, 0, 144, second_ref)
    for at, to, count in FIRST_ROWS:
        write(red1.out, at, to, count, first_ref)

    for copy in sent + rule_copies:
        copy.wait_send()
    for red in (red2, red1):
        red.finish()
        red.z_send_done()
        red.z_gather_sent()


def on_device(features, conv_first, conv_second, cotangent, edge_pick, edge_flip, corner_rule):
    vmem = pl.BlockSpec(memory_space=pltpu.VMEM)
    smem = pl.BlockSpec(memory_space=pltpu.SMEM)
    hbm = pl.BlockSpec(memory_space=pl.ANY)
    pooled, input_grad, first, second = pl.pallas_call(
        step_kernel,
        out_shape=(
            jax.ShapeDtypeStruct((64, C2), BF),
            jax.ShapeDtypeStruct((256, C1), BF),
            jax.ShapeDtypeStruct((9 * C1, C2), BF),
            jax.ShapeDtypeStruct((9 * C2, C2), BF),
        ),
        in_specs=[vmem, hbm, hbm, vmem, smem, smem, smem],
        out_specs=[vmem, vmem, vmem, vmem],
        scratch_shapes=(
            halo_scratch(C1)
            + halo_scratch(C2)
            + reduce_scratch(*M2)
            + reduce_scratch(*M1)
            + [
                pltpu.VMEM((3, 3 * C1, C2), BF),
                pltpu.VMEM((3, 3 * C2, C2), BF),
                pltpu.SemaphoreType.DMA((2,)),
                pltpu.VMEM((8, 256), jnp.int32),
                pltpu.VMEM((4, 8, 256), jnp.int32),
                pltpu.SemaphoreType.DMA((4,)),
                pltpu.SemaphoreType.DMA((4,)),
                pltpu.VMEM((320, 256), BF),
                pltpu.VMEM((128, 384), BF),
                pltpu.VMEM((256, C2), F32),
                pltpu.VMEM((256, C2), F32),
            ]
        ),
        compiler_params=pltpu.CompilerParams(
            collective_id=0, has_side_effects=True, vmem_limit_bytes=40 * 1024 * 1024
        ),
        name="level_step",
    )(
        features.reshape(256, C1),
        conv_first.reshape(3, 3 * C1, C2),
        conv_second.reshape(3, 3 * C2, C2),
        cotangent.reshape(64, C2),
        edge_pick,
        edge_flip,
        corner_rule,
    )
    return (
        pooled.reshape(1, 1, 8, 8, C2),
        input_grad.reshape(1, 1, 16, 16, C1),
        first.reshape(3, 3, C1, C2),
        second.reshape(3, 3, C2, C2),
    )


def solution(mesh):
    return jax.shard_map(
        on_device,
        mesh=mesh,
        in_specs=(
            P("lon", "lat", None, None, None),
            P(),
            P(),
            P("lon", "lat", None, None, None),
            P("lon", "lat", None),
            P("lon", "lat", None),
            P("lon", "lat", None),
        ),
        out_specs=(P("lon", "lat", None, None, None), P("lon", "lat", None, None, None), P(), P()),
        check_vma=False,
    )
```

time: 641 us -> 89 us (0.14)
  waiting for transfers between devices: 490 us -> 0 us
  Pallas kernels: 0 us -> 79.1 us
  starting transfers between devices: 72.8 us -> 0 us
  between operations: 25.8 us -> 0.66 us
  other arithmetic: 20.8 us -> 0 us
  matrix products: 10.8 us -> 0 us
  local copies, waits for them, and re-layouts: 18.2 us -> 8.96 us
    psum x1 -> x0, waiting for transfers between devices: 461 us -> none  [on_device(): lax.psum((grad_first, grad_second), ('lon', 'lat'))]
    pallas_call x0 -> x1, Pallas kernels: none -> 79.1 us  [on_device(): pl.pallas_call(step_kernel, out_shape=(jax.ShapeDtypeStruct((64, C2), BF)...]
    ppermute x20 -> x0, starting transfers between devices: 72.7 us -> none  [the longest x12 44.4 us: shifted(): return lax.ppermute(value, axis, pairs)]
    ppermute x20 -> x0, waiting for transfers between devices: 29.8 us -> none  [the longest x12 25.9 us: shifted(): return lax.ppermute(value, axis, pairs)]
    dot_general x54 -> x0, matrix products: 10.8 us -> none  [the longest x18 3.86 us: weight_grad(): lax.dot_general(window, flat_grad, (((0,), (0,)), ((), ())), preferred_el...]
  transfers between devices with their start and end apart: 21 -> 0, of which waited for: 9 -> 0; matrix products, arithmetic and copies ran while one was open for 2% -> 0% of each run, Pallas kernels for 0% -> 0%
where the time goes in v1:
time: 89 us; the launch traced here: 88.7 us
  Pallas kernels  79.1 us (89%)
  local copies, waits for them, and re-layouts  8.96 us (10%)
    pallas_call x1, Pallas kernels, on_device(): pl.pallas_call(step_kernel, out_shape=(jax.ShapeDtypeStruct((64, C2), BF)...  79.1 us
    unnamed x18, local copies, waits for them, and re-layouts  8.96 us

profile of v1, /device:TPU:1, one launch (start us, length us, event | category | flops | bytes accessed | tf_op | source)
XLA Modules:
  0.0 88.7 jit_solution(16189850447956001242)
XLA Ops:
  0.6 0.0 copy-start
  0.6 1.3 %copy-done = bf16[3,3,256,256]{3,2,1,0:T(8,128)(2,1)S(1)} copy-done((bf16[3,3,256,256]{3,2,1,0:T(8,128)(2,1)S(1)}, bf16[3,3,256,256]{3,2,1,0:T(8,128)(2,1)}, u32[]{:S(2)}) %copy-start) | copy-done | bytes 1179672
  1.9 0.0 copy-start.1
  1.9 1.1 %copy-done.1 = bf16[3,3,128,256]{3,2,1,0:T(8,128)(2,1)S(1)} copy-done((bf16[3,3,128,256]{3,2,1,0:T(8,128)(2,1)S(1)}, bf16[3,3,128,256]{3,2,1,0:T(8,128)(2,1)}, u32[]{:S(2)}) %copy-start.1) | copy-done | bytes 589848
  3.0 0.0 copy-start.2
  3.0 0.8 copy-done.2
  3.8 0.0 copy-start.3
  3.8 0.8 copy-done.3
  4.6 0.0 copy-start.4
  4.6 0.7 copy-done.4
  5.2 0.0 copy-start.5
  5.2 0.7 copy-done.5
  5.9 0.0 copy-start.6
  5.9 0.7 copy-done.6
  6.5 79.1 %level_step.1 = (bf16[64,256]{1,0:T(8,128)(2,1)S(1)}, bf16[256,128]{1,0:T(8,128)(2,1)S(1)}, bf16[1152,256]{1,0:T(8,128)(2,1)S(1)}, bf16[2304,256]{1,0:T(8,128)(2,1)S(1)}) custom-call(bf16[256,128]{1,0:T(8,128)(2,1)S(1)} %bitcast.12, bf16[3,384,256]{2,1,0:T(8,128)(2,1)S(1)} %bitcast.11, bf16[3,768,256]{2,1,0:T(8,128)(2,1)S(1)} %bitcast.9, ...), custom_call_target="tpu_custom_call" | custom-call | tf_op jit(solution)/shard_map/level_step/pallas_call | solution.py:720
  85.6 0.6 copy.15
  86.2 0.6 copy.16
  86.9 0.8 copy.17
  87.7 1.0 %copy.18 = bf16[3,3,256,256]{3,2,1,0:T(8,128)(2,1)} copy(bf16[3,3,256,256]{3,2,1,0:T(8,128)(2,1)S(1)} %bitcast.8) | data formatting | bytes 2359296
Async XLA Ops:
  0.6 1.3 %copy-start = (bf16[3,3,256,256]{3,2,1,0:T(8,128)(2,1)S(1)}, bf16[3,3,256,256]{3,2,1,0:T(8,128)(2,1)}, u32[]{:S(2)}) copy-start(bf16[3,3,256,256]{3,2,1,0:T(8,128)(2,1)} %param.9) | copy-start | bytes 3538948
  1.9 1.1 %copy-start.1 = (bf16[3,3,128,256]{3,2,1,0:T(8,128)(2,1)S(1)}, bf16[3,3,128,256]{3,2,1,0:T(8,128)(2,1)}, u32[]{:S(2)}) copy-start(bf16[3,3,128,256]{3,2,1,0:T(8,128)(2,1)} %param.8) | copy-start | bytes 1769476
  3.0 0.8 copy-start.2
  3.8 0.8 copy-start.3
  4.6 0.7 copy-start.4
  5.2 0.7 copy-start.5
  5.9 0.7 copy-start.6

commit v2 on v1

--- a/solution.py
+++ b/solution.py
@@ -307,7 +307,6 @@
         pltpu.VMEM((3, mb, 16, 128), BF),
         pltpu.VMEM((total, 16, 128), BF),
         pltpu.VMEM((NZ - 1, 16, 128), BF),
-        pltpu.VMEM((2, units, 16, 128), BF),
         pltpu.SemaphoreType.DMA((13 + total,)),
         pltpu.SemaphoreType.DMA((13,)),
         pltpu.SemaphoreType.DMA((NZ - 1,)),
@@ -317,7 +316,7 @@
     ]
 
 
-N_REDUCE = 18
+N_REDUCE = 17
 M2 = (5, 4)
 M1 = (3, 2)
 FIRST_ROWS = ((0, 0, 40), (48, 40, 32))
@@ -345,14 +344,17 @@
 
 
 def step_kernel(*refs):
-    (feat_ref, w1_hbm, w2_hbm, cot_ref, pick_ref, flip_ref, rule_ref,
-     pooled_ref, grad_ref, first_ref, second_ref) = refs[:11]
+    (feat_hbm, w1_hbm, w2_hbm, cot_hbm, pick_hbm, flip_hbm, rule_hbm,
+     pooled_ref, grad_ref, first_out, second_out) = refs[:11]
     refs = refs[11:]
     halo1, refs = refs[:N_HALO], refs[N_HALO:]
     halo2, refs = refs[:N_HALO], refs[N_HALO:]
     red2_refs, refs = refs[:N_REDUCE], refs[N_REDUCE:]
     red1_refs, refs = refs[:N_REDUCE], refs[N_REDUCE:]
-    (w1, w2, w_sem, rules_out, rules_in, rule_send, rule_recv, q_fwd, q_back, slope1, pre2) = refs
+    (feat_ref, w1, w2, cot_ref, pick_ref, flip_ref, rule_ref, load_sem,
+     rules_out, rules_in, rule_send, rule_recv, q_fwd, q_back, slope1, pre2) = refs
+    red2_refs = red2_refs[:11] + (second_out,) + red2_refs[11:]
+    red1_refs = red1_refs[:11] + (first_out,) + red1_refs[11:]
 
     lon, lat = lax.axis_index("lon"), lax.axis_index("lat")
     y = lax.div(lon, 2 * NZ)
@@ -386,10 +388,15 @@
         (east_of(vert[1]), 2 * seen[1]),
     ]
 
-    load1 = pltpu.make_async_copy(w1_hbm, w1, w_sem.at[0])
-    load2 = pltpu.make_async_copy(w2_hbm, w2, w_sem.at[1])
-    load1.start()
-    load2.start()
+    loads = [
+        pltpu.make_async_copy(src, dst, load_sem.at[n])
+        for n, (src, dst) in enumerate((
+            (pick_hbm, pick_ref), (flip_hbm, flip_ref), (rule_hbm, rule_ref), (feat_hbm, feat_ref),
+            (w1_hbm, w1), (cot_hbm, cot_ref), (w2_hbm, w2),
+        ))
+    ]
+    for load in loads:
+        load.start()
 
     barrier = pltpu.get_barrier_semaphore()
     partners = [vert[0], vert[1], west, east] + [d[0] for d in diagonal]
@@ -402,6 +409,8 @@
     for partner in partners:
         pl.semaphore_signal(barrier, inc=1, device_id=partner, device_id_type=MESH)
 
+    for load in loads[:3]:
+        load.wait()
     picks = [pick_ref[0, 0, s] for s in range(2)]
     flips = [flip_ref[0, 0, s] for s in range(2)]
     rules = [rule_ref[0, 0, k] for k in range(4)]
@@ -420,6 +429,7 @@
     )
     take_edges = hot(cell == want).astype(BF)
 
+    loads[3].wait()
     halo1[0][...] = mm(take_edges, feat_ref[...]).astype(BF)
     halo1[1][224:256, :] = jnp.zeros((32, C1), BF)
     halo2[1][224:256, :] = jnp.zeros((32, C2), BF)
@@ -612,7 +622,7 @@
 
     halo_waits(halo1)
     pad_tile(halo1, feat_ref[...], C1)
-    load1.wait()
+    loads[4].wait()
     pre1 = convolve(halo1, w1)
     cdf1 = normal_cdf(pre1)
     act1 = (pre1 * cdf1).astype(BF)
@@ -621,8 +631,9 @@
     slope1[...] = gelu_slope(pre1, cdf1)
     r, c = iota((256, 64), 0), iota((256, 64), 1)
     spread = hot(c == 8 * (r >> 5) + ((r & 15) >> 1), 0.25).astype(BF)
+    loads[5].wait()
     cot = mm(spread, cot_ref[...])
-    load2.wait()
+    loads[6].wait()
 
     halo_waits(halo2)
     pad_tile(halo2, act1, C2)
@@ -676,6 +687,21 @@
     red2.gather_done()
     red1.gather_done()
 
+    for copy in sent + rule_copies:
+        copy.wait_send()
+    for red in (red2, red1):
+        red.finish()
+        red.z_send_done()
+        red.z_gather_sent()
+
+
+def finish_kernel(pooled_ref, grad_ref, first_ref, second_ref, pooled_out, grad_out, first_out, second_out,
+                  first_rows, second_rows, sems):
+    copies = [pltpu.make_async_copy(pooled_ref, pooled_out, sems.at[0]),
+              pltpu.make_async_copy(grad_ref, grad_out, sems.at[1])]
+    for copy in copies:
+        copy.start()
+
     def squares(ref, at, count, total):
         def body(i, total):
             values = ref[:, pl.ds(at + i * 8, 8)].astype(F32)
@@ -683,10 +709,9 @@
 
         return lax.fori_loop(0, count // 8, body, total)
 
-    total = jnp.zeros((16, 128), F32)
-    total = squares(red2.out, 0, 144, total)
+    total = squares(second_ref, 0, 144, jnp.zeros((16, 128), F32))
     for at, _, count in FIRST_ROWS:
-        total = squares(red1.out, at, count, total)
+        total = squares(first_ref, at, count, total)
     squared = jnp.sum(jnp.sum(total, axis=0, keepdims=True), axis=1, keepdims=True)
     target_norm = math.sqrt(9.0 * (C1 + C2) * C2)
     scale = jnp.broadcast_to(target_norm / jnp.sqrt(squared + 1e-06), (16, 128))
@@ -701,41 +726,44 @@
 
         lax.fori_loop(0, count // 8, body, 0)
 
-    write(red2.out, 0, 0, 144, second_ref)
-    for at, to, count in FIRST_ROWS:
-        write(red1.out, at, to, count, first_ref)
-
-    for copy in sent + rule_copies:
-        copy.wait_send()
-    for red in (red2, red1):
-        red.finish()
-        red.z_send_done()
-        red.z_gather_sent()
+    jobs = [(second_ref, n * 48, n * 48, 48, second_rows, second_out) for n in range(3)]
+    jobs += [(first_ref, at, to, count, first_rows, first_out) for at, to, count in FIRST_ROWS]
+    for n, (ref, at, to, count, rows, out) in enumerate(jobs):
+        write(ref, at, to, count, rows)
+        span = pl.ds(16 * to, 16 * count)
+        copies.append(pltpu.make_async_copy(rows.at[span], out.at[span], sems.at[2 + n]))
+        copies[-1].start()
+    for copy in copies:
+        copy.wait()
 
 
 def on_device(features, conv_first, conv_second, cotangent, edge_pick, edge_flip, corner_rule):
     vmem = pl.BlockSpec(memory_space=pltpu.VMEM)
-    smem = pl.BlockSpec(memory_space=pltpu.SMEM)
-    hbm = pl.BlockSpec(memory_space=pl.ANY)
+    hbm = pl.BlockSpec(memory_space=pltpu.HBM)
     pooled, input_grad, first, second = pl.pallas_call(
         step_kernel,
         out_shape=(
             jax.ShapeDtypeStruct((64, C2), BF),
             jax.ShapeDtypeStruct((256, C1), BF),
-            jax.ShapeDtypeStruct((9 * C1, C2), BF),
-            jax.ShapeDtypeStruct((9 * C2, C2), BF),
+            jax.ShapeDtypeStruct((2, 16 * sum(M1), 16, 128), BF),
+            jax.ShapeDtypeStruct((2, 16 * sum(M2), 16, 128), BF),
         ),
-        in_specs=[vmem, hbm, hbm, vmem, smem, smem, smem],
-        out_specs=[vmem, vmem, vmem, vmem],
+        in_specs=[hbm] * 7,
+        out_specs=[vmem] * 4,
         scratch_shapes=(
             halo_scratch(C1)
             + halo_scratch(C2)
             + reduce_scratch(*M2)
             + reduce_scratch(*M1)
             + [
+                pltpu.VMEM((256, C1), BF),
                 pltpu.VMEM((3, 3 * C1, C2), BF),
                 pltpu.VMEM((3, 3 * C2, C2), BF),
-                pltpu.SemaphoreType.DMA((2,)),
+                pltpu.VMEM((64, C2), BF),
+                pltpu.SMEM((1, 1, 2), jnp.int32),
+                pltpu.SMEM((1, 1, 2), jnp.int32),
+                pltpu.SMEM((1, 1, 4), jnp.int32),
+                pltpu.SemaphoreType.DMA((7,)),
                 pltpu.VMEM((8, 256), jnp.int32),
                 pltpu.VMEM((4, 8, 256), jnp.int32),
                 pltpu.SemaphoreType.DMA((4,)),
@@ -747,18 +775,39 @@
             ]
         ),
         compiler_params=pltpu.CompilerParams(
-            collective_id=0, has_side_effects=True, vmem_limit_bytes=40 * 1024 * 1024
+            collective_id=0, has_side_effects=True, vmem_limit_bytes=32 * 1024 * 1024
         ),
         name="level_step",
-    )(
-        features.reshape(256, C1),
-        conv_first.reshape(3, 3 * C1, C2),
-        conv_second.reshape(3, 3 * C2, C2),
-        cotangent.reshape(64, C2),
-        edge_pick,
-        edge_flip,
-        corner_rule,
-    )
+    )(*(
+        pltpu.with_memory_space_constraint(value, pltpu.HBM)
+        for value in (
+            features.reshape(256, C1),
+            conv_first.reshape(3, 3 * C1, C2),
+            conv_second.reshape(3, 3 * C2, C2),
+            cotangent.reshape(64, C2),
+            edge_pick,
+            edge_flip,
+            corner_rule,
+        )
+    ))
+    pooled, input_grad, first, second = pl.pallas_call(
+        finish_kernel,
+        out_shape=(
+            jax.ShapeDtypeStruct((64, C2), BF),
+            jax.ShapeDtypeStruct((256, C1), BF),
+            jax.ShapeDtypeStruct((9 * C1, C2), BF),
+            jax.ShapeDtypeStruct((9 * C2, C2), BF),
+        ),
+        in_specs=[vmem] * 4,
+        out_specs=[hbm] * 4,
+        scratch_shapes=[
+            pltpu.VMEM((9 * C1, C2), BF),
+            pltpu.VMEM((9 * C2, C2), BF),
+            pltpu.SemaphoreType.DMA((7,)),
+        ],
+        compiler_params=pltpu.CompilerParams(vmem_limit_bytes=16 * 1024 * 1024),
+        name="scale_outputs",
+    )(pooled, input_grad, first, second)
     return (
         pooled.reshape(1, 1, 8, 8, C2),
         input_grad.reshape(1, 1, 16, 16, C1),

time: 89 us -> 79.9 us (0.90)
  local copies, waits for them, and re-layouts: 8.96 us -> 0 us
    unnamed x18 -> x0, local copies, waits for them, and re-layouts: 8.96 us -> none
    pallas_call x0 -> x1, Pallas kernels: none -> 1.87 us  [on_device(): pl.pallas_call(finish_kernel, out_shape=(jax.ShapeDtypeStruct((64, C2), B...]
    pallas_call x1, Pallas kernels: 79.1 us -> 77.3 us  [on_device(): pl.pallas_call(step_kernel, out_shape=(jax.ShapeDtypeStruct((64, C2), BF)...]
where the time goes in v2:
time: 79.9 us; the launch traced here: 79.8 us
  Pallas kernels  79.1 us (99%)
    pallas_call x1, Pallas kernels, on_device(): pl.pallas_call(step_kernel, out_shape=(jax.ShapeDtypeStruct((64, C2), BF)...  77.3 us
    pallas_call x1, Pallas kernels, on_device(): pl.pallas_call(finish_kernel, out_shape=(jax.ShapeDtypeStruct((64, C2), B...  1.87 us

profile of v2, /device:TPU:1, one launch (start us, length us, event | category | flops | bytes accessed | tf_op | source)
XLA Modules:
  0.0 79.8 jit_solution(4487079010906941768)
XLA Ops:
  0.6 77.3 %level_step.1 = (bf16[64,256]{1,0:T(8,128)(2,1)S(1)}, bf16[256,128]{1,0:T(8,128)(2,1)S(1)}, bf16[2,80,16,128]{3,2,1,0:T(8,128)(2,1)S(1)}, bf16[2,144,16,128]{3,2,1,0:T(8,128)(2,1)S(1)}) custom-call(bf16[256,128]{1,0:T(8,128)(2,1)} %bitcast.10, bf16[3,384,256]{2,1,0:T(8,128)(2,1)} %bitcast.9, bf16[3,768,256]{2,1,0:T(8,128)(2,1)} %bitcast.8, ...), custom_call_target="tpu_custom_call" | custom-call | tf_op jit(solution)/shard_map/level_step/pallas_call | solution.py:743
  77.9 1.9 %scale_outputs.1 = (bf16[64,256]{1,0:T(8,128)(2,1)}, bf16[256,128]{1,0:T(8,128)(2,1)}, bf16[1152,256]{1,0:T(8,128)(2,1)}, bf16[2304,256]{1,0:T(8,128)(2,1)}) custom-call(bf16[64,256]{1,0:T(8,128)(2,1)S(1)} %get-tuple-element.12.pooled_ref, bf16[256,128]{1,0:T(8,128)(2,1)S(1)} %get-tuple-element.13.grad_ref, ...), custom_call_target="tpu_custom_call" | custom-call | tf_op jit(solution)/shard_map/scale_outputs/pallas_call | solution.py:793

commit v3 on v2

--- a/solution.py
+++ b/solution.py
@@ -29,6 +29,15 @@
 
 def hot(cond, value=1.0):
     return jnp.where(cond, jnp.float32(value), jnp.float32(0.0))
+
+
+def wide(row, count):
+    return jnp.concatenate([row] * count, axis=1)
+
+
+def edge_cell(edge, flip, position):
+    at = jnp.where(flip == 1, 15 - position, position)
+    return jnp.where(edge == 0, at, jnp.where(edge == 1, 240 + at, jnp.where(edge == 2, 16 * at, 16 * at + 15)))
 
 
 def mm(a, b):
@@ -322,14 +331,32 @@
 FIRST_ROWS = ((0, 0, 40), (48, 40, 32))
 
 
-def halo_scratch(channels):
+def edge_scratch(channels):
     return [
         pltpu.VMEM((80, channels), BF),
         pltpu.VMEM((256, channels), BF),
         pltpu.SemaphoreType.DMA((8,)),
         pltpu.SemaphoreType.DMA((8,)),
+    ]
+
+
+def patch_scratch():
+    return [
+        pltpu.VMEM((32, 9 * C1), BF),
+        pltpu.VMEM((2, 32, 3 * C1), BF),
+        pltpu.VMEM((4, 16, C1), BF),
+        pltpu.VMEM((128, 9 * C1), BF),
+        pltpu.VMEM((2, 32, 3 * C1), BF),
+        pltpu.VMEM((4, 16, C1), BF),
+        pltpu.SemaphoreType.DMA((8,)),
+        pltpu.SemaphoreType.DMA((8,)),
+    ]
+
+
+def layer_scratch(channels):
+    return [
         pltpu.VMEM((304, channels), F32),
-        pltpu.VMEM((288, 3 * channels), BF),
+        pltpu.VMEM((384, 3 * channels), BF),
         pltpu.VMEM((416, C2), BF),
         pltpu.VMEM((304, 3 * channels), F32),
         pltpu.VMEM((384, channels), BF),
@@ -340,19 +367,21 @@
     ]
 
 
-N_HALO = 13
+N_EDGE, N_PATCH, N_LAYER = 4, 8, 9
 
 
 def step_kernel(*refs):
     (feat_hbm, w1_hbm, w2_hbm, cot_hbm, pick_hbm, flip_hbm, rule_hbm,
      pooled_ref, grad_ref, first_out, second_out) = refs[:11]
     refs = refs[11:]
-    halo1, refs = refs[:N_HALO], refs[N_HALO:]
-    halo2, refs = refs[:N_HALO], refs[N_HALO:]
+    edges, refs = refs[:N_EDGE], refs[N_EDGE:]
+    patch_refs, refs = refs[:N_PATCH], refs[N_PATCH:]
+    layer1, refs = refs[:N_LAYER], refs[N_LAYER:]
+    layer2, refs = refs[:N_LAYER], refs[N_LAYER:]
     red2_refs, refs = refs[:N_REDUCE], refs[N_REDUCE:]
     red1_refs, refs = refs[:N_REDUCE], refs[N_REDUCE:]
     (feat_ref, w1, w2, cot_ref, pick_ref, flip_ref, rule_ref, load_sem,
-     rules_out, rules_in, rule_send, rule_recv, q_fwd, q_back, slope1, pre2) = refs
+     rules_out, rules_in, rule_send, rule_recv, q_fwd, q_back, q_act, slope1, pre2) = refs
     red2_refs = red2_refs[:11] + (second_out,) + red2_refs[11:]
     red1_refs = red1_refs[:11] + (first_out,) + red1_refs[11:]
 
@@ -415,7 +444,7 @@
     flips = [flip_ref[0, 0, s] for s in range(2)]
     rules = [rule_ref[0, 0, k] for k in range(4)]
 
-    row8 = iota((8, 256), 0)
+    row8 = iota((8, 128), 0)
     rules_out[...] = jnp.where(
         row8 == 0, picks[0], jnp.where(row8 == 1, flips[0], jnp.where(row8 == 2, picks[1], flips[1]))
     )
@@ -430,14 +459,14 @@
     take_edges = hot(cell == want).astype(BF)
 
     loads[3].wait()
-    halo1[0][...] = mm(take_edges, feat_ref[...]).astype(BF)
-    halo1[1][224:256, :] = jnp.zeros((32, C1), BF)
-    halo2[1][224:256, :] = jnp.zeros((32, C2), BF)
+    edges[0][...] = mm(take_edges, feat_ref[...]).astype(BF)
+    edges[1][224:256, :] = jnp.zeros((32, C1), BF)
+    layer1[1][288:384, :] = jnp.zeros((96, 3 * C1), BF)
 
     pl.semaphore_wait(barrier, len(partners))
 
-    def halo_sends(halo):
-        out, got, send, recv = halo[:4]
+    def edge_sends():
+        out, got, send, recv = edges
         copies = []
         for side in range(2):
             copies.append(remote(out.at[0:64], got.at[pl.ds(pl.multiple_of(64 * seen[side], 64), 64)],
@@ -451,8 +480,8 @@
             copy.start()
         return copies
 
-    def halo_waits(halo):
-        out, got, send, recv = halo[:4]
+    def edge_waits():
+        out, got, send, recv = edges
         spots = [(0, 64), (64, 64), (128, 16), (144, 16), (160, 16), (176, 16), (192, 16), (208, 16)]
         for i, (at, size) in enumerate(spots):
             remote(out.at[0:size], got.at[at:at + size], send.at[i], recv.at[i], west).wait_recv()
@@ -462,7 +491,7 @@
         rule_copies.append(remote(rules_out, rules_in.at[slot], rule_send.at[i], rule_recv.at[slot], target))
     for copy in rule_copies:
         copy.start()
-    sent = halo_sends(halo1)
+    sent = edge_sends()
 
     r, c = iota((288, 256), 0), iota((288, 256), 1)
     j, i = r & 15, r >> 4
@@ -475,26 +504,29 @@
     want = jnp.where(north, 64, 0) + 16 * pick + jnp.where(flip == 1, 15 - k, k)
     q_fwd[288:320, :] = hot(c == want).astype(BF)
 
-    p, q = iota((128, 384), 0), iota((128, 384), 1)
-    block, k = p >> 4, p & 15
-    low, high = k == 0, k == 15
-    corner_at = (0, 15, 272, 287)
-    want = jnp.where(block == 0, 288 + k, jnp.where(block == 1, 304 + k, jnp.where(
-        block == 2, 16 * k + 16, jnp.where(block == 3, 16 * k + 31, -1))))
-    half = jnp.full_like(want, -1)
-    ends = ((0, 1), (2, 3), (0, 2), (1, 3))
-    for b in range(4):
-        first, second = ends[b]
-        half = jnp.where((block == b) & low & (rules[first] == 1), corner_at[first], half)
-        half = jnp.where((block == b) & high & (rules[second] == 1), corner_at[second], half)
-        want = jnp.where((block == 4 + b) & low & (rules[b] != 1), corner_at[b], want)
-    q_back[...] = (hot(q == want) + hot(q == half, 0.5)).astype(BF)
-
-    for halo in (halo1, halo2):
-        g_pad = halo[6]
+    def halo_cells(p, q):
+        block, k = p >> 4, p & 15
+        low, high = k == 0, k == 15
+        corner_at = (0, 15, 272, 287)
+        want = jnp.where(block == 0, 288 + k, jnp.where(block == 1, 304 + k, jnp.where(
+            block == 2, 16 * k + 16, jnp.where(block == 3, 16 * k + 31, -1))))
+        half = jnp.full_like(want, -1)
+        ends = ((0, 1), (2, 3), (0, 2), (1, 3))
+        for b in range(4):
+            first, second = ends[b]
+            half = jnp.where((block == b) & low & (rules[first] == 1), corner_at[first], half)
+            half = jnp.where((block == b) & high & (rules[second] == 1), corner_at[second], half)
+            want = jnp.where((block == 4 + b) & low & (rules[b] != 1), corner_at[b], want)
+        return (hot(q == want) + hot(q == half, 0.5)).astype(BF)
+
+    q_back[...] = halo_cells(iota((128, 384), 0), iota((128, 384), 1))
+    q_act[...] = halo_cells(iota((320, 128), 1), iota((320, 128), 0))
+
+    for layer in (layer1, layer2):
+        g_pad = layer[2]
         g_pad[0:32, :] = jnp.zeros((32, C2), BF)
         g_pad[288:416, :] = jnp.zeros((128, C2), BF)
-        halo[8][320:384, :] = jnp.zeros((64, halo[8].shape[1]), BF)
+        layer[4][320:384, :] = jnp.zeros((64, layer[4].shape[1]), BF)
 
     red2 = Reduce(M2, 0, red2_refs, (x, y, z, core, device))
     red1 = Reduce(M1, 9, red1_refs, (x, y, z, core, device))
@@ -509,8 +541,8 @@
             return 64 * side + 16 * picks[side] + jnp.where(flips[side] == 1, 15 - position, position)
 
         rows = 2 * side
-        w_pick, w_flip = rules_in[2, rows:rows + 1, :], rules_in[2, rows + 1:rows + 2, :]
-        e_pick, e_flip = rules_in[3, rows:rows + 1, :], rules_in[3, rows + 1:rows + 2, :]
+        w_pick, w_flip = wide(rules_in[2, rows:rows + 1, :], 2), wide(rules_in[2, rows + 1:rows + 2, :], 2)
+        e_pick, e_flip = wide(rules_in[3, rows:rows + 1, :], 2), wide(rules_in[3, rows + 1:rows + 2, :], 2)
         w_at = 160 + 32 * side + corner_slot(w_pick, jnp.where(w_flip == 1, 0, 1))
         e_at = 176 + 32 * side + corner_slot(e_pick, jnp.where(e_flip == 1, 1, 0))
         w_rule, e_rule = rules[2 * side] == 1, rules[2 * side + 1] == 1
@@ -538,34 +570,88 @@
     pick = jnp.where(on_north, facing[1][0], facing[0][0])
     flip = jnp.where(on_north, facing[1][1], facing[0][1])
     position = jnp.where(block < 2, k, jnp.where((block & 1) == 1, 15, 0))
-    position = jnp.where(flip == 1, 15 - position, position)
-    target = jnp.where(pick == 0, position, jnp.where(pick == 1, 240 + position, jnp.where(
-        pick == 2, 16 * position, 16 * position + 15)))
+    target = edge_cell(pick, flip, position)
     target = jnp.where(block == 2, 16 * k + 15, jnp.where(block == 3, 16 * k, target))
     target = jnp.where((block >= 4) & (k != 0), -1, target)
     place_grads = hot(iota((256, 128), 0) == target).astype(BF)
 
-    def pad_tile(halo, tile, channels):
-        got, ext, padded = halo[1], halo[4], halo[5]
-        cells = mm(q_fwd[...], got[...])
+    r, c = iota((32, 256), 0), iota((32, 256), 1)
+    pick = jnp.where(r < 16, wide(facing[0][0], 2), wide(facing[1][0], 2))
+    flip = jnp.where(r < 16, wide(facing[0][1], 2), wide(facing[1][1], 2))
+    take_cells = hot(c == edge_cell(pick, flip, r & 15)).astype(BF)
+    r, c = iota((64, 384), 0), iota((64, 384), 1)
+    row = r & 31
+    take_strips = hot((row < 18) & (c == 16 * row + jnp.where(r < 32, 15, 0))).astype(BF)
+    tap, which = r & 15, r >> 4
+    tap_row = (tap * 11) >> 5
+    pick = jnp.where(which < 2, wide(facing[0][0], 3), wide(facing[1][0], 3))
+    flip = jnp.where(which < 2, wide(facing[0][1], 3), wide(facing[1][1], 3))
+    at = 16 * tap_row + edge_cell(pick, flip, jnp.where((which & 1) == 1, 15, 0))
+    take_corners = [
+        hot((tap < 9) & (tap - 3 * tap_row == dw) & (c == at)).astype(BF) for dw in range(3)
+    ]
+
+    def patch_sends():
+        cells, strips, corners, got_cells, got_strips, got_corners, send, recv = patch_refs
+        padded = layer1[1]
+        for dh in range(3):
+            cells[:, 384 * dh:384 * dh + 384] = mm(take_cells, padded[16 * dh:16 * dh + 256, :]).astype(BF)
+        strips[...] = mm(take_strips, padded[...]).astype(BF).reshape(2, 32, 3 * C1)
+        values = mm(take_corners[0], padded[:, 0:C1])
+        for dw in (1, 2):
+            values = values + mm(take_corners[dw], padded[:, dw * C1:(dw + 1) * C1])
+        corners[...] = values.astype(BF).reshape(4, 16, C1)
+        copies = []
+        for side in range(2):
+            copies.append(remote(cells.at[16 * side:16 * side + 16],
+                                 got_cells.at[pl.ds(pl.multiple_of(16 * seen[side], 16), 16)],
+                                 send.at[side], recv.at[seen[side]], vert[side]))
+        copies.append(remote(strips.at[0], got_strips.at[0], send.at[2], recv.at[2], east))
+        copies.append(remote(strips.at[1], got_strips.at[1], send.at[3], recv.at[3], west))
+        for i, (target_at, slot) in enumerate(diagonal):
+            copies.append(remote(corners.at[i], got_corners.at[slot], send.at[4 + i], recv.at[4 + slot], target_at))
+        for copy in copies:
+            copy.start()
+        return copies
+
+    def patch_waits():
+        cells, strips, corners, got_cells, got_strips, got_corners, send, recv = patch_refs
+        for i in range(2):
+            remote(cells.at[0:16], got_cells.at[16 * i:16 * i + 16], send.at[i], recv.at[i], west).wait_recv()
+            remote(strips.at[i], got_strips.at[i], send.at[2 + i], recv.at[2 + i], west).wait_recv()
+        r, c = iota((32, 64), 0), iota((32, 64), 1)
+        both = got_strips[...].reshape(64, 3 * C1)
+        for dh in range(3):
+            spread_rows = hot(c == jnp.where(r < 16, r, r + 16) + dh).astype(BF)
+            got_cells[32:64, 384 * dh:384 * dh + 384] = mm(spread_rows, both).astype(BF)
+        for i in range(4):
+            remote(corners.at[i], got_corners.at[i], send.at[4 + i], recv.at[4 + i], west).wait_recv()
+        r, c = iota((64, 64), 0), iota((64, 64), 1)
+        taps = got_corners[...].reshape(64, C1)
+        for tap in range(9):
+            first_row = hot(((r & 15) == 0) & (c == r + tap)).astype(BF)
+            got_cells[64:128, C1 * tap:C1 * tap + C1] = mm(first_row, taps).astype(BF)
+
+    def pad_tile(layer, tile, cells, channels):
+        ext, padded = layer[:2]
         south, north = cells[288:304], cells[304:320]
         ext[8:24, :] = south
         ext[24:280, :] = tile.astype(F32)
         ext[280:296, :] = north
         j = iota((288, channels), 0) & 15
-        padded[:, 0:channels] = jnp.where(j == 0, cells[0:288], ext[7:295, :]).astype(BF)
-        padded[:, channels:2 * channels] = ext[8:296, :].astype(BF)
-        padded[:, 2 * channels:] = jnp.where(j == 15, cells[0:288], ext[9:297, :]).astype(BF)
-
-    def convolve(halo, weight):
-        padded = halo[5]
+        padded[0:288, 0:channels] = jnp.where(j == 0, cells[0:288], ext[7:295, :]).astype(BF)
+        padded[0:288, channels:2 * channels] = ext[8:296, :].astype(BF)
+        padded[0:288, 2 * channels:] = jnp.where(j == 15, cells[0:288], ext[9:297, :]).astype(BF)
+
+    def convolve(layer, weight):
+        padded = layer[1]
         total = mm(padded[0:256, :], weight[0])
         for dh in (1, 2):
             total = total + mm(padded[16 * dh:16 * dh + 256, :], weight[dh])
         return total
 
-    def input_side(halo, weight, channels):
-        g_pad, by_shift, leaving, out = halo[6], halo[7], halo[8], halo[9]
+    def input_side(layer, weight, channels):
+        g_pad, by_shift, leaving, out = layer[2:6]
         total = mm_nt(g_pad[32:320, :], weight[0])
         for dh in (1, 2):
             at = 32 - 16 * dh
@@ -584,8 +670,8 @@
         out[...] = mm(q_back[...], leaving[...]).astype(BF)
         return centre[16:272]
 
-    def grad_sends(halo):
-        out, got, send, recv = halo[9:13]
+    def grad_sends(layer):
+        out, got, send, recv = layer[5:9]
         copies = []
         for side in range(2):
             copies.append(remote(out.at[16 * side:16 * side + 16],
@@ -601,33 +687,31 @@
             copy.start()
         return copies
 
-    def grad_waits(halo):
-        out, got, send, recv = halo[9:13]
+    def grad_waits(layer):
+        out, got, send, recv = layer[5:9]
         for i in range(8):
             remote(out.at[0:16], got.at[16 * i:16 * i + 16], send.at[i], recv.at[i], west).wait_recv()
 
-    def weight_grads(halo, halves, channels, starts):
-        padded, g_pad = halo[5], halo[6]
-        units = channels // 16
-        gradient = g_pad[32:288, :]
+    def weight_grads(halves, channels, spots, pairs):
+        units = 3 * channels // 16
         for dh in range(3):
-            for dw in range(3):
-                tap = 3 * dh + dw
-                block = mm_tn(padded[16 * dh:16 * dh + 256, dw * channels:(dw + 1) * channels], gradient)
-                block = block.astype(BF)
-                for h in range(2):
-                    halves[h, starts[tap]:starts[tap] + units] = (
-                        block[:, 128 * h:128 * h + 128].reshape(units, 16, 128)
-                    )
-
-    halo_waits(halo1)
-    pad_tile(halo1, feat_ref[...], C1)
+            block = None
+            for cells, gradient in pairs(dh):
+                part = mm_tn(cells, gradient)
+                block = part if block is None else block + part
+            block = block.astype(BF)
+            for h in range(2):
+                values = block[:, 128 * h:128 * h + 128].reshape(units, 16, 128)
+                for first, count, to in spots[dh]:
+                    halves[h, to:to + count] = values[first:first + count]
+
+    edge_waits()
+    pad_tile(layer1, feat_ref[...], mm(q_fwd[...], edges[1][...]), C1)
+    sent += patch_sends()
     loads[4].wait()
-    pre1 = convolve(halo1, w1)
+    pre1 = convolve(layer1, w1)
     cdf1 = normal_cdf(pre1)
     act1 = (pre1 * cdf1).astype(BF)
-    halo2[0][...] = mm(take_edges, act1).astype(BF)
-    sent += halo_sends(halo2)
     slope1[...] = gelu_slope(pre1, cdf1)
     r, c = iota((256, 64), 0), iota((256, 64), 1)
     spread = hot(c == 8 * (r >> 5) + ((r & 15) >> 1), 0.25).astype(BF)
@@ -635,36 +719,35 @@
     cot = mm(spread, cot_ref[...])
     loads[6].wait()
 
-    halo_waits(halo2)
-    pad_tile(halo2, act1, C2)
-    second_pre = convolve(halo2, w2)
+    patch_waits()
+    patches = patch_refs[3]
+    halo_pre = mm(patches[:, 0:384], w1[0])
+    for dh in (1, 2):
+        halo_pre = halo_pre + mm(patches[:, 384 * dh:384 * dh + 384], w1[dh])
+    halo_cdf = normal_cdf(halo_pre)
+    halo_act = (halo_pre * halo_cdf).astype(BF)
+    pad_tile(layer2, act1, mm(q_act[...], halo_act), C2)
+    second_pre = convolve(layer2, w2)
     cdf2 = normal_cdf(second_pre)
-    halo2[6][32:288, :] = (cot * gelu_slope(second_pre, cdf2)).astype(BF)
-    centre2 = input_side(halo2, w2, C2)
-    sent += grad_sends(halo2)
+    grad2 = (cot * gelu_slope(second_pre, cdf2)).astype(BF)
+    layer2[2][32:288, :] = grad2
     pre2[...] = second_pre * cdf2
-    weight_grads(halo2, red2.halves, C2, [16 * tap for tap in range(9)])
+    weight_grads(red2.halves, C2, [[(0, 48, 48 * dh)] for dh in range(3)],
+                 lambda dh: [(layer2[1][16 * dh:16 * dh + 256, :], grad2)])
     red2.core_send()
-
-    grad_waits(halo2)
-    first_grad = centre2.astype(F32) + mm(place_grads, halo2[10][...])
-    halo1[6][32:288, :] = (first_grad * slope1[...]).astype(BF)
-    weight_grads(halo1, red1.halves, C1, [8 * tap + (8 if tap >= 5 else 0) for tap in range(9)])
+    centre2 = input_side(layer2, w2, C2)
+    sent += grad_sends(layer2)
+
+    own = (centre2.astype(F32) * slope1[...]).astype(BF)
+    leaving = (layer2[5][...].astype(F32) * gelu_slope(halo_pre, halo_cdf)).astype(BF)
+    weight_grads(red1.halves, C1, [[(0, 24, 0)], [(0, 16, 24), (16, 8, 48)], [(0, 24, 56)]],
+                 lambda dh: [(layer1[1][16 * dh:16 * dh + 256, :], own),
+                             (patches[:, 384 * dh:384 * dh + 384], leaving)])
     red1.core_send()
     red2.core_add()
     red2.first_send()
-    centre1 = input_side(halo1, w1, C1)
-    sent += grad_sends(halo1)
     red1.core_add()
     red1.first_send()
-    red2.first_add()
-    red2.second_send()
-    red1.first_add()
-    red1.second_send()
-    red2.second_add()
-    red2.z_send()
-    red1.second_add()
-    red1.z_send()
 
     r, c = iota((64, 256), 0), iota((64, 256), 1)
     gather_cells = hot(r == 8 * (c >> 5) + ((c & 15) >> 1), 0.25).astype(BF)
@@ -673,8 +756,24 @@
     low = (act2 - high.astype(F32)).astype(BF)
     pooled_ref[...] = (mm(gather_cells, high) + mm(gather_cells, low)).astype(BF)
 
-    grad_waits(halo1)
-    grad_ref[...] = (centre1.astype(F32) + mm(place_grads, halo1[10][...])).astype(BF)
+    red2.first_add()
+    red2.second_send()
+    red1.first_add()
+    red1.second_send()
+
+    grad_waits(layer2)
+    first_grad = centre2.astype(F32) + mm(place_grads, layer2[6][...])
+    layer1[2][32:288, :] = (first_grad * slope1[...]).astype(BF)
+    centre1 = input_side(layer1, w1, C1)
+    sent += grad_sends(layer1)
+
+    red2.second_add()
+    red2.z_send()
+    red1.second_add()
+    red1.z_send()
+
+    grad_waits(layer1)
+    grad_ref[...] = (centre1.astype(F32) + mm(place_grads, layer1[6][...])).astype(BF)
 
     red2.z_add_and_gather()
     red1.z_add_and_gather()
@@ -751,8 +850,10 @@
         in_specs=[hbm] * 7,
         out_specs=[vmem] * 4,
         scratch_shapes=(
-            halo_scratch(C1)
-            + halo_scratch(C2)
+            edge_scratch(C1)
+            + patch_scratch()
+            + layer_scratch(C1)
+            + layer_scratch(C2)
             + reduce_scratch(*M2)
             + reduce_scratch(*M1)
             + [
@@ -764,12 +865,13 @@
                 pltpu.SMEM((1, 1, 2), jnp.int32),
                 pltpu.SMEM((1, 1, 4), jnp.int32),
                 pltpu.SemaphoreType.DMA((7,)),
-                pltpu.VMEM((8, 256), jnp.int32),
-                pltpu.VMEM((4, 8, 256), jnp.int32),
+                pltpu.VMEM((8, 128), jnp.int32),
+                pltpu.VMEM((4, 8, 128), jnp.int32),
                 pltpu.SemaphoreType.DMA((4,)),
                 pltpu.SemaphoreType.DMA((4,)),
                 pltpu.VMEM((320, 256), BF),
                 pltpu.VMEM((128, 384), BF),
+                pltpu.VMEM((320, 128), BF),
                 pltpu.VMEM((256, C2), F32),
                 pltpu.VMEM((256, C2), F32),
             ]

time: 79.9 us -> 75.3 us (0.942)
  Pallas kernels: 79.1 us -> 74.5 us
    pallas_call x1, Pallas kernels: 77.3 us -> 72.7 us  [on_device(): pl.pallas_call(step_kernel, out_shape=(jax.ShapeDtypeStruct((64, C2), BF)...]
where the time goes in v3:
time: 75.3 us; the launch traced here: 75.2 us
  Pallas kernels  74.5 us (99%)
    pallas_call x1, Pallas kernels, on_device(): pl.pallas_call(step_kernel, out_shape=(jax.ShapeDtypeStruct((64, C2), BF)...  72.7 us
    pallas_call x1, Pallas kernels, on_device(): pl.pallas_call(finish_kernel, out_shape=(jax.ShapeDtypeStruct((64, C2), B...  1.87 us

profile of v3, /device:TPU:1, one launch (start us, length us, event | category | flops | bytes accessed | tf_op | source)
XLA Modules:
  0.0 75.2 jit_solution(7949281874068700364)
XLA Ops:
  0.6 72.7 %level_step.1 = (bf16[64,256]{1,0:T(8,128)(2,1)S(1)}, bf16[256,128]{1,0:T(8,128)(2,1)S(1)}, bf16[2,80,16,128]{3,2,1,0:T(8,128)(2,1)S(1)}, bf16[2,144,16,128]{3,2,1,0:T(8,128)(2,1)S(1)}) custom-call(bf16[256,128]{1,0:T(8,128)(2,1)} %bitcast.10, bf16[3,384,256]{2,1,0:T(8,128)(2,1)} %bitcast.9, bf16[3,768,256]{2,1,0:T(8,128)(2,1)} %bitcast.8, ...), custom_call_target="tpu_custom_call" | custom-call | tf_op jit(solution)/shard_map/level_step/pallas_call | solution.py:842
  73.3 1.9 %scale_outputs.1 = (bf16[64,256]{1,0:T(8,128)(2,1)}, bf16[256,128]{1,0:T(8,128)(2,1)}, bf16[1152,256]{1,0:T(8,128)(2,1)}, bf16[2304,256]{1,0:T(8,128)(2,1)}) custom-call(bf16[64,256]{1,0:T(8,128)(2,1)S(1)} %get-tuple-element.12.pooled_ref, bf16[256,128]{1,0:T(8,128)(2,1)S(1)} %get-tuple-element.13.grad_ref, ...), custom_call_target="tpu_custom_call" | custom-call | tf_op jit(solution)/shard_map/scale_outputs/pallas_call | solution.py:895

commit v4 on v3

--- a/solution.py
+++ b/solution.py
@@ -66,25 +66,26 @@
 
 
 class Reduce:
-    def __init__(self, m, z_base, refs, place):
+    def __init__(self, m, refs, place):
         self.m = m
-        self.z_base = z_base
         self.total = m[0] + m[1]
         self.start = (0, 16 * m[0])
-        (self.halves, self.r0, self.a1, self.r1a, self.r1b, self.a2a, self.a2b, self.r2a, self.r2b,
-         self.a3, self.r3, self.out, self.s_send, self.s_recv, self.z_recv, self.g_send, self.g_recv,
-         self.gz_send) = refs
-        self.place = place
+        (self.halves, self.r0, self.a1, r1a, r1b, a2a, a2b, r2a, r2b, self.a3, self.n3, self.f3, self.out,
+         self.s_send, self.s_recv, self.g_send, self.g_recv) = refs
+        self.r1, self.a2, self.r2 = (r1a, r1b), (a2a, a2b), (r2a, r2b)
         self.x, self.y, self.z, self.core, self.device = place
+        self.near, self.far = lax.rem(self.z, 4), lax.div(self.z, 4)
         self.pending = []
+        self.pieces = []
+        self.waited = 0
+
+    def other_core(self):
+        return self.device(self.x, self.y, self.z, 1 - self.core)
 
     def peer(self, axis, d):
-        x, y = self.x, self.y
-        if axis == "x":
-            x = lax.rem(x + d, NX)
-        else:
-            y = lax.rem(y + d, NY)
-        return x, y
+        x = lax.rem(self.x + d, NX) if axis == "x" else self.x
+        y = lax.rem(self.y + d, NY) if axis == "y" else self.y
+        return self.device(x, y, self.z, self.core)
 
     def axes(self, part):
         return ("x", "y") if part == 0 else ("y", "x")
@@ -96,214 +97,169 @@
         copy.start()
         self.pending.append(copy)
 
+    def received(self, ref, sem):
+        remote(ref, ref, self.s_send.at[0], sem, self.other_core()).wait_recv()
+
     def finish(self):
         for copy in self.pending:
             copy.wait_send()
-        self.pending = []
-
-    def core_send(self):
-        self.send(remote(self.halves.at[1 - self.core], self.r0, self.s_send.at[0], self.s_recv.at[0],
-                         self.device(self.x, self.y, self.z, 1 - self.core)))
+
+        @pl.when(self.near < self.total // 2)
+        def _():
+            for copy in self.near_copies():
+                copy.wait_send()
+
+    def core_send(self, at, count):
+        k = len(self.pieces)
+        self.pieces.append((at, count))
+        self.send(remote(self.halves.at[1 - self.core, at:at + count], self.r0.at[at:at + count],
+                         self.s_send.at[k], self.s_recv.at[k], self.other_core()))
 
     def core_add(self):
-        remote(self.halves.at[0], self.r0, self.s_send.at[0], self.s_recv.at[0],
-               self.device(self.x, self.y, self.z, 1 - self.core)).wait_recv()
-        units = 16 * self.total
-
-        step = 8
-
-        def body(i, carry):
-            at = pl.ds(i * step, step)
-            self.a1[at] = (self.halves[self.core, at].astype(F32) + self.r0[at].astype(F32)).astype(BF)
-            return carry
-
-        lax.fori_loop(0, units // step, body, 0)
-
-    def first_send(self):
         for part in range(2):
             n = 4 * self.m[part]
-            r1 = (self.r1a, self.r1b)[part]
             mine = self.coords(part)[0]
-            for d in (2, 1, 3):
-                x, y = self.peer(self.axes(part)[0], d)
-                block = lax.rem(mine + d, 4)
-                k = 1 + part * 3 + d - 1
-                self.send(remote(self.a1.at[pl.ds(self.start[part] + block * n, n)], r1.at[d - 1],
-                                 self.s_send.at[k], self.s_recv.at[k], self.device(x, y, self.z, self.core)))
+            while self.waited < len(self.pieces) and self.pieces[self.waited][0] < self.start[part] + 4 * n:
+                at, count = self.pieces[self.waited]
+                self.received(self.r0.at[at:at + count], self.s_recv.at[self.waited])
+                self.waited += 1
+            for d in (2, 1, 3, 0):
+                at = pl.ds(self.start[part] + lax.rem(mine + d, 4) * n, n)
+                self.a1[at] = (self.halves[self.core, at].astype(F32) + self.r0[at].astype(F32)).astype(BF)
+                if d:
+                    k = 3 + part * 3 + d - 1
+                    self.send(remote(self.a1.at[at], self.r1[part].at[d - 1], self.s_send.at[k], self.s_recv.at[k],
+                                     self.peer(self.axes(part)[0], d)))
 
     def first_add(self):
         for part in range(2):
-            n = 4 * self.m[part]
-            r1 = (self.r1a, self.r1b)[part]
-            a2 = (self.a2a, self.a2b)[part]
-            mine = self.coords(part)[0]
-            for d in (1, 2, 3):
-                k = 1 + part * 3 + d - 1
-                remote(r1.at[d - 1], r1.at[d - 1], self.s_send.at[k], self.s_recv.at[k],
-                       self.device(self.x, self.y, self.z, 1 - self.core)).wait_recv()
-            step = self.m[part]
-
-            def body(i, carry):
-                at = pl.ds(i * step, step)
-                total = self.a1[pl.ds(self.start[part] + mine * n + i * step, step)].astype(F32)
-                for d in range(3):
-                    total = total + r1[d, at].astype(F32)
+            m = self.m[part]
+            r1, a2, r2 = self.r1[part], self.a2[part], self.r2[part]
+            ca, cb = self.coords(part)
+            for d in (1, 3, 2):
+                self.received(r1.at[d - 1], self.s_recv.at[3 + part * 3 + d - 1])
+            for d in (2, 1, 3, 0):
+                block = lax.rem(cb + d, 4)
+                at = pl.ds(block * m, m)
+                total = self.a1[pl.ds(self.start[part] + (ca * 4 + block) * m, m)].astype(F32)
+                for e in range(3):
+                    total = total + r1[e, at].astype(F32)
                 a2[at] = total.astype(BF)
-                return carry
-
-            lax.fori_loop(0, 4, body, 0)
-
-    def second_send(self):
-        for part in range(2):
-            m = self.m[part]
-            a2 = (self.a2a, self.a2b)[part]
-            r2 = (self.r2a, self.r2b)[part]
-            mine = self.coords(part)[1]
-            for d in (2, 1, 3):
-                x, y = self.peer(self.axes(part)[1], d)
-                block = lax.rem(mine + d, 4)
-                k = 7 + part * 3 + d - 1
-                self.send(remote(a2.at[pl.ds(block * m, m)], r2.at[d - 1],
-                                 self.s_send.at[k], self.s_recv.at[k], self.device(x, y, self.z, self.core)))
+                if d:
+                    k = 9 + part * 3 + d - 1
+                    self.send(remote(a2.at[at], r2.at[d - 1], self.s_send.at[k], self.s_recv.at[k],
+                                     self.peer(self.axes(part)[1], d)))
 
     def second_add(self):
         for part in range(2):
             m = self.m[part]
-            a2 = (self.a2a, self.a2b)[part]
-            r2 = (self.r2a, self.r2b)[part]
-            mine = self.coords(part)[1]
-            for d in (1, 2, 3):
-                k = 7 + part * 3 + d - 1
-                remote(r2.at[d - 1], r2.at[d - 1], self.s_send.at[k], self.s_recv.at[k],
-                       self.device(self.x, self.y, self.z, 1 - self.core)).wait_recv()
-            total = a2[pl.ds(mine * m, m)].astype(F32)
-            for d in range(3):
-                total = total + r2[d].astype(F32)
-            self.a3[pl.ds(part * self.m[0], m)] = total.astype(BF)
-
-    def z_send(self):
-        for u in range(self.total):
-            owner = self.z_base + u
-            away = lax.rem(self.z - owner + NZ, NZ)
-
-            @pl.when(away != 0)
-            def _():
-                remote(self.a3.at[u], self.r3.at[away - 1], self.s_send.at[13 + u], self.z_recv.at[away - 1],
-                       self.device(self.x, self.y, owner, self.core)).start()
-
-    def z_send_done(self):
-        for u in range(self.total):
-            @pl.when(self.z != self.z_base + u)
-            def _():
-                remote(self.a3.at[u], self.r3.at[0], self.s_send.at[13 + u], self.z_recv.at[0],
-                       self.device(self.x, self.y, self.z_base + u, self.core)).wait_send()
+            a2, r2 = self.a2[part], self.r2[part]
+            cb = self.coords(part)[1]
+            for d in (1, 3, 2):
+                self.received(r2.at[d - 1], self.s_recv.at[9 + part * 3 + d - 1])
+            total = a2[pl.ds(cb * m, m)].astype(F32)
+            for e in range(3):
+                total = total + r2[e].astype(F32)
+            self.a3[part * self.m[0]:part * self.m[0] + m] = total.astype(BF)
+        for d in (2, 1, 3):
+            owner = lax.rem(self.near + d, 4)
+            self.send(remote(self.a3.at[pl.ds(2 * owner, 2)], self.n3.at[d - 1], self.s_send.at[14 + d],
+                             self.s_recv.at[14 + d], self.device(self.x, self.y, 4 * self.far + owner, self.core)))
+
+    def near_add(self):
+        for d in (1, 3, 2):
+            self.received(self.n3.at[d - 1], self.s_recv.at[14 + d])
+        total = self.a3[pl.ds(2 * self.near, 2)].astype(F32)
+        for e in range(3):
+            total = total + self.n3[e].astype(F32)
+        self.f3[self.far] = total.astype(BF)
+        for d in (2, 1, 3):
+            self.send(remote(self.f3.at[self.far], self.f3.at[self.far], self.s_send.at[17 + d], self.s_recv.at[17 + d],
+                             self.device(self.x, self.y, 4 * lax.rem(self.far + d, 4) + self.near, self.core)))
 
     def unit_at(self, u):
         ma, mb = self.m
         first = (self.x * 4 + self.y) * ma + u
         second = self.start[1] + (self.y * 4 + self.x) * mb + u - ma
-        if isinstance(u, int):
-            return first if u < ma else second
         return jnp.where(u < ma, first, second)
 
-    def owner(self):
-        return jnp.logical_and(self.z >= self.z_base, self.z < self.z_base + self.total)
-
-    def z_add_and_gather(self):
-        mine = self.z - self.z_base
-
-        @pl.when(self.owner())
+    def near_copies(self):
+        at = pl.ds(self.unit_at(2 * self.near), 2)
+        return [
+            remote(self.out.at[self.core, at], self.out.at[self.core, at], self.g_send.at[19 + d], self.g_recv.at[19 + d],
+                   self.device(self.x, self.y, 4 * self.far + lax.rem(self.near + d, 4), self.core))
+            for d in (2, 1, 3)
+        ]
+
+    def far_add(self):
+        for d in (1, 3, 2):
+            self.received(self.f3.at[lax.rem(self.far + 4 - d, 4)], self.s_recv.at[17 + d])
+
+        @pl.when(self.near < self.total // 2)
         def _():
-            for d in range(1, NZ):
-                remote(self.r3.at[d - 1], self.r3.at[d - 1], self.s_send.at[13], self.z_recv.at[d - 1],
-                       self.device(self.x, self.y, self.z, 1 - self.core)).wait_recv()
-            total = self.a3[mine].astype(F32)
-            for d in range(NZ - 1):
-                total = total + self.r3[d].astype(F32)
-            at = self.unit_at(mine)
-            self.out[self.core, at] = total.astype(BF)
-            for d in (8, 7, 9, 6, 10, 5, 11, 4, 12, 3, 13, 2, 14, 1, 15):
-                remote(self.out.at[self.core, at], self.out.at[self.core, at], self.gz_send.at[d - 1],
-                       self.g_recv.at[mine],
-                       self.device(self.x, self.y, lax.rem(self.z + d, NZ), self.core)).start()
-
-    def z_gather_sent(self):
-        mine = self.z - self.z_base
-
-        @pl.when(self.owner())
-        def _():
-            at = self.unit_at(mine)
-            for d in range(1, NZ):
-                remote(self.out.at[self.core, at], self.out.at[self.core, at], self.gz_send.at[d - 1],
-                       self.g_recv.at[mine],
-                       self.device(self.x, self.y, lax.rem(self.z + d, NZ), self.core)).wait_send()
+            total = self.f3[0].astype(F32)
+            for e in range(1, 4):
+                total = total + self.f3[e].astype(F32)
+            self.out[self.core, pl.ds(self.unit_at(2 * self.near), 2)] = total.astype(BF)
+            for copy in self.near_copies():
+                copy.start()
 
     def gather_second(self):
-        for u in range(self.total):
-            at = self.unit_at(u)
-
-            @pl.when(self.z != self.z_base + u)
+        for d in (1, 3, 2):
+            owner = lax.rem(self.near + 4 - d, 4)
+
+            @pl.when(owner < self.total // 2)
             def _():
-                remote(self.out.at[self.core, at], self.out.at[self.core, at], self.gz_send.at[0],
-                       self.g_recv.at[u], self.device(self.x, self.y, self.z, 1 - self.core)).wait_recv()
+                self.received(self.out.at[self.core, pl.ds(self.unit_at(2 * owner), 2)], self.g_recv.at[19 + d])
+
         for part in range(2):
             m = self.m[part]
             ca, cb = self.coords(part)
             at = pl.ds(self.start[part] + (ca * 4 + cb) * m, m)
             for d in (2, 1, 3):
-                x, y = self.peer(self.axes(part)[1], d)
                 k = part * 3 + d - 1
                 self.send(remote(self.out.at[self.core, at], self.out.at[self.core, at], self.g_send.at[k],
-                                 self.g_recv.at[9 + k], self.device(x, y, self.z, self.core)))
+                                 self.g_recv.at[k], self.peer(self.axes(part)[1], d)))
 
     def gather_first(self):
         for part in range(2):
             m = self.m[part]
             ca, cb = self.coords(part)
             for d in (1, 3, 2):
-                k = part * 3 + d - 1
-                there = lax.rem(cb + 4 - d, 4)
-                at = pl.ds(self.start[part] + (ca * 4 + there) * m, m)
-                remote(self.out.at[self.core, at], self.out.at[self.core, at], self.g_send.at[k],
-                       self.g_recv.at[9 + k], self.device(self.x, self.y, self.z, 1 - self.core)).wait_recv()
+                at = pl.ds(self.start[part] + (ca * 4 + lax.rem(cb + 4 - d, 4)) * m, m)
+                self.received(self.out.at[self.core, at], self.g_recv.at[part * 3 + d - 1])
             at = pl.ds(self.start[part] + ca * 4 * m, 4 * m)
             for d in (2, 1, 3):
-                x, y = self.peer(self.axes(part)[0], d)
                 k = 6 + part * 3 + d - 1
                 self.send(remote(self.out.at[self.core, at], self.out.at[self.core, at], self.g_send.at[k],
-                                 self.g_recv.at[9 + k], self.device(x, y, self.z, self.core)))
+                                 self.g_recv.at[k], self.peer(self.axes(part)[0], d)))
             self.to_core(part, 0, at)
 
     def to_core(self, part, d, at):
         k = 12 + part * 4 + d
         self.send(remote(self.out.at[self.core, at], self.out.at[self.core, at], self.g_send.at[k],
-                         self.g_recv.at[9 + k], self.device(self.x, self.y, self.z, 1 - self.core)))
+                         self.g_recv.at[k], self.other_core()))
+
+    def block_of(self, part, d):
+        n = 4 * self.m[part]
+        return pl.ds(self.start[part] + lax.rem(self.coords(part)[0] + 4 - d, 4) * n, n)
 
     def gather_core(self):
         for d in (1, 3, 2):
             for part in range(2):
-                n = 4 * self.m[part]
-                ca = self.coords(part)[0]
-                k = 6 + part * 3 + d - 1
-                at = pl.ds(self.start[part] + lax.rem(ca + 4 - d, 4) * n, n)
-                remote(self.out.at[self.core, at], self.out.at[self.core, at], self.g_send.at[k],
-                       self.g_recv.at[9 + k], self.device(self.x, self.y, self.z, 1 - self.core)).wait_recv()
+                at = self.block_of(part, d)
+                self.received(self.out.at[self.core, at], self.g_recv.at[6 + part * 3 + d - 1])
                 self.to_core(part, d, at)
 
     def gather_done(self):
-        for part in range(2):
-            n = 4 * self.m[part]
-            ca = self.coords(part)[0]
-            for d in range(4):
-                k = 12 + part * 4 + d
-                at = pl.ds(self.start[part] + lax.rem(ca + 4 - d, 4) * n, n)
-                remote(self.out.at[1 - self.core, at], self.out.at[1 - self.core, at], self.g_send.at[k],
-                       self.g_recv.at[9 + k], self.device(self.x, self.y, self.z, 1 - self.core)).wait_recv()
+        for d in (0, 1, 3, 2):
+            for part in range(2):
+                at = self.block_of(part, d)
+                self.received(self.out.at[1 - self.core, at], self.g_recv.at[12 + part * 4 + d])
 
 
 def reduce_scratch(ma, mb):
     units = 16 * (ma + mb)
-    total = ma + mb
     return [
         pltpu.VMEM((2, units, 16, 128), BF),
         pltpu.VMEM((units, 16, 128), BF),
@@ -314,21 +270,19 @@
         pltpu.VMEM((4 * mb, 16, 128), BF),
         pltpu.VMEM((3, ma, 16, 128), BF),
         pltpu.VMEM((3, mb, 16, 128), BF),
-        pltpu.VMEM((total, 16, 128), BF),
-        pltpu.VMEM((NZ - 1, 16, 128), BF),
-        pltpu.SemaphoreType.DMA((13 + total,)),
-        pltpu.SemaphoreType.DMA((13,)),
-        pltpu.SemaphoreType.DMA((NZ - 1,)),
-        pltpu.SemaphoreType.DMA((20,)),
-        pltpu.SemaphoreType.DMA((9 + 20,)),
-        pltpu.SemaphoreType.DMA((NZ - 1,)),
+        pltpu.VMEM((8, 16, 128), BF),
+        pltpu.VMEM((3, 2, 16, 128), BF),
+        pltpu.VMEM((4, 2, 16, 128), BF),
+        pltpu.SemaphoreType.DMA((21,)),
+        pltpu.SemaphoreType.DMA((21,)),
+        pltpu.SemaphoreType.DMA((23,)),
+        pltpu.SemaphoreType.DMA((23,)),
     ]
 
 
-N_REDUCE = 17
-M2 = (5, 4)
-M1 = (3, 2)
-FIRST_ROWS = ((0, 0, 40), (48, 40, 32))
+N_REDUCE = 16
+MA, MB = (4, 4), (4, 2)
+A_UNITS, B_UNITS, FIRST_UNITS, LAST_UNITS = 128, 96, 72, 16
 
 
 def edge_scratch(channels):
@@ -382,8 +336,8 @@
     red1_refs, refs = refs[:N_REDUCE], refs[N_REDUCE:]
     (feat_ref, w1, w2, cot_ref, pick_ref, flip_ref, rule_ref, load_sem,
      rules_out, rules_in, rule_send, rule_recv, q_fwd, q_back, q_act, slope1, pre2) = refs
-    red2_refs = red2_refs[:11] + (second_out,) + red2_refs[11:]
-    red1_refs = red1_refs[:11] + (first_out,) + red1_refs[11:]
+    red2_refs = red2_refs[:12] + (second_out,) + red2_refs[12:]
+    red1_refs = red1_refs[:12] + (first_out,) + red1_refs[12:]
 
     lon, lat = lax.axis_index("lon"), lax.axis_index("lat")
     y = lax.div(lon, 2 * NZ)
@@ -433,8 +387,8 @@
     for d in (1, 2, 3):
         partners.append(device(lax.rem(x + d, NX), y, z, core))
         partners.append(device(x, lax.rem(y + d, NY), z, core))
-    for d in range(1, NZ):
-        partners.append(device(x, y, lax.rem(z + d, NZ), core))
+        partners.append(device(x, y, 4 * lax.div(z, 4) + lax.rem(z + d, 4), core))
+        partners.append(device(x, y, lax.rem(z + 4 * d, NZ), core))
     for partner in partners:
         pl.semaphore_signal(barrier, inc=1, device_id=partner, device_id_type=MESH)
 
@@ -528,9 +482,11 @@
         g_pad[288:416, :] = jnp.zeros((128, C2), BF)
         layer[4][320:384, :] = jnp.zeros((64, layer[4].shape[1]), BF)
 
-    red2 = Reduce(M2, 0, red2_refs, (x, y, z, core, device))
-    red1 = Reduce(M1, 9, red1_refs, (x, y, z, core, device))
-    red1.halves[:, 40:48] = jnp.zeros((2, 8, 16, 128), BF)
+    red2 = Reduce(MA, red2_refs, (x, y, z, core, device))
+    red1 = Reduce(MB, red1_refs, (x, y, z, core, device))
+    used = FIRST_UNITS + LAST_UNITS
+    red1.halves[:, used:B_UNITS] = jnp.zeros((2, B_UNITS - used, 16, 128), BF)
+    red1.a3[6:8] = jnp.zeros((2, 16, 128), BF)
 
     for slot in range(4):
         remote(rules_out, rules_in.at[slot], rule_send.at[slot], rule_recv.at[slot], west).wait_recv()
@@ -692,18 +648,17 @@
         for i in range(8):
             remote(out.at[0:16], got.at[16 * i:16 * i + 16], send.at[i], recv.at[i], west).wait_recv()
 
-    def weight_grads(halves, channels, spots, pairs):
-        units = 3 * channels // 16
-        for dh in range(3):
-            block = None
-            for cells, gradient in pairs(dh):
-                part = mm_tn(cells, gradient)
-                block = part if block is None else block + part
-            block = block.astype(BF)
-            for h in range(2):
-                values = block[:, 128 * h:128 * h + 128].reshape(units, 16, 128)
-                for first, count, to in spots[dh]:
-                    halves[h, to:to + count] = values[first:first + count]
+    def weight_grad(pairs, spots):
+        block = None
+        for cells, gradient in pairs:
+            part = mm_tn(cells, gradient)
+            block = part if block is None else block + part
+        block = block.astype(BF)
+        units = block.shape[0] // 16
+        for h in range(2):
+            values = block[:, 128 * h:128 * h + 128].reshape(units, 16, 128)
+            for first, count, red, to in spots:
+                red.halves[h, to:to + count] = values[first:first + count]
 
     edge_waits()
     pad_tile(layer1, feat_ref[...], mm(q_fwd[...], edges[1][...]), C1)
@@ -732,22 +687,21 @@
     grad2 = (cot * gelu_slope(second_pre, cdf2)).astype(BF)
     layer2[2][32:288, :] = grad2
     pre2[...] = second_pre * cdf2
-    weight_grads(red2.halves, C2, [[(0, 48, 48 * dh)] for dh in range(3)],
-                 lambda dh: [(layer2[1][16 * dh:16 * dh + 256, :], grad2)])
-    red2.core_send()
+    for dh in range(3):
+        spots = [(0, 48, red2, 48 * dh)] if dh < 2 else [(0, 32, red2, 96), (32, 16, red1, FIRST_UNITS)]
+        weight_grad([(layer2[1][16 * dh:16 * dh + 256, :], grad2)], spots)
+        red2.core_send(48 * dh, spots[0][1])
     centre2 = input_side(layer2, w2, C2)
     sent += grad_sends(layer2)
 
     own = (centre2.astype(F32) * slope1[...]).astype(BF)
     leaving = (layer2[5][...].astype(F32) * gelu_slope(halo_pre, halo_cdf)).astype(BF)
-    weight_grads(red1.halves, C1, [[(0, 24, 0)], [(0, 16, 24), (16, 8, 48)], [(0, 24, 56)]],
-                 lambda dh: [(layer1[1][16 * dh:16 * dh + 256, :], own),
-                             (patches[:, 384 * dh:384 * dh + 384], leaving)])
-    red1.core_send()
+    for dh in range(3):
+        weight_grad([(layer1[1][16 * dh:16 * dh + 256, :], own),
+                     (patches[:, 384 * dh:384 * dh + 384], leaving)], [(0, 24, red1, 24 * dh)])
+    red1.core_send(0, B_UNITS)
     red2.core_add()
-    red2.first_send()
     red1.core_add()
-    red1.first_send()
 
     r, c = iota((64, 256), 0), iota((64, 256), 1)
     gather_cells = hot(r == 8 * (c >> 5) + ((c & 15) >> 1), 0.25).astype(BF)
@@ -757,9 +711,7 @@
     pooled_ref[...] = (mm(gather_cells, high) + mm(gather_cells, low)).astype(BF)
 
     red2.first_add()
-    red2.second_send()
     red1.first_add()
-    red1.second_send()
 
     grad_waits(layer2)
     first_grad = centre2.astype(F32) + mm(place_grads, layer2[6][...])
@@ -768,15 +720,15 @@
     sent += grad_sends(layer1)
 
     red2.second_add()
-    red2.z_send()
     red1.second_add()
-    red1.z_send()
+    red2.near_add()
+    red1.near_add()
 
     grad_waits(layer1)
     grad_ref[...] = (centre1.astype(F32) + mm(place_grads, layer1[6][...])).astype(BF)
 
-    red2.z_add_and_gather()
-    red1.z_add_and_gather()
+    red2.far_add()
+    red1.far_add()
     red2.gather_second()
     red1.gather_second()
     red2.gather_first()
@@ -790,8 +742,6 @@
         copy.wait_send()
     for red in (red2, red1):
         red.finish()
-        red.z_send_done()
-        red.z_gather_sent()
 
 
 def finish_kernel(pooled_ref, grad_ref, first_ref, second_ref, pooled_out, grad_out, first_out, second_out,
@@ -808,9 +758,8 @@
 
         return lax.fori_loop(0, count // 8, body, total)
 
-    total = squares(second_ref, 0, 144, jnp.zeros((16, 128), F32))
-    for at, _, count in FIRST_ROWS:
-        total = squares(first_ref, at, count, total)
+    total = squares(second_ref, 0, A_UNITS, jnp.zeros((16, 128), F32))
+    total = squares(first_ref, 0, FIRST_UNITS + LAST_UNITS, total)
     squared = jnp.sum(jnp.sum(total, axis=0, keepdims=True), axis=1, keepdims=True)
     target_norm = math.sqrt(9.0 * (C1 + C2) * C2)
     scale = jnp.broadcast_to(target_norm / jnp.sqrt(squared + 1e-06), (16, 128))
@@ -825,8 +774,9 @@
 
         lax.fori_loop(0, count // 8, body, 0)
 
-    jobs = [(second_ref, n * 48, n * 48, 48, second_rows, second_out) for n in range(3)]
-    jobs += [(first_ref, at, to, count, first_rows, first_out) for at, to, count in FIRST_ROWS]
+    jobs = [(second_ref, n * 64, n * 64, 64, second_rows, second_out) for n in range(2)]
+    jobs.append((first_ref, 0, 0, FIRST_UNITS, first_rows, first_out))
+    jobs.append((first_ref, FIRST_UNITS, A_UNITS, LAST_UNITS, second_rows, second_out))
     for n, (ref, at, to, count, rows, out) in enumerate(jobs):
         write(ref, at, to, count, rows)
         span = pl.ds(16 * to, 16 * count)
@@ -844,8 +794,8 @@
         out_shape=(
             jax.ShapeDtypeStruct((64, C2), BF),
             jax.ShapeDtypeStruct((256, C1), BF),
-            jax.ShapeDtypeStruct((2, 16 * sum(M1), 16, 128), BF),
-            jax.ShapeDtypeStruct((2, 16 * sum(M2), 16, 128), BF),
+            jax.ShapeDtypeStruct((2, B_UNITS, 16, 128), BF),
+            jax.ShapeDtypeStruct((2, A_UNITS, 16, 128), BF),
         ),
         in_specs=[hbm] * 7,
         out_specs=[vmem] * 4,
@@ -854,8 +804,8 @@
             + patch_scratch()
             + layer_scratch(C1)
             + layer_scratch(C2)
-            + reduce_scratch(*M2)
-            + reduce_scratch(*M1)
+            + reduce_scratch(*MA)
+            + reduce_scratch(*MB)
             + [
                 pltpu.VMEM((256, C1), BF),
                 pltpu.VMEM((3, 3 * C1, C2), BF),
@@ -905,7 +855,7 @@
         scratch_shapes=[
             pltpu.VMEM((9 * C1, C2), BF),
             pltpu.VMEM((9 * C2, C2), BF),
-            pltpu.SemaphoreType.DMA((7,)),
+            pltpu.SemaphoreType.DMA((6,)),
         ],
         compiler_params=pltpu.CompilerParams(vmem_limit_bytes=16 * 1024 * 1024),
         name="scale_outputs",

time: 75.3 us -> 72.8 us (0.967)
  Pallas kernels: 74.5 us -> 72 us
    pallas_call x1, Pallas kernels: 72.7 us -> 70.1 us  [on_device(): pl.pallas_call(step_kernel, out_shape=(jax.ShapeDtypeStruct((64, C2), BF)...]
where the time goes in v4:
time: 72.8 us; the launch traced here: 72.7 us
  Pallas kernels  72 us (99%)
    pallas_call x1, Pallas kernels, on_device(): pl.pallas_call(step_kernel, out_shape=(jax.ShapeDtypeStruct((64, C2), BF)...  70.1 us
    pallas_call x1, Pallas kernels, on_device(): pl.pallas_call(finish_kernel, out_shape=(jax.ShapeDtypeStruct((64, C2), B...  1.89 us

profile of v4, /device:TPU:1, one launch (start us, length us, event | category | flops | bytes accessed | tf_op | source)
XLA Modules:
  0.0 72.7 jit_solution(506667499656254275)
XLA Ops:
  0.6 70.1 %level_step.1 = (bf16[64,256]{1,0:T(8,128)(2,1)S(1)}, bf16[256,128]{1,0:T(8,128)(2,1)S(1)}, bf16[2,96,16,128]{3,2,1,0:T(8,128)(2,1)S(1)}, bf16[2,128,16,128]{3,2,1,0:T(8,128)(2,1)S(1)}) custom-call(bf16[256,128]{1,0:T(8,128)(2,1)} %bitcast.10, bf16[3,384,256]{2,1,0:T(8,128)(2,1)} %bitcast.9, bf16[3,768,256]{2,1,0:T(8,128)(2,1)} %bitcast.8, ...), custom_call_target="tpu_custom_call" | custom-call | tf_op jit(solution)/shard_map/level_step/pallas_call | solution.py:792
  70.8 1.9 %scale_outputs.1 = (bf16[64,256]{1,0:T(8,128)(2,1)}, bf16[256,128]{1,0:T(8,128)(2,1)}, bf16[1152,256]{1,0:T(8,128)(2,1)}, bf16[2304,256]{1,0:T(8,128)(2,1)}) custom-call(bf16[64,256]{1,0:T(8,128)(2,1)S(1)} %get-tuple-element.12.pooled_ref, bf16[256,128]{1,0:T(8,128)(2,1)S(1)} %get-tuple-element.13.grad_ref, ...), custom_call_target="tpu_custom_call" | custom-call | tf_op jit(solution)/shard_map/scale_outputs/pallas_call | solution.py:845

commit v5 on v4

--- a/solution.py
+++ b/solution.py
@@ -100,10 +100,12 @@
     def received(self, ref, sem):
         remote(ref, ref, self.s_send.at[0], sem, self.other_core()).wait_recv()
 
-    def finish(self):
+    def flush(self):
         for copy in self.pending:
             copy.wait_send()
-
+        self.pending = []
+
+    def near_flush(self):
         @pl.when(self.near < self.total // 2)
         def _():
             for copy in self.near_copies():
@@ -326,8 +328,8 @@
 
 def step_kernel(*refs):
     (feat_hbm, w1_hbm, w2_hbm, cot_hbm, pick_hbm, flip_hbm, rule_hbm,
-     pooled_ref, grad_ref, first_out, second_out) = refs[:11]
-    refs = refs[11:]
+     pooled_ref, grad_ref, first_out, second_out, square_ref) = refs[:12]
+    refs = refs[12:]
     edges, refs = refs[:N_EDGE], refs[N_EDGE:]
     patch_refs, refs = refs[:N_PATCH], refs[N_PATCH:]
     layer1, refs = refs[:N_LAYER], refs[N_LAYER:]
@@ -335,7 +337,8 @@
     red2_refs, refs = refs[:N_REDUCE], refs[N_REDUCE:]
     red1_refs, refs = refs[:N_REDUCE], refs[N_REDUCE:]
     (feat_ref, w1, w2, cot_ref, pick_ref, flip_ref, rule_ref, load_sem,
-     rules_out, rules_in, rule_send, rule_recv, q_fwd, q_back, q_act, slope1, pre2) = refs
+     rules_out, rules_in, rule_send, rule_recv, q_fwd, q_back, q_act, slope1, pre2,
+     windows) = refs
     red2_refs = red2_refs[:12] + (second_out,) + red2_refs[12:]
     red1_refs = red1_refs[:12] + (first_out,) + red1_refs[12:]
 
@@ -648,11 +651,7 @@
         for i in range(8):
             remote(out.at[0:16], got.at[16 * i:16 * i + 16], send.at[i], recv.at[i], west).wait_recv()
 
-    def weight_grad(pairs, spots):
-        block = None
-        for cells, gradient in pairs:
-            part = mm_tn(cells, gradient)
-            block = part if block is None else block + part
+    def weight_grad(block, spots):
         block = block.astype(BF)
         units = block.shape[0] // 16
         for h in range(2):
@@ -668,6 +667,8 @@
     cdf1 = normal_cdf(pre1)
     act1 = (pre1 * cdf1).astype(BF)
     slope1[...] = gelu_slope(pre1, cdf1)
+    for dh in range(3):
+        windows[dh] = layer1[1][16 * dh:16 * dh + 256, :].T
     r, c = iota((256, 64), 0), iota((256, 64), 1)
     spread = hot(c == 8 * (r >> 5) + ((r & 15) >> 1), 0.25).astype(BF)
     loads[5].wait()
@@ -686,10 +687,9 @@
     cdf2 = normal_cdf(second_pre)
     grad2 = (cot * gelu_slope(second_pre, cdf2)).astype(BF)
     layer2[2][32:288, :] = grad2
-    pre2[...] = second_pre * cdf2
     for dh in range(3):
         spots = [(0, 48, red2, 48 * dh)] if dh < 2 else [(0, 32, red2, 96), (32, 16, red1, FIRST_UNITS)]
-        weight_grad([(layer2[1][16 * dh:16 * dh + 256, :], grad2)], spots)
+        weight_grad(mm_tn(layer2[1][16 * dh:16 * dh + 256, :], grad2), spots)
         red2.core_send(48 * dh, spots[0][1])
     centre2 = input_side(layer2, w2, C2)
     sent += grad_sends(layer2)
@@ -697,11 +697,12 @@
     own = (centre2.astype(F32) * slope1[...]).astype(BF)
     leaving = (layer2[5][...].astype(F32) * gelu_slope(halo_pre, halo_cdf)).astype(BF)
     for dh in range(3):
-        weight_grad([(layer1[1][16 * dh:16 * dh + 256, :], own),
-                     (patches[:, 384 * dh:384 * dh + 384], leaving)], [(0, 24, red1, 24 * dh)])
+        block = mm(windows[dh], own) + mm_tn(patches[:, 384 * dh:384 * dh + 384], leaving)
+        weight_grad(block, [(0, 24, red1, 24 * dh)])
     red1.core_send(0, B_UNITS)
     red2.core_add()
     red1.core_add()
+    pre2[...] = second_pre * cdf2
 
     r, c = iota((64, 256), 0), iota((64, 256), 1)
     gather_cells = hot(r == 8 * (c >> 5) + ((c & 15) >> 1), 0.25).astype(BF)
@@ -727,39 +728,43 @@
     grad_waits(layer1)
     grad_ref[...] = (centre1.astype(F32) + mm(place_grads, layer1[6][...])).astype(BF)
 
+    for copy in sent + rule_copies:
+        copy.wait_send()
+    red2.flush()
+    red1.flush()
     red2.far_add()
     red1.far_add()
     red2.gather_second()
     red1.gather_second()
+    red2.near_flush()
+    red1.near_flush()
     red2.gather_first()
     red1.gather_first()
     red2.gather_core()
     red1.gather_core()
     red2.gather_done()
+    red2.flush()
+    square_ref[...] = sum_squares(second_out, 0, A_UNITS, jnp.zeros((16, 128), F32))
     red1.gather_done()
-
-    for copy in sent + rule_copies:
-        copy.wait_send()
-    for red in (red2, red1):
-        red.finish()
-
-
-def finish_kernel(pooled_ref, grad_ref, first_ref, second_ref, pooled_out, grad_out, first_out, second_out,
+    red1.flush()
+
+
+def sum_squares(ref, at, count, total):
+    def body(i, total):
+        values = ref[:, pl.ds(at + i * 8, 8)].astype(F32)
+        return total + jnp.sum(values * values, axis=(0, 1))
+
+    return lax.fori_loop(0, count // 8, body, total)
+
+
+def finish_kernel(pooled_ref, grad_ref, first_ref, second_ref, square_ref, pooled_out, grad_out, first_out, second_out,
                   first_rows, second_rows, sems):
     copies = [pltpu.make_async_copy(pooled_ref, pooled_out, sems.at[0]),
               pltpu.make_async_copy(grad_ref, grad_out, sems.at[1])]
     for copy in copies:
         copy.start()
 
-    def squares(ref, at, count, total):
-        def body(i, total):
-            values = ref[:, pl.ds(at + i * 8, 8)].astype(F32)
-            return total + jnp.sum(values * values, axis=(0, 1))
-
-        return lax.fori_loop(0, count // 8, body, total)
-
-    total = squares(second_ref, 0, A_UNITS, jnp.zeros((16, 128), F32))
-    total = squares(first_ref, 0, FIRST_UNITS + LAST_UNITS, total)
+    total = sum_squares(first_ref, 0, FIRST_UNITS + LAST_UNITS, square_ref[...])
     squared = jnp.sum(jnp.sum(total, axis=0, keepdims=True), axis=1, keepdims=True)
     target_norm = math.sqrt(9.0 * (C1 + C2) * C2)
     scale = jnp.broadcast_to(target_norm / jnp.sqrt(squared + 1e-06), (16, 128))
@@ -789,16 +794,17 @@
 def on_device(features, conv_first, conv_second, cotangent, edge_pick, edge_flip, corner_rule):
     vmem = pl.BlockSpec(memory_space=pltpu.VMEM)
     hbm = pl.BlockSpec(memory_space=pltpu.HBM)
-    pooled, input_grad, first, second = pl.pallas_call(
+    pooled, input_grad, first, second, square = pl.pallas_call(
         step_kernel,
         out_shape=(
             jax.ShapeDtypeStruct((64, C2), BF),
             jax.ShapeDtypeStruct((256, C1), BF),
             jax.ShapeDtypeStruct((2, B_UNITS, 16, 128), BF),
             jax.ShapeDtypeStruct((2, A_UNITS, 16, 128), BF),
+            jax.ShapeDtypeStruct((16, 128), F32),
         ),
         in_specs=[hbm] * 7,
-        out_specs=[vmem] * 4,
+        out_specs=[vmem] * 5,
         scratch_shapes=(
             edge_scratch(C1)
             + patch_scratch()
@@ -824,6 +830,7 @@
                 pltpu.VMEM((320, 128), BF),
                 pltpu.VMEM((256, C2), F32),
                 pltpu.VMEM((256, C2), F32),
+                pltpu.VMEM((3, 3 * C1, 256), BF),
             ]
         ),
         compiler_params=pltpu.CompilerParams(
@@ -850,7 +857,7 @@
             jax.ShapeDtypeStruct((9 * C1, C2), BF),
             jax.ShapeDtypeStruct((9 * C2, C2), BF),
         ),
-        in_specs=[vmem] * 4,
+        in_specs=[vmem] * 5,
         out_specs=[hbm] * 4,
         scratch_shapes=[
             pltpu.VMEM((9 * C1, C2), BF),
@@ -859,7 +866,7 @@
         ],
         compiler_params=pltpu.CompilerParams(vmem_limit_bytes=16 * 1024 * 1024),
         name="scale_outputs",
-    )(pooled, input_grad, first, second)
+    )(pooled, input_grad, first, second, square)
     return (
         pooled.reshape(1, 1, 8, 8, C2),
         input_grad.reshape(1, 1, 16, 16, C1),

time: 72.8 us -> 72.4 us (level)
  no operation moved by 1% of the time
where the time goes in v5:
time: 72.4 us; the launch traced here: 72.2 us
  Pallas kernels  71.6 us (99%)
    pallas_call x1, Pallas kernels, on_device(): pl.pallas_call(step_kernel, out_shape=(jax.ShapeDtypeStruct((64, C2), BF)...  70 us
    pallas_call x1, Pallas kernels, on_device(): pl.pallas_call(finish_kernel, out_shape=(jax.ShapeDtypeStruct((64, C2), B...  1.65 us

profile of v5, /device:TPU:1, one launch (start us, length us, event | category | flops | bytes accessed | tf_op | source)
XLA Modules:
  0.0 72.2 jit_solution(1613937659279020170)
XLA Ops:
  0.6 70.0 %level_step.1 = (bf16[64,256]{1,0:T(8,128)(2,1)S(1)}, bf16[256,128]{1,0:T(8,128)(2,1)S(1)}, bf16[2,96,16,128]{3,2,1,0:T(8,128)(2,1)S(1)}, bf16[2,128,16,128]{3,2,1,0:T(8,128)(2,1)S(1)}, f32[16,128]{1,0:T(8,128)S(1)}) custom-call(bf16[256,128]{1,0:T(8,128)(2,1)} %bitcast.10, bf16[3,384,256]{2,1,0:T(8,128)(2,1)} %bitcast.9, bf16[3,768,256]{2,1,0:T(8,128)(2,1)} %bitcast.8, ...), custom_call_target="tpu_custom_call" | custom-call | tf_op jit(solution)/shard_map/level_step/pallas_call | solution.py:797
  70.6 1.6 %scale_outputs.1 = (bf16[64,256]{1,0:T(8,128)(2,1)}, bf16[256,128]{1,0:T(8,128)(2,1)}, bf16[1152,256]{1,0:T(8,128)(2,1)}, bf16[2304,256]{1,0:T(8,128)(2,1)}) custom-call(bf16[64,256]{1,0:T(8,128)(2,1)S(1)} %get-tuple-element.13.pooled_ref, bf16[256,128]{1,0:T(8,128)(2,1)S(1)} %get-tuple-element.14.grad_ref, ...), custom_call_target="tpu_custom_call" | custom-call | tf_op jit(solution)/shard_map/scale_outputs/pallas_call | solution.py:852

commit v6 on v5

--- a/solution.py
+++ b/solution.py
@@ -125,12 +125,13 @@
                 at, count = self.pieces[self.waited]
                 self.received(self.r0.at[at:at + count], self.s_recv.at[self.waited])
                 self.waited += 1
+            k = 3 + part
             for d in (2, 1, 3, 0):
                 at = pl.ds(self.start[part] + lax.rem(mine + d, 4) * n, n)
                 self.a1[at] = (self.halves[self.core, at].astype(F32) + self.r0[at].astype(F32)).astype(BF)
                 if d:
-                    k = 3 + part * 3 + d - 1
-                    self.send(remote(self.a1.at[at], self.r1[part].at[d - 1], self.s_send.at[k], self.s_recv.at[k],
+                    self.send(remote(self.a1.at[at], self.r1[part].at[d - 1],
+                                     self.s_send.at[3 * k - 7 + d], self.s_recv.at[k],
                                      self.peer(self.axes(part)[0], d)))
 
     def first_add(self):
@@ -138,8 +139,8 @@
             m = self.m[part]
             r1, a2, r2 = self.r1[part], self.a2[part], self.r2[part]
             ca, cb = self.coords(part)
-            for d in (1, 3, 2):
-                self.received(r1.at[d - 1], self.s_recv.at[3 + part * 3 + d - 1])
+            self.received(r1, self.s_recv.at[3 + part])
+            k = 5 + part
             for d in (2, 1, 3, 0):
                 block = lax.rem(cb + d, 4)
                 at = pl.ds(block * m, m)
@@ -148,8 +149,8 @@
                     total = total + r1[e, at].astype(F32)
                 a2[at] = total.astype(BF)
                 if d:
-                    k = 9 + part * 3 + d - 1
-                    self.send(remote(a2.at[at], r2.at[d - 1], self.s_send.at[k], self.s_recv.at[k],
+                    self.send(remote(a2.at[at], r2.at[d - 1],
+                                     self.s_send.at[3 * k - 7 + d], self.s_recv.at[k],
                                      self.peer(self.axes(part)[1], d)))
 
     def second_add(self):
@@ -157,8 +158,7 @@
             m = self.m[part]
             a2, r2 = self.a2[part], self.r2[part]
             cb = self.coords(part)[1]
-            for d in (1, 3, 2):
-                self.received(r2.at[d - 1], self.s_recv.at[9 + part * 3 + d - 1])
+            self.received(r2, self.s_recv.at[5 + part])
             total = a2[pl.ds(cb * m, m)].astype(F32)
             for e in range(3):
                 total = total + r2[e].astype(F32)
@@ -166,17 +166,16 @@
         for d in (2, 1, 3):
             owner = lax.rem(self.near + d, 4)
             self.send(remote(self.a3.at[pl.ds(2 * owner, 2)], self.n3.at[d - 1], self.s_send.at[14 + d],
-                             self.s_recv.at[14 + d], self.device(self.x, self.y, 4 * self.far + owner, self.core)))
+                             self.s_recv.at[7], self.device(self.x, self.y, 4 * self.far + owner, self.core)))
 
     def near_add(self):
-        for d in (1, 3, 2):
-            self.received(self.n3.at[d - 1], self.s_recv.at[14 + d])
+        self.received(self.n3, self.s_recv.at[7])
         total = self.a3[pl.ds(2 * self.near, 2)].astype(F32)
         for e in range(3):
             total = total + self.n3[e].astype(F32)
         self.f3[self.far] = total.astype(BF)
         for d in (2, 1, 3):
-            self.send(remote(self.f3.at[self.far], self.f3.at[self.far], self.s_send.at[17 + d], self.s_recv.at[17 + d],
+            self.send(remote(self.f3.at[self.far], self.f3.at[self.far], self.s_send.at[17 + d], self.s_recv.at[8],
                              self.device(self.x, self.y, 4 * lax.rem(self.far + d, 4) + self.near, self.core)))
 
     def unit_at(self, u):
@@ -194,8 +193,7 @@
         ]
 
     def far_add(self):
-        for d in (1, 3, 2):
-            self.received(self.f3.at[lax.rem(self.far + 4 - d, 4)], self.s_recv.at[17 + d])
+        self.received(self.f3.at[0:3], self.s_recv.at[8])
 
         @pl.when(self.near < self.total // 2)
         def _():
@@ -219,17 +217,14 @@
             ca, cb = self.coords(part)
             at = pl.ds(self.start[part] + (ca * 4 + cb) * m, m)
             for d in (2, 1, 3):
-                k = part * 3 + d - 1
-                self.send(remote(self.out.at[self.core, at], self.out.at[self.core, at], self.g_send.at[k],
-                                 self.g_recv.at[k], self.peer(self.axes(part)[1], d)))
+                self.send(remote(self.out.at[self.core, at], self.out.at[self.core, at], self.g_send.at[part * 3 + d - 1],
+                                 self.g_recv.at[part], self.peer(self.axes(part)[1], d)))
 
     def gather_first(self):
         for part in range(2):
             m = self.m[part]
-            ca, cb = self.coords(part)
-            for d in (1, 3, 2):
-                at = pl.ds(self.start[part] + (ca * 4 + lax.rem(cb + 4 - d, 4)) * m, m)
-                self.received(self.out.at[self.core, at], self.g_recv.at[part * 3 + d - 1])
+            ca = self.coords(part)[0]
+            self.received(self.r2[part], self.g_recv.at[part])
             at = pl.ds(self.start[part] + ca * 4 * m, 4 * m)
             for d in (2, 1, 3):
                 k = 6 + part * 3 + d - 1
@@ -374,6 +369,17 @@
         (east_of(vert[1]), 2 * seen[1]),
     ]
 
+    barrier = pltpu.get_barrier_semaphore()
+    partners = [device(x, y, lax.rem(z + 4 * d, NZ), core) for d in (2, 1, 3)]
+    partners += [d[0] for d in diagonal] + [west, east, vert[0], vert[1]]
+    for d in (2, 1, 3):
+        partners.append(device(x, y, 4 * lax.div(z, 4) + lax.rem(z + d, 4), core))
+        partners.append(device(lax.rem(x + d, NX), y, z, core))
+        partners.append(device(x, lax.rem(y + d, NY), z, core))
+    partners.append(device(x, y, z, 1 - core))
+    for partner in partners:
+        pl.semaphore_signal(barrier, inc=1, device_id=partner, device_id_type=MESH)
+
     loads = [
         pltpu.make_async_copy(src, dst, load_sem.at[n])
         for n, (src, dst) in enumerate((
@@ -384,17 +390,6 @@
     for load in loads:
         load.start()
 
-    barrier = pltpu.get_barrier_semaphore()
-    partners = [vert[0], vert[1], west, east] + [d[0] for d in diagonal]
-    partners.append(device(x, y, z, 1 - core))
-    for d in (1, 2, 3):
-        partners.append(device(lax.rem(x + d, NX), y, z, core))
-        partners.append(device(x, lax.rem(y + d, NY), z, core))
-        partners.append(device(x, y, 4 * lax.div(z, 4) + lax.rem(z + d, 4), core))
-        partners.append(device(x, y, lax.rem(z + 4 * d, NZ), core))
-    for partner in partners:
-        pl.semaphore_signal(barrier, inc=1, device_id=partner, device_id_type=MESH)
-
     for load in loads[:3]:
         load.wait()
     picks = [pick_ref[0, 0, s] for s in range(2)]
@@ -425,14 +420,14 @@
     def edge_sends():
         out, got, send, recv = edges
         copies = []
+        for i, (target, slot) in enumerate(diagonal):
+            copies.append(remote(out.at[64:80], got.at[pl.ds(pl.multiple_of(160 + 16 * slot, 16), 16)],
+                                 send.at[4 + i], recv.at[4 + slot], target))
         for side in range(2):
             copies.append(remote(out.at[0:64], got.at[pl.ds(pl.multiple_of(64 * seen[side], 64), 64)],
                                  send.at[side], recv.at[seen[side]], vert[side]))
         copies.append(remote(out.at[32:48], got.at[144:160], send.at[2], recv.at[3], west))
         copies.append(remote(out.at[48:64], got.at[128:144], send.at[3], recv.at[2], east))
-        for i, (target, slot) in enumerate(diagonal):
-            copies.append(remote(out.at[64:80], got.at[pl.ds(pl.multiple_of(160 + 16 * slot, 16), 16)],
-                                 send.at[4 + i], recv.at[4 + slot], target))
         for copy in copies:
             copy.start()
         return copies
@@ -443,12 +438,12 @@
         for i, (at, size) in enumerate(spots):
             remote(out.at[0:size], got.at[at:at + size], send.at[i], recv.at[i], west).wait_recv()
 
+    sent = edge_sends()
     rule_copies = []
     for i, (target, slot) in enumerate(((vert[0], seen[0]), (vert[1], seen[1]), (west, 3), (east, 2))):
         rule_copies.append(remote(rules_out, rules_in.at[slot], rule_send.at[i], rule_recv.at[slot], target))
     for copy in rule_copies:
         copy.start()
-    sent = edge_sends()
 
     r, c = iota((288, 256), 0), iota((288, 256), 1)
     j, i = r & 15, r >> 4
@@ -553,24 +548,26 @@
     def patch_sends():
         cells, strips, corners, got_cells, got_strips, got_corners, send, recv = patch_refs
         padded = layer1[1]
-        for dh in range(3):
-            cells[:, 384 * dh:384 * dh + 384] = mm(take_cells, padded[16 * dh:16 * dh + 256, :]).astype(BF)
-        strips[...] = mm(take_strips, padded[...]).astype(BF).reshape(2, 32, 3 * C1)
         values = mm(take_corners[0], padded[:, 0:C1])
         for dw in (1, 2):
             values = values + mm(take_corners[dw], padded[:, dw * C1:(dw + 1) * C1])
         corners[...] = values.astype(BF).reshape(4, 16, C1)
         copies = []
+        for i, (target_at, slot) in enumerate(diagonal):
+            copies.append(remote(corners.at[i], got_corners.at[slot], send.at[4 + i], recv.at[4 + slot], target_at))
+            copies[-1].start()
+        strips[...] = mm(take_strips, padded[...]).astype(BF).reshape(2, 32, 3 * C1)
+        copies.append(remote(strips.at[0], got_strips.at[0], send.at[2], recv.at[2], east))
+        copies.append(remote(strips.at[1], got_strips.at[1], send.at[3], recv.at[3], west))
+        for copy in copies[-2:]:
+            copy.start()
+        for dh in range(3):
+            cells[:, 384 * dh:384 * dh + 384] = mm(take_cells, padded[16 * dh:16 * dh + 256, :]).astype(BF)
         for side in range(2):
             copies.append(remote(cells.at[16 * side:16 * side + 16],
                                  got_cells.at[pl.ds(pl.multiple_of(16 * seen[side], 16), 16)],
                                  send.at[side], recv.at[seen[side]], vert[side]))
-        copies.append(remote(strips.at[0], got_strips.at[0], send.at[2], recv.at[2], east))
-        copies.append(remote(strips.at[1], got_strips.at[1], send.at[3], recv.at[3], west))
-        for i, (target_at, slot) in enumerate(diagonal):
-            copies.append(remote(corners.at[i], got_corners.at[slot], send.at[4 + i], recv.at[4 + slot], target_at))
-        for copy in copies:
-            copy.start()
+            copies[-1].start()
         return copies
 
     def patch_waits():

time: 72.4 us -> 71.8 us (level)
  no operation moved by 1% of the time
where the time goes in v6:
time: 71.8 us; the launch traced here: 71.7 us
  Pallas kernels  71.1 us (99%)
    pallas_call x1, Pallas kernels, on_device(): pl.pallas_call(step_kernel, out_shape=(jax.ShapeDtypeStruct((64, C2), BF)...  69.4 us
    pallas_call x1, Pallas kernels, on_device(): pl.pallas_call(finish_kernel, out_shape=(jax.ShapeDtypeStruct((64, C2), B...  1.65 us

profile of v6, /device:TPU:1, one launch (start us, length us, event | category | flops | bytes accessed | tf_op | source)
XLA Modules:
  0.0 71.7 jit_solution(11777737158219204178)
XLA Ops:
  0.6 69.4 %level_step.1 = (bf16[64,256]{1,0:T(8,128)(2,1)S(1)}, bf16[256,128]{1,0:T(8,128)(2,1)S(1)}, bf16[2,96,16,128]{3,2,1,0:T(8,128)(2,1)S(1)}, bf16[2,128,16,128]{3,2,1,0:T(8,128)(2,1)S(1)}, f32[16,128]{1,0:T(8,128)S(1)}) custom-call(bf16[256,128]{1,0:T(8,128)(2,1)} %bitcast.10, bf16[3,384,256]{2,1,0:T(8,128)(2,1)} %bitcast.9, bf16[3,768,256]{2,1,0:T(8,128)(2,1)} %bitcast.8, ...), custom_call_target="tpu_custom_call" | custom-call | tf_op jit(solution)/shard_map/level_step/pallas_call | solution.py:794
  70.0 1.6 %scale_outputs.1 = (bf16[64,256]{1,0:T(8,128)(2,1)}, bf16[256,128]{1,0:T(8,128)(2,1)}, bf16[1152,256]{1,0:T(8,128)(2,1)}, bf16[2304,256]{1,0:T(8,128)(2,1)}) custom-call(bf16[64,256]{1,0:T(8,128)(2,1)S(1)} %get-tuple-element.13.pooled_ref, bf16[256,128]{1,0:T(8,128)(2,1)S(1)} %get-tuple-element.14.grad_ref, ...), custom_call_target="tpu_custom_call" | custom-call | tf_op jit(solution)/shard_map/scale_outputs/pallas_call | solution.py:849

commit v7 on v6

--- a/solution.py
+++ b/solution.py
@@ -104,6 +104,12 @@
         for copy in self.pending:
             copy.wait_send()
         self.pending = []
+
+    def far_flush(self):
+        @pl.when(self.near < self.total // 2)
+        def _():
+            for copy in self.far_copies():
+                copy.wait_send()
 
     def near_flush(self):
         @pl.when(self.near < self.total // 2)
@@ -174,9 +180,18 @@
         for e in range(3):
             total = total + self.n3[e].astype(F32)
         self.f3[self.far] = total.astype(BF)
-        for d in (2, 1, 3):
-            self.send(remote(self.f3.at[self.far], self.f3.at[self.far], self.s_send.at[17 + d], self.s_recv.at[8],
-                             self.device(self.x, self.y, 4 * lax.rem(self.far + d, 4) + self.near, self.core)))
+
+        @pl.when(self.near < self.total // 2)
+        def _():
+            for copy in self.far_copies():
+                copy.start()
+
+    def far_copies(self):
+        return [
+            remote(self.f3.at[self.far], self.f3.at[self.far], self.s_send.at[17 + d], self.s_recv.at[8],
+                   self.device(self.x, self.y, 4 * lax.rem(self.far + d, 4) + self.near, self.core))
+            for d in (2, 1, 3)
+        ]
 
     def unit_at(self, u):
         ma, mb = self.m
@@ -193,10 +208,9 @@
         ]
 
     def far_add(self):
-        self.received(self.f3.at[0:3], self.s_recv.at[8])
-
         @pl.when(self.near < self.total // 2)
         def _():
+            self.received(self.f3.at[0:3], self.s_recv.at[8])
             total = self.f3[0].astype(F32)
             for e in range(1, 4):
                 total = total + self.f3[e].astype(F32)
@@ -253,6 +267,7 @@
             for part in range(2):
                 at = self.block_of(part, d)
                 self.received(self.out.at[1 - self.core, at], self.g_recv.at[12 + part * 4 + d])
+                yield part, at.start
 
 
 def reduce_scratch(ma, mb):
@@ -733,25 +748,31 @@
     red1.far_add()
     red2.gather_second()
     red1.gather_second()
-    red2.near_flush()
-    red1.near_flush()
+    for red in (red2, red1):
+        red.far_flush()
+        red.near_flush()
     red2.gather_first()
     red1.gather_first()
     red2.gather_core()
     red1.gather_core()
-    red2.gather_done()
+    list(red2.gather_done())
     red2.flush()
-    square_ref[...] = sum_squares(second_out, 0, A_UNITS, jnp.zeros((16, 128), F32))
-    red1.gather_done()
+    squares = jnp.zeros((16, 128), F32)
+    for h in range(2):
+        squares = sum_squares(second_out, h, 0, A_UNITS // 8, squares)
+    squares = sum_squares(first_out, core, 0, B_UNITS // 8, squares)
+    for part, at in red1.gather_done():
+        squares = sum_squares(first_out, 1 - core, at, red1.m[part] // 2, squares)
+    square_ref[...] = squares
     red1.flush()
 
 
-def sum_squares(ref, at, count, total):
+def sum_squares(ref, half, at, steps, total):
     def body(i, total):
-        values = ref[:, pl.ds(at + i * 8, 8)].astype(F32)
-        return total + jnp.sum(values * values, axis=(0, 1))
-
-    return lax.fori_loop(0, count // 8, body, total)
+        values = ref[half, pl.ds(at + i * 8, 8)].astype(F32)
+        return total + jnp.sum(values * values, axis=0)
+
+    return lax.fori_loop(0, steps, body, total)
 
 
 def finish_kernel(pooled_ref, grad_ref, first_ref, second_ref, square_ref, pooled_out, grad_out, first_out, second_out,
@@ -761,8 +782,7 @@
     for copy in copies:
         copy.start()
 
-    total = sum_squares(first_ref, 0, FIRST_UNITS + LAST_UNITS, square_ref[...])
-    squared = jnp.sum(jnp.sum(total, axis=0, keepdims=True), axis=1, keepdims=True)
+    squared = jnp.sum(jnp.sum(square_ref[...], axis=0, keepdims=True), axis=1, keepdims=True)
     target_norm = math.sqrt(9.0 * (C1 + C2) * C2)
     scale = jnp.broadcast_to(target_norm / jnp.sqrt(squared + 1e-06), (16, 128))
 

time: 71.8 us -> 71.7 us (level)
  no operation moved by 1% of the time
where the time goes in v7:
time: 71.7 us; the launch traced here: 71.5 us
  Pallas kernels  70.9 us (99%)
    pallas_call x1, Pallas kernels, on_device(): pl.pallas_call(step_kernel, out_shape=(jax.ShapeDtypeStruct((64, C2), BF)...  69.4 us
    pallas_call x1, Pallas kernels, on_device(): pl.pallas_call(finish_kernel, out_shape=(jax.ShapeDtypeStruct((64, C2), B...  1.48 us

profile of v7, /device:TPU:1, one launch (start us, length us, event | category | flops | bytes accessed | tf_op | source)
XLA Modules:
  0.0 71.5 jit_solution(14008172213880696762)
XLA Ops:
  0.6 69.4 %level_step.1 = (bf16[64,256]{1,0:T(8,128)(2,1)S(1)}, bf16[256,128]{1,0:T(8,128)(2,1)S(1)}, bf16[2,96,16,128]{3,2,1,0:T(8,128)(2,1)S(1)}, bf16[2,128,16,128]{3,2,1,0:T(8,128)(2,1)S(1)}, f32[16,128]{1,0:T(8,128)S(1)}) custom-call(bf16[256,128]{1,0:T(8,128)(2,1)} %bitcast.10, bf16[3,384,256]{2,1,0:T(8,128)(2,1)} %bitcast.9, bf16[3,768,256]{2,1,0:T(8,128)(2,1)} %bitcast.8, ...), custom_call_target="tpu_custom_call" | custom-call | tf_op jit(solution)/shard_map/level_step/pallas_call | solution.py:814
  70.1 1.5 %scale_outputs.1 = (bf16[64,256]{1,0:T(8,128)(2,1)}, bf16[256,128]{1,0:T(8,128)(2,1)}, bf16[1152,256]{1,0:T(8,128)(2,1)}, bf16[2304,256]{1,0:T(8,128)(2,1)}) custom-call(bf16[64,256]{1,0:T(8,128)(2,1)S(1)} %get-tuple-element.13.pooled_ref, bf16[256,128]{1,0:T(8,128)(2,1)S(1)} %get-tuple-element.14.grad_ref, ...), custom_call_target="tpu_custom_call" | custom-call | tf_op jit(solution)/shard_map/scale_outputs/pallas_call | solution.py:869

commit v8 on v7

--- a/solution.py
+++ b/solution.py
@@ -124,58 +124,55 @@
                          self.s_send.at[k], self.s_recv.at[k], self.other_core()))
 
     def core_add(self):
-        for part in range(2):
-            n = 4 * self.m[part]
-            mine = self.coords(part)[0]
-            while self.waited < len(self.pieces) and self.pieces[self.waited][0] < self.start[part] + 4 * n:
-                at, count = self.pieces[self.waited]
-                self.received(self.r0.at[at:at + count], self.s_recv.at[self.waited])
-                self.waited += 1
-            k = 3 + part
-            for d in (2, 1, 3, 0):
-                at = pl.ds(self.start[part] + lax.rem(mine + d, 4) * n, n)
-                self.a1[at] = (self.halves[self.core, at].astype(F32) + self.r0[at].astype(F32)).astype(BF)
-                if d:
-                    self.send(remote(self.a1.at[at], self.r1[part].at[d - 1],
-                                     self.s_send.at[3 * k - 7 + d], self.s_recv.at[k],
+        for k, (at, count) in enumerate(self.pieces):
+            self.received(self.r0.at[at:at + count], self.s_recv.at[k])
+        for e in (2, 1, 3, 0):
+            for part in range(2):
+                m = self.m[part]
+                ca, cb = self.coords(part)
+                block = lax.rem(cb + e, 4)
+                for d in (2, 1, 3):
+                    at = pl.ds(self.start[part] + (lax.rem(ca + d, 4) * 4 + block) * m, m)
+                    self.a1[at] = (self.halves[self.core, at].astype(F32) + self.r0[at].astype(F32)).astype(BF)
+                    self.send(remote(self.a1.at[at], self.r1[part].at[d - 1, pl.ds(block * m, m)],
+                                     self.s_send.at[3 + 12 * part + 3 * e + d - 1], self.s_recv.at[3 + 4 * part + e],
                                      self.peer(self.axes(part)[0], d)))
 
     def first_add(self):
-        for part in range(2):
-            m = self.m[part]
-            r1, a2, r2 = self.r1[part], self.a2[part], self.r2[part]
-            ca, cb = self.coords(part)
-            self.received(r1, self.s_recv.at[3 + part])
-            k = 5 + part
-            for d in (2, 1, 3, 0):
-                block = lax.rem(cb + d, 4)
+        for e in (2, 1, 3, 0):
+            for part in range(2):
+                m = self.m[part]
+                r1, a2, r2 = self.r1[part], self.a2[part], self.r2[part]
+                ca, cb = self.coords(part)
+                self.received(r2, self.s_recv.at[3 + 4 * part + e])
+                block = lax.rem(cb + e, 4)
                 at = pl.ds(block * m, m)
-                total = self.a1[pl.ds(self.start[part] + (ca * 4 + block) * m, m)].astype(F32)
-                for e in range(3):
-                    total = total + r1[e, at].astype(F32)
+                own = pl.ds(self.start[part] + (ca * 4 + block) * m, m)
+                total = self.halves[self.core, own].astype(F32) + self.r0[own].astype(F32)
+                for d in range(3):
+                    total = total + r1[d, at].astype(F32)
                 a2[at] = total.astype(BF)
-                if d:
-                    self.send(remote(a2.at[at], r2.at[d - 1],
-                                     self.s_send.at[3 * k - 7 + d], self.s_recv.at[k],
-                                     self.peer(self.axes(part)[1], d)))
+                if e:
+                    self.send(remote(a2.at[at], r2.at[e - 1], self.s_send.at[27 + 3 * part + e - 1],
+                                     self.s_recv.at[11 + part], self.peer(self.axes(part)[1], e)))
 
     def second_add(self):
         for part in range(2):
             m = self.m[part]
             a2, r2 = self.a2[part], self.r2[part]
             cb = self.coords(part)[1]
-            self.received(r2, self.s_recv.at[5 + part])
+            self.received(r2, self.s_recv.at[11 + part])
             total = a2[pl.ds(cb * m, m)].astype(F32)
             for e in range(3):
                 total = total + r2[e].astype(F32)
             self.a3[part * self.m[0]:part * self.m[0] + m] = total.astype(BF)
         for d in (2, 1, 3):
             owner = lax.rem(self.near + d, 4)
-            self.send(remote(self.a3.at[pl.ds(2 * owner, 2)], self.n3.at[d - 1], self.s_send.at[14 + d],
-                             self.s_recv.at[7], self.device(self.x, self.y, 4 * self.far + owner, self.core)))
+            self.send(remote(self.a3.at[pl.ds(2 * owner, 2)], self.n3.at[d - 1], self.s_send.at[32 + d],
+                             self.s_recv.at[13], self.device(self.x, self.y, 4 * self.far + owner, self.core)))
 
     def near_add(self):
-        self.received(self.n3, self.s_recv.at[7])
+        self.received(self.n3, self.s_recv.at[13])
         total = self.a3[pl.ds(2 * self.near, 2)].astype(F32)
         for e in range(3):
             total = total + self.n3[e].astype(F32)
@@ -188,7 +185,7 @@
 
     def far_copies(self):
         return [
-            remote(self.f3.at[self.far], self.f3.at[self.far], self.s_send.at[17 + d], self.s_recv.at[8],
+            remote(self.f3.at[self.far], self.f3.at[self.far], self.s_send.at[35 + d], self.s_recv.at[14],
                    self.device(self.x, self.y, 4 * lax.rem(self.far + d, 4) + self.near, self.core))
             for d in (2, 1, 3)
         ]
@@ -210,7 +207,7 @@
     def far_add(self):
         @pl.when(self.near < self.total // 2)
         def _():
-            self.received(self.f3.at[0:3], self.s_recv.at[8])
+            self.received(self.f3.at[0:3], self.s_recv.at[14])
             total = self.f3[0].astype(F32)
             for e in range(1, 4):
                 total = total + self.f3[e].astype(F32)
@@ -231,20 +228,32 @@
             ca, cb = self.coords(part)
             at = pl.ds(self.start[part] + (ca * 4 + cb) * m, m)
             for d in (2, 1, 3):
-                self.send(remote(self.out.at[self.core, at], self.out.at[self.core, at], self.g_send.at[part * 3 + d - 1],
-                                 self.g_recv.at[part], self.peer(self.axes(part)[1], d)))
+                k = part * 3 + d - 1
+                self.send(remote(self.out.at[self.core, at], self.out.at[self.core, at], self.g_send.at[k],
+                                 self.g_recv.at[k], self.peer(self.axes(part)[1], d)))
+        for part in range(2):
+            self.forward(part, 0)
+
+    def forward(self, part, e):
+        m = self.m[part]
+        ca, cb = self.coords(part)
+        at = pl.ds(self.start[part] + (ca * 4 + lax.rem(cb + 4 - e, 4)) * m, m)
+        for d in (2, 1, 3):
+            self.send(remote(self.out.at[self.core, at], self.out.at[self.core, at],
+                             self.g_send.at[23 + 12 * part + 3 * e + d - 1], self.g_recv.at[6 + part * 3 + d - 1],
+                             self.peer(self.axes(part)[0], d)))
 
     def gather_first(self):
+        for e in (1, 3, 2):
+            for part in range(2):
+                m = self.m[part]
+                ca, cb = self.coords(part)
+                at = pl.ds(self.start[part] + (ca * 4 + lax.rem(cb + 4 - e, 4)) * m, m)
+                self.received(self.out.at[self.core, at], self.g_recv.at[part * 3 + e - 1])
+                self.forward(part, e)
         for part in range(2):
-            m = self.m[part]
-            ca = self.coords(part)[0]
-            self.received(self.r2[part], self.g_recv.at[part])
-            at = pl.ds(self.start[part] + ca * 4 * m, 4 * m)
-            for d in (2, 1, 3):
-                k = 6 + part * 3 + d - 1
-                self.send(remote(self.out.at[self.core, at], self.out.at[self.core, at], self.g_send.at[k],
-                                 self.g_recv.at[k], self.peer(self.axes(part)[0], d)))
-            self.to_core(part, 0, at)
+            n = 4 * self.m[part]
+            self.to_core(part, 0, pl.ds(self.start[part] + self.coords(part)[0] * n, n))
 
     def to_core(self, part, d, at):
         k = 12 + part * 4 + d
@@ -285,9 +294,9 @@
         pltpu.VMEM((8, 16, 128), BF),
         pltpu.VMEM((3, 2, 16, 128), BF),
         pltpu.VMEM((4, 2, 16, 128), BF),
-        pltpu.SemaphoreType.DMA((21,)),
-        pltpu.SemaphoreType.DMA((21,)),
-        pltpu.SemaphoreType.DMA((23,)),
+        pltpu.SemaphoreType.DMA((39,)),
+        pltpu.SemaphoreType.DMA((15,)),
+        pltpu.SemaphoreType.DMA((47,)),
         pltpu.SemaphoreType.DMA((23,)),
     ]
 

time: 71.7 us -> 71.6 us (level)
  no operation moved by 1% of the time
where the time goes in v8:
time: 71.6 us; the launch traced here: 71.5 us
  Pallas kernels  70.8 us (99%)
    pallas_call x1, Pallas kernels, on_device(): pl.pallas_call(step_kernel, out_shape=(jax.ShapeDtypeStruct((64, C2), BF)...  69.4 us
    pallas_call x1, Pallas kernels, on_device(): pl.pallas_call(finish_kernel, out_shape=(jax.ShapeDtypeStruct((64, C2), B...  1.48 us

profile of v8, /device:TPU:1, one launch (start us, length us, event | category | flops | bytes accessed | tf_op | source)
XLA Modules:
  0.0 71.5 jit_solution(11996255348902203688)
XLA Ops:
  0.6 69.4 %level_step.1 = (bf16[64,256]{1,0:T(8,128)(2,1)S(1)}, bf16[256,128]{1,0:T(8,128)(2,1)S(1)}, bf16[2,96,16,128]{3,2,1,0:T(8,128)(2,1)S(1)}, bf16[2,128,16,128]{3,2,1,0:T(8,128)(2,1)S(1)}, f32[16,128]{1,0:T(8,128)S(1)}) custom-call(bf16[256,128]{1,0:T(8,128)(2,1)} %bitcast.10, bf16[3,384,256]{2,1,0:T(8,128)(2,1)} %bitcast.9, bf16[3,768,256]{2,1,0:T(8,128)(2,1)} %bitcast.8, ...), custom_call_target="tpu_custom_call" | custom-call | tf_op jit(solution)/shard_map/level_step/pallas_call | solution.py:823
  70.0 1.5 %scale_outputs.1 = (bf16[64,256]{1,0:T(8,128)(2,1)}, bf16[256,128]{1,0:T(8,128)(2,1)}, bf16[1152,256]{1,0:T(8,128)(2,1)}, bf16[2304,256]{1,0:T(8,128)(2,1)}) custom-call(bf16[64,256]{1,0:T(8,128)(2,1)S(1)} %get-tuple-element.13.pooled_ref, bf16[256,128]{1,0:T(8,128)(2,1)S(1)} %get-tuple-element.14.grad_ref, ...), custom_call_target="tpu_custom_call" | custom-call | tf_op jit(solution)/shard_map/scale_outputs/pallas_call | solution.py:878

commit v9 on v7

--- a/solution.py
+++ b/solution.py
@@ -200,12 +200,15 @@
         return jnp.where(u < ma, first, second)
 
     def near_copies(self):
-        at = pl.ds(self.unit_at(2 * self.near), 2)
-        return [
-            remote(self.out.at[self.core, at], self.out.at[self.core, at], self.g_send.at[19 + d], self.g_recv.at[19 + d],
-                   self.device(self.x, self.y, 4 * self.far + lax.rem(self.near + d, 4), self.core))
-            for d in (2, 1, 3)
-        ]
+        copies = []
+        for d in (2, 1, 3):
+            for q in range(2):
+                at = self.unit_at(2 * self.near + q)
+                copies.append(remote(
+                    self.out.at[self.core, at], self.out.at[self.core, at], self.g_send.at[19 + 2 * d + q - 1],
+                    self.g_recv.at[19 + d], self.device(self.x, self.y, 4 * self.far + lax.rem(self.near + d, 4), self.core)
+                ))
+        return copies
 
     def far_add(self):
         @pl.when(self.near < self.total // 2)
@@ -214,7 +217,9 @@
             total = self.f3[0].astype(F32)
             for e in range(1, 4):
                 total = total + self.f3[e].astype(F32)
-            self.out[self.core, pl.ds(self.unit_at(2 * self.near), 2)] = total.astype(BF)
+            total = total.astype(BF)
+            for q in range(2):
+                self.out[self.core, self.unit_at(2 * self.near + q)] = total[q]
             for copy in self.near_copies():
                 copy.start()
 
@@ -224,7 +229,7 @@
 
             @pl.when(owner < self.total // 2)
             def _():
-                self.received(self.out.at[self.core, pl.ds(self.unit_at(2 * owner), 2)], self.g_recv.at[19 + d])
+                self.received(self.f3.at[0], self.g_recv.at[19 + d])
 
         for part in range(2):
             m = self.m[part]
@@ -287,13 +292,13 @@
         pltpu.VMEM((4, 2, 16, 128), BF),
         pltpu.SemaphoreType.DMA((21,)),
         pltpu.SemaphoreType.DMA((21,)),
-        pltpu.SemaphoreType.DMA((23,)),
+        pltpu.SemaphoreType.DMA((27,)),
         pltpu.SemaphoreType.DMA((23,)),
     ]
 
 
 N_REDUCE = 16
-MA, MB = (4, 4), (4, 2)
+MA, MB = (4, 4), (3, 3)
 A_UNITS, B_UNITS, FIRST_UNITS, LAST_UNITS = 128, 96, 72, 16
 
 
@@ -759,17 +764,17 @@
     red2.flush()
     squares = jnp.zeros((16, 128), F32)
     for h in range(2):
-        squares = sum_squares(second_out, h, 0, A_UNITS // 8, squares)
-    squares = sum_squares(first_out, core, 0, B_UNITS // 8, squares)
+        squares = sum_squares(second_out, h, 0, A_UNITS // 4, squares)
+    squares = sum_squares(first_out, core, 0, B_UNITS // 4, squares)
     for part, at in red1.gather_done():
-        squares = sum_squares(first_out, 1 - core, at, red1.m[part] // 2, squares)
+        squares = sum_squares(first_out, 1 - core, at, red1.m[part], squares)
     square_ref[...] = squares
     red1.flush()
 
 
 def sum_squares(ref, half, at, steps, total):
     def body(i, total):
-        values = ref[half, pl.ds(at + i * 8, 8)].astype(F32)
+        values = ref[half, pl.ds(at + i * 4, 4)].astype(F32)
         return total + jnp.sum(values * values, axis=0)
 
     return lax.fori_loop(0, steps, body, total)

time: 71.7 us -> 72.4 us (level)
  no operation moved by 1% of the time
where the time goes in v9:
time: 72.4 us; the launch traced here: 72.2 us
  Pallas kernels  71.6 us (99%)
    pallas_call x1, Pallas kernels, on_device(): pl.pallas_call(step_kernel, out_shape=(jax.ShapeDtypeStruct((64, C2), BF)...  70.1 us
    pallas_call x1, Pallas kernels, on_device(): pl.pallas_call(finish_kernel, out_shape=(jax.ShapeDtypeStruct((64, C2), B...  1.48 us

profile of v9, /device:TPU:1, one launch (start us, length us, event | category | flops | bytes accessed | tf_op | source)
XLA Modules:
  0.0 72.2 jit_solution(15788165625987583946)
XLA Ops:
  0.6 70.1 %level_step.1 = (bf16[64,256]{1,0:T(8,128)(2,1)S(1)}, bf16[256,128]{1,0:T(8,128)(2,1)S(1)}, bf16[2,96,16,128]{3,2,1,0:T(8,128)(2,1)S(1)}, bf16[2,128,16,128]{3,2,1,0:T(8,128)(2,1)S(1)}, f32[16,128]{1,0:T(8,128)S(1)}) custom-call(bf16[256,128]{1,0:T(8,128)(2,1)} %bitcast.10, bf16[3,384,256]{2,1,0:T(8,128)(2,1)} %bitcast.9, bf16[3,768,256]{2,1,0:T(8,128)(2,1)} %bitcast.8, ...), custom_call_target="tpu_custom_call" | custom-call | tf_op jit(solution)/shard_map/level_step/pallas_call | solution.py:819
  70.8 1.5 %scale_outputs.1 = (bf16[64,256]{1,0:T(8,128)(2,1)}, bf16[256,128]{1,0:T(8,128)(2,1)}, bf16[1152,256]{1,0:T(8,128)(2,1)}, bf16[2304,256]{1,0:T(8,128)(2,1)}) custom-call(bf16[64,256]{1,0:T(8,128)(2,1)S(1)} %get-tuple-element.13.pooled_ref, bf16[256,128]{1,0:T(8,128)(2,1)S(1)} %get-tuple-element.14.grad_ref, ...), custom_call_target="tpu_custom_call" | custom-call | tf_op jit(solution)/shard_map/scale_outputs/pallas_call | solution.py:874

commit v10 on v7

--- a/solution.py
+++ b/solution.py
@@ -70,12 +70,13 @@
         self.m = m
         self.total = m[0] + m[1]
         self.start = (0, 16 * m[0])
-        (self.halves, self.r0, self.a1, r1a, r1b, a2a, a2b, r2a, r2b, self.a3, self.n3, self.f3, self.out,
+        (self.halves, self.r0, self.a1, r1a, r1b, a2a, a2b, r2a, r2b, self.f3, self.out,
          self.s_send, self.s_recv, self.g_send, self.g_recv) = refs
         self.r1, self.a2, self.r2 = (r1a, r1b), (a2a, a2b), (r2a, r2b)
         self.x, self.y, self.z, self.core, self.device = place
         self.near, self.far = lax.rem(self.z, 4), lax.div(self.z, 4)
         self.pending = []
+        self.guarded = []
         self.pieces = []
         self.waited = 0
 
@@ -103,19 +104,25 @@
     def flush(self):
         for copy in self.pending:
             copy.wait_send()
-        self.pending = []
-
-    def far_flush(self):
-        @pl.when(self.near < self.total // 2)
-        def _():
-            for copy in self.far_copies():
-                copy.wait_send()
-
-    def near_flush(self):
-        @pl.when(self.near < self.total // 2)
-        def _():
-            for copy in self.near_copies():
-                copy.wait_send()
+        for wanted, copy in self.guarded:
+            pl.when(wanted)(copy.wait_send)
+        self.pending, self.guarded = [], []
+
+    def send_if(self, wanted, copy):
+        pl.when(wanted)(copy.start)
+        self.guarded.append((wanted, copy))
+
+    def plane(self, part):
+        for db in (2, 1, 3, 0):
+            for dz in (2, 3, 1, 0):
+                if db or dz:
+                    x, y = self.x, self.y
+                    if part == 0:
+                        y = lax.rem(y + db, 4)
+                    else:
+                        x = lax.rem(x + db, 4)
+                    near = lax.rem(self.near + dz, 4)
+                    yield 4 * db + dz - 1, (y if part == 0 else x), near, self.device(x, y, 4 * self.far + near, self.core)
 
     def core_send(self, at, count):
         k = len(self.pieces)
@@ -144,111 +151,77 @@
         for part in range(2):
             m = self.m[part]
             r1, a2, r2 = self.r1[part], self.a2[part], self.r2[part]
-            ca, cb = self.coords(part)
+            ca = self.coords(part)[0]
             self.received(r1, self.s_recv.at[3 + part])
-            k = 5 + part
-            for d in (2, 1, 3, 0):
-                block = lax.rem(cb + d, 4)
-                at = pl.ds(block * m, m)
-                total = self.a1[pl.ds(self.start[part] + (ca * 4 + block) * m, m)].astype(F32)
-                for e in range(3):
-                    total = total + r1[e, at].astype(F32)
-                a2[at] = total.astype(BF)
-                if d:
-                    self.send(remote(a2.at[at], r2.at[d - 1],
-                                     self.s_send.at[3 * k - 7 + d], self.s_recv.at[k],
-                                     self.peer(self.axes(part)[1], d)))
+            total = self.a1[pl.ds(self.start[part] + ca * 4 * m, 4 * m)].astype(F32)
+            for e in range(3):
+                total = total + r1[e].astype(F32)
+            a2[...] = total.astype(BF)
+            for slot, b_at, near, target in self.plane(part):
+                self.send_if(near < m, remote(
+                    a2.at[b_at * m + lax.rem(near, m)], r2.at[slot], self.s_send.at[9 + 15 * part + slot],
+                    self.s_recv.at[5 + part], target))
 
     def second_add(self):
         for part in range(2):
             m = self.m[part]
-            a2, r2 = self.a2[part], self.r2[part]
             cb = self.coords(part)[1]
-            self.received(r2, self.s_recv.at[5 + part])
-            total = a2[pl.ds(cb * m, m)].astype(F32)
-            for e in range(3):
-                total = total + r2[e].astype(F32)
-            self.a3[part * self.m[0]:part * self.m[0] + m] = total.astype(BF)
+
+            @pl.when(self.near < m)
+            def _():
+                self.received(self.r2[part], self.s_recv.at[5 + part])
+                total = self.a2[part][cb * m + lax.rem(self.near, m)].astype(F32)
+                for e in range(15):
+                    total = total + self.r2[part][e].astype(F32)
+                self.f3[self.far, part] = total.astype(BF)
+
         for d in (2, 1, 3):
-            owner = lax.rem(self.near + d, 4)
-            self.send(remote(self.a3.at[pl.ds(2 * owner, 2)], self.n3.at[d - 1], self.s_send.at[14 + d],
-                             self.s_recv.at[7], self.device(self.x, self.y, 4 * self.far + owner, self.core)))
-
-    def near_add(self):
-        self.received(self.n3, self.s_recv.at[7])
-        total = self.a3[pl.ds(2 * self.near, 2)].astype(F32)
-        for e in range(3):
-            total = total + self.n3[e].astype(F32)
-        self.f3[self.far] = total.astype(BF)
-
-        @pl.when(self.near < self.total // 2)
-        def _():
-            for copy in self.far_copies():
-                copy.start()
-
-    def far_copies(self):
-        return [
-            remote(self.f3.at[self.far], self.f3.at[self.far], self.s_send.at[17 + d], self.s_recv.at[8],
-                   self.device(self.x, self.y, 4 * lax.rem(self.far + d, 4) + self.near, self.core))
-            for d in (2, 1, 3)
-        ]
-
-    def unit_at(self, u):
-        ma, mb = self.m
-        first = (self.x * 4 + self.y) * ma + u
-        second = self.start[1] + (self.y * 4 + self.x) * mb + u - ma
-        return jnp.where(u < ma, first, second)
-
-    def near_copies(self):
-        at = pl.ds(self.unit_at(2 * self.near), 2)
-        return [
-            remote(self.out.at[self.core, at], self.out.at[self.core, at], self.g_send.at[19 + d], self.g_recv.at[19 + d],
-                   self.device(self.x, self.y, 4 * self.far + lax.rem(self.near + d, 4), self.core))
-            for d in (2, 1, 3)
-        ]
+            self.send(remote(self.f3.at[self.far], self.f3.at[self.far], self.s_send.at[39 + d - 1], self.s_recv.at[8],
+                             self.device(self.x, self.y, 4 * lax.rem(self.far + d, 4) + self.near, self.core)))
 
     def far_add(self):
-        @pl.when(self.near < self.total // 2)
-        def _():
-            self.received(self.f3.at[0:3], self.s_recv.at[8])
-            total = self.f3[0].astype(F32)
-            for e in range(1, 4):
-                total = total + self.f3[e].astype(F32)
-            self.out[self.core, pl.ds(self.unit_at(2 * self.near), 2)] = total.astype(BF)
-            for copy in self.near_copies():
-                copy.start()
-
-    def gather_second(self):
-        for d in (1, 3, 2):
-            owner = lax.rem(self.near + 4 - d, 4)
-
-            @pl.when(owner < self.total // 2)
-            def _():
-                self.received(self.out.at[self.core, pl.ds(self.unit_at(2 * owner), 2)], self.g_recv.at[19 + d])
-
+        self.received(self.f3.at[0:3], self.s_recv.at[8])
         for part in range(2):
             m = self.m[part]
             ca, cb = self.coords(part)
-            at = pl.ds(self.start[part] + (ca * 4 + cb) * m, m)
-            for d in (2, 1, 3):
-                self.send(remote(self.out.at[self.core, at], self.out.at[self.core, at], self.g_send.at[part * 3 + d - 1],
-                                 self.g_recv.at[part], self.peer(self.axes(part)[1], d)))
-
-    def gather_first(self):
+            total = self.f3[0, part].astype(F32)
+            for e in range(1, 4):
+                total = total + self.f3[e, part].astype(F32)
+            at = self.start[part] + (ca * 4 + cb) * m + lax.rem(self.near, m)
+
+            @pl.when(self.near < m)
+            def _():
+                self.out[self.core, at] = total.astype(BF)
+
+            for slot, _, _, target in self.plane(part):
+                self.send_if(self.near < m, remote(
+                    self.out.at[self.core, at], self.out.at[self.core, at], self.g_send.at[15 * part + slot],
+                    self.g_recv.at[part], target))
+
+    def gather_second(self):
         for part in range(2):
             m = self.m[part]
             ca = self.coords(part)[0]
-            self.received(self.r2[part], self.g_recv.at[part])
+            owns = self.near < m
+
+            @pl.when(owns)
+            def _():
+                self.received(self.a1.at[0:4 * m - 1], self.g_recv.at[part])
+
+            @pl.when(jnp.logical_not(owns))
+            def _():
+                self.received(self.a1.at[0:4 * m], self.g_recv.at[part])
+
             at = pl.ds(self.start[part] + ca * 4 * m, 4 * m)
             for d in (2, 1, 3):
-                k = 6 + part * 3 + d - 1
-                self.send(remote(self.out.at[self.core, at], self.out.at[self.core, at], self.g_send.at[k],
-                                 self.g_recv.at[k], self.peer(self.axes(part)[0], d)))
+                k = part * 3 + d - 1
+                self.send(remote(self.out.at[self.core, at], self.out.at[self.core, at], self.g_send.at[30 + k],
+                                 self.g_recv.at[6 + k], self.peer(self.axes(part)[0], d)))
             self.to_core(part, 0, at)
 
     def to_core(self, part, d, at):
         k = 12 + part * 4 + d
-        self.send(remote(self.out.at[self.core, at], self.out.at[self.core, at], self.g_send.at[k],
+        self.send(remote(self.out.at[self.core, at], self.out.at[self.core, at], self.g_send.at[24 + k],
                          self.g_recv.at[k], self.other_core()))
 
     def block_of(self, part, d):
@@ -280,19 +253,17 @@
         pltpu.VMEM((3, 4 * mb, 16, 128), BF),
         pltpu.VMEM((4 * ma, 16, 128), BF),
         pltpu.VMEM((4 * mb, 16, 128), BF),
-        pltpu.VMEM((3, ma, 16, 128), BF),
-        pltpu.VMEM((3, mb, 16, 128), BF),
-        pltpu.VMEM((8, 16, 128), BF),
-        pltpu.VMEM((3, 2, 16, 128), BF),
+        pltpu.VMEM((15, 16, 128), BF),
+        pltpu.VMEM((15, 16, 128), BF),
         pltpu.VMEM((4, 2, 16, 128), BF),
-        pltpu.SemaphoreType.DMA((21,)),
-        pltpu.SemaphoreType.DMA((21,)),
-        pltpu.SemaphoreType.DMA((23,)),
-        pltpu.SemaphoreType.DMA((23,)),
+        pltpu.SemaphoreType.DMA((42,)),
+        pltpu.SemaphoreType.DMA((9,)),
+        pltpu.SemaphoreType.DMA((44,)),
+        pltpu.SemaphoreType.DMA((20,)),
     ]
 
 
-N_REDUCE = 16
+N_REDUCE = 14
 MA, MB = (4, 4), (4, 2)
 A_UNITS, B_UNITS, FIRST_UNITS, LAST_UNITS = 128, 96, 72, 16
 
@@ -349,8 +320,8 @@
     (feat_ref, w1, w2, cot_ref, pick_ref, flip_ref, rule_ref, load_sem,
      rules_out, rules_in, rule_send, rule_recv, q_fwd, q_back, q_act, slope1, pre2,
      windows) = refs
-    red2_refs = red2_refs[:12] + (second_out,) + red2_refs[12:]
-    red1_refs = red1_refs[:12] + (first_out,) + red1_refs[12:]
+    red2_refs = red2_refs[:10] + (second_out,) + red2_refs[10:]
+    red1_refs = red1_refs[:10] + (first_out,) + red1_refs[10:]
 
     lon, lat = lax.axis_index("lon"), lax.axis_index("lat")
     y = lax.div(lon, 2 * NZ)
@@ -388,9 +359,11 @@
     partners = [device(x, y, lax.rem(z + 4 * d, NZ), core) for d in (2, 1, 3)]
     partners += [d[0] for d in diagonal] + [west, east, vert[0], vert[1]]
     for d in (2, 1, 3):
+        for dz in (2, 1, 3, 0):
+            z_at = 4 * lax.div(z, 4) + lax.rem(z + dz, 4)
+            partners.append(device(lax.rem(x + d, NX), y, z_at, core))
+            partners.append(device(x, lax.rem(y + d, NY), z_at, core))
         partners.append(device(x, y, 4 * lax.div(z, 4) + lax.rem(z + d, 4), core))
-        partners.append(device(lax.rem(x + d, NX), y, z, core))
-        partners.append(device(x, lax.rem(y + d, NY), z, core))
     partners.append(device(x, y, z, 1 - core))
     for partner in partners:
         pl.semaphore_signal(barrier, inc=1, device_id=partner, device_id_type=MESH)
@@ -499,7 +472,7 @@
     red1 = Reduce(MB, red1_refs, (x, y, z, core, device))
     used = FIRST_UNITS + LAST_UNITS
     red1.halves[:, used:B_UNITS] = jnp.zeros((2, B_UNITS - used, 16, 128), BF)
-    red1.a3[6:8] = jnp.zeros((2, 16, 128), BF)
+    red1.f3[red1.far] = jnp.zeros((2, 16, 128), BF)
 
     for slot in range(4):
         remote(rules_out, rules_in.at[slot], rule_send.at[slot], rule_recv.at[slot], west).wait_recv()
@@ -734,8 +707,6 @@
 
     red2.second_add()
     red1.second_add()
-    red2.near_add()
-    red1.near_add()
 
     grad_waits(layer1)
     grad_ref[...] = (centre1.astype(F32) + mm(place_grads, layer1[6][...])).astype(BF)
@@ -748,11 +719,6 @@
     red1.far_add()
     red2.gather_second()
     red1.gather_second()
-    for red in (red2, red1):
-        red.far_flush()
-        red.near_flush()
-    red2.gather_first()
-    red1.gather_first()
     red2.gather_core()
     red1.gather_core()
     list(red2.gather_done())

time: 71.7 us -> 67.6 us (0.943)
  Pallas kernels: 70.9 us -> 66.8 us
    pallas_call x1, Pallas kernels: 69.4 us -> 65.3 us  [on_device(): pl.pallas_call(step_kernel, out_shape=(jax.ShapeDtypeStruct((64, C2), BF)...]
where the time goes in v10:
time: 67.6 us; the launch traced here: 67.4 us
  Pallas kernels  66.8 us (99%)
    pallas_call x1, Pallas kernels, on_device(): pl.pallas_call(step_kernel, out_shape=(jax.ShapeDtypeStruct((64, C2), BF)...  65.3 us
    pallas_call x1, Pallas kernels, on_device(): pl.pallas_call(finish_kernel, out_shape=(jax.ShapeDtypeStruct((64, C2), B...  1.48 us

profile of v10, /device:TPU:1, one launch (start us, length us, event | category | flops | bytes accessed | tf_op | source)
XLA Modules:
  0.0 67.4 jit_solution(5996577920903847807)
XLA Ops:
  0.6 65.3 %level_step.1 = (bf16[64,256]{1,0:T(8,128)(2,1)S(1)}, bf16[256,128]{1,0:T(8,128)(2,1)S(1)}, bf16[2,96,16,128]{3,2,1,0:T(8,128)(2,1)S(1)}, bf16[2,128,16,128]{3,2,1,0:T(8,128)(2,1)S(1)}, f32[16,128]{1,0:T(8,128)S(1)}) custom-call(bf16[256,128]{1,0:T(8,128)(2,1)} %bitcast.10, bf16[3,384,256]{2,1,0:T(8,128)(2,1)} %bitcast.9, bf16[3,768,256]{2,1,0:T(8,128)(2,1)} %bitcast.8, ...), custom_call_target="tpu_custom_call" | custom-call | tf_op jit(solution)/shard_map/level_step/pallas_call | solution.py:780
  65.9 1.5 %scale_outputs.1 = (bf16[64,256]{1,0:T(8,128)(2,1)}, bf16[256,128]{1,0:T(8,128)(2,1)}, bf16[1152,256]{1,0:T(8,128)(2,1)}, bf16[2304,256]{1,0:T(8,128)(2,1)}) custom-call(bf16[64,256]{1,0:T(8,128)(2,1)S(1)} %get-tuple-element.13.pooled_ref, bf16[256,128]{1,0:T(8,128)(2,1)S(1)} %get-tuple-element.14.grad_ref, ...), custom_call_target="tpu_custom_call" | custom-call | tf_op jit(solution)/shard_map/scale_outputs/pallas_call | solution.py:835

commit v11 on v10

--- a/solution.py
+++ b/solution.py
@@ -101,12 +101,13 @@
     def received(self, ref, sem):
         remote(ref, ref, self.s_send.at[0], sem, self.other_core()).wait_recv()
 
-    def flush(self):
-        for copy in self.pending:
+    def flush(self, keep=0):
+        done = len(self.pending) - keep
+        for copy in self.pending[:done]:
             copy.wait_send()
         for wanted, copy in self.guarded:
             pl.when(wanted)(copy.wait_send)
-        self.pending, self.guarded = [], []
+        self.pending, self.guarded = self.pending[done:], []
 
     def send_if(self, wanted, copy):
         pl.when(wanted)(copy.start)
@@ -713,8 +714,8 @@
 
     for copy in sent + rule_copies:
         copy.wait_send()
-    red2.flush()
-    red1.flush()
+    red2.flush(3)
+    red1.flush(3)
     red2.far_add()
     red1.far_add()
     red2.gather_second()

time: 67.6 us -> 67.6 us (level)
  no operation moved by 1% of the time
where the time goes in v11:
time: 67.6 us; the launch traced here: 67.4 us
  Pallas kernels  66.8 us (99%)
    pallas_call x1, Pallas kernels, on_device(): pl.pallas_call(step_kernel, out_shape=(jax.ShapeDtypeStruct((64, C2), BF)...  65.3 us
    pallas_call x1, Pallas kernels, on_device(): pl.pallas_call(finish_kernel, out_shape=(jax.ShapeDtypeStruct((64, C2), B...  1.48 us

profile of v11, /device:TPU:1, one launch (start us, length us, event | category | flops | bytes accessed | tf_op | source)
XLA Modules:
  0.0 67.4 jit_solution(14643307545333699229)
XLA Ops:
  0.6 65.3 %level_step.1 = (bf16[64,256]{1,0:T(8,128)(2,1)S(1)}, bf16[256,128]{1,0:T(8,128)(2,1)S(1)}, bf16[2,96,16,128]{3,2,1,0:T(8,128)(2,1)S(1)}, bf16[2,128,16,128]{3,2,1,0:T(8,128)(2,1)S(1)}, f32[16,128]{1,0:T(8,128)S(1)}) custom-call(bf16[256,128]{1,0:T(8,128)(2,1)} %bitcast.10, bf16[3,384,256]{2,1,0:T(8,128)(2,1)} %bitcast.9, bf16[3,768,256]{2,1,0:T(8,128)(2,1)} %bitcast.8, ...), custom_call_target="tpu_custom_call" | custom-call | tf_op jit(solution)/shard_map/level_step/pallas_call | solution.py:781
  66.0 1.5 %scale_outputs.1 = (bf16[64,256]{1,0:T(8,128)(2,1)}, bf16[256,128]{1,0:T(8,128)(2,1)}, bf16[1152,256]{1,0:T(8,128)(2,1)}, bf16[2304,256]{1,0:T(8,128)(2,1)}) custom-call(bf16[64,256]{1,0:T(8,128)(2,1)S(1)} %get-tuple-element.13.pooled_ref, bf16[256,128]{1,0:T(8,128)(2,1)S(1)} %get-tuple-element.14.grad_ref, ...), custom_call_target="tpu_custom_call" | custom-call | tf_op jit(solution)/shard_map/scale_outputs/pallas_call | solution.py:836
